TPU v7x, 32 devices: a whole 2x2x4 slice. The times are simulated.
32 devices in a mesh: prow: 4 (over y, x), pcol: 8 (over z, core).
Axes of the slice: x: 2, y: 2, z: 4, core: 2. Of those that a mesh axis runs over, the one named last changes fastest.
Arguments:
- known_inverse: bfloat16 [4096, 4, 8, 128], P('prow', None, 'pcol'), may hold values from -6 to 6
- pattern: int32 [32, 4, 8, 1], P('prow', None, 'pcol'), may hold values 0 or 1
- panel_one: bfloat16 [4096, 512], P(('prow', 'pcol')), may hold values from -0.09375 to 0.09375
- panel_two: bfloat16 [4096, 512], P(('prow', 'pcol')), may hold values from -0.09375 to 0.09375
- panel_top: bfloat16 [512, 512], replicated, may hold values from -0.25 to 0.25
- structure: int32 [4096], P(('prow', 'pcol')), may hold values from 0 to 1, as said below
- diag_one: bfloat16 [512, 512], replicated, may hold values from -6 to 6
- diag_two: bfloat16 [512, 512], replicated, may hold values from -6 to 6
Outputs:
- inverse_one: bfloat16 [4096, 512], P(('prow', 'pcol'))
- corner_one: bfloat16 [512, 512], replicated
- inverse_top: bfloat16 [512, 512], replicated
- inverse_two: bfloat16 [4096, 512], P(('prow', 'pcol'))
- corner_two: bfloat16 [512, 512], replicated
Inputs may be any that keep to these rules, and one draw needn't show every extreme that they name: `structure`: in every aligned pair of rows (2 k and 2 k + 1) at least one entry is 1.
All inputs are finite; a program needn't handle non-finite values. No bound on the sum of `pattern` on one device may be relied on, other than what follows from the above.
Results may differ from a plain program's by a relative error of at most 0.0058.
Values may be sent and summed in bfloat16 or wider, within the bound.
No kernel may reach another device: no remote copies, remote signals or barrier semaphores. Data moves between devices by JAX's collectives and lax.ppermute only.
A program may use at most 128 MiB of HBM per device.

v0:
```python
import functools
import math

import jax
import jax.numpy as jnp
from jax import lax
from jax.experimental import pallas as pl
from jax.experimental.pallas import tpu as pltpu
from jax.sharding import PartitionSpec as P


BLK = 128
BF = jnp.bfloat16
F32 = jnp.float32

VMEM = pl.BlockSpec(memory_space=pltpu.VMEM)


def sds(shape, dtype):
    return jax.ShapeDtypeStruct(shape, dtype)


def scratch(shape, dtype):
    return pltpu.VMEM(shape, dtype)


def call(body, out, temps, args, flops):
    size = lambda a: math.prod(a.shape) * jnp.dtype(a.dtype).itemsize
    held = sum(size(a) for a in (*args, *out))
    room = held + sum(size(t) for t in temps) + sum(2 * size(t) for t in out)
    return pl.pallas_call(
        body,
        out_shape=out,
        in_specs=[VMEM] * len(args),
        out_specs=[VMEM] * len(out),
        scratch_shapes=temps,
        cost_estimate=pl.CostEstimate(flops=flops, bytes_accessed=held, transcendentals=0),
        compiler_params=pltpu.CompilerParams(vmem_limit_bytes=room + (4 << 20)),
    )(*args)


def tree(parts):
    while len(parts) > 1:
        parts = [parts[k] + parts[k + 1] for k in range(0, len(parts), 2)]
    return parts[0]


def dot(a, b):
    return jnp.dot(a, b, preferred_element_type=F32)


def place():
    j = lax.axis_index("pcol")
    return lax.axis_index("prow"), j >> 1, j & 1


def block(index, size):
    return pl.ds(pl.multiple_of(index * size, size), size)


def pick_body(own, got, out):
    _, _, c = place()
    rows, half = own.shape[0], out.shape[1]
    out[:rows, :] = own[:, block(c, half)]
    out[rows:, :] = got[:, block(c, half)]


def pick(own, got):
    rows, width = own.shape
    return call(pick_body, [sds((2 * rows, width // 2), BF)], [], [own, got], 0)[0]


def start_body(one, top, start, top_t):
    start[...] = dot(one[...], top[...])
    top_t[...] = top[...].T


def start_parts(one, top):
    out = [sds(top.shape, F32), sds(top.shape, BF)]
    return call(start_body, out, [], [one, top], 2 * top.shape[0] ** 3)


def product_body(n, nz, mine, theirs, *refs):
    q, outs, rhs = refs[:n], refs[n : n + nz], refs[n + nz]
    p, z, c = place()
    rows = q[0].shape[0] // 2
    depth = rhs.shape[0] // 2
    for s in range(n):
        rhs[block(p ^ s, rows), :] = q[s][:rows, :]
        rhs[pl.ds(pl.multiple_of(depth + (p ^ s) * rows, rows), rows), :] = q[s][rows:, :]
    for s in range(nz):
        span = block(z ^ s, 2 * rows)
        value = dot(mine[span, :], rhs[:depth, :]) + dot(theirs[span, :], rhs[depth:, :])
        for t in range(2):
            outs[s][block(c ^ t, rows), :] = value[t * rows : (t + 1) * rows].astype(outs[s].dtype)


def product(mine, theirs, q, nz):
    n, shape = len(q), q[0].shape
    depth = mine.shape[1]
    out = [sds(shape, F32)] + [sds(shape, BF)] * (nz - 1) + [sds((2 * depth, shape[1]), BF)]
    *parts, rhs = call(
        functools.partial(product_body, n, nz), out, [],
        [mine, theirs, *q], 4 * mine.shape[0] * depth * shape[1],
    )
    return parts, rhs


def first_body(n, nz, *refs):
    parts = refs[:nz]
    keep, give, outs, turned = refs[nz], refs[nz + 1], refs[nz + 2 : nz + 2 + n], refs[nz + 2 + n]
    p, _, _ = place()
    rows = keep.shape[0]
    inverse = -tree([parts[s][...].astype(F32) for s in range(nz)])
    keep[...] = inverse[:rows].astype(BF)
    give[...] = inverse[rows:].astype(BF)
    turned[...] = inverse.T
    for s in range(n):
        outs[s][...] = turned[block(p ^ s, outs[s].shape[0]), :].astype(BF)


def second_body(n, nz, *refs):
    parts, give_one = refs[:nz], refs[nz]
    keep, give, outs, turned = refs[nz + 1], refs[nz + 2], refs[nz + 3 : nz + 3 + n], refs[nz + 3 + n]
    p, _, _ = place()
    rows, half = keep.shape
    value = tree([parts[s][...].astype(F32) for s in range(nz)])
    keep[...] = value[:rows]
    give[:, :half] = give_one[...].astype(F32)
    give[:, half:] = value[rows:]
    turned[...] = value.T
    for s in range(n):
        outs[s][...] = turned[block(p ^ s, outs[s].shape[0]), :].astype(BF)


def first_turn(parts, n):
    nz, (rows2, half) = len(parts), parts[0].shape
    out = [sds((rows2 // 2, half), BF)] * 2 + [sds((half // n, rows2), BF)] * n
    return call(
        functools.partial(first_body, n, nz), out, [scratch((half, rows2), F32)],
        parts, nz * rows2 * half,
    )


def second_turn(parts, give_one, n):
    nz, (rows2, half) = len(parts), parts[0].shape
    out = [sds((rows2 // 2, half), F32), sds((rows2 // 2, 2 * half), F32)]
    out += [sds((half // n, rows2), BF)] * n
    return call(
        functools.partial(second_body, n, nz), out, [scratch((half, rows2), F32)],
        [*parts, give_one], nz * rows2 * half,
    )


def sums_body(n, *refs):
    pieces, panels, out, left = refs[:n], refs[n:-2], refs[-2], refs[-1]
    p, _, c = place()
    rows = pieces[0].shape[1] // 2
    depth, half = left.shape[1] // 2, panels[0].shape[1]
    for s in range(n):
        left[:, block(p ^ s, rows)] = pieces[s][:, :rows]
        left[:, pl.ds(pl.multiple_of(depth + (p ^ s) * rows, rows), rows)] = pieces[s][:, rows:]
    for k in range(len(panels) // 2):
        ours, got = panels[2 * k : 2 * k + 2]
        near = dot(left[...], ours[...])
        far = dot(left[:, :depth], got[depth:, :]) + dot(left[:, depth:], got[:depth, :])
        out[:, block(2 * k + c, half)] = near.astype(BF)
        out[:, block(2 * k + 1 - c, half)] = far.astype(BF)


def sums(pieces, panels):
    n, (low, _) = len(pieces), pieces[0].shape
    deep, half = panels[0].shape
    return call(
        functools.partial(sums_body, n), [sds((low, len(panels) * half), BF)], [scratch((low, deep), BF)],
        [*pieces, *panels], 2 * low * deep * half * len(panels),
    )[0]


def top_body(n, *refs):
    mine, theirs = refs[:n], refs[n : 2 * n]
    start, top, top_t, one, two = refs[2 * n : 2 * n + 5]
    corner, inverse_top, rest, own_t, cross = refs[2 * n + 5 :]
    p, _, c = place()
    low, width = mine[0].shape[0], own_t.shape[1]
    for s in range(n):
        for source, t in ((mine[s], c), (theirs[s], 1 - c)):
            rows = block(t * n + (p ^ s), low)
            own_t[rows, :] = source[:, :width]
            cross[rows, :] = source[:, width:]
    own = own_t[...].T
    corner[...] = (one[...].astype(F32) - own.astype(F32)).astype(BF)
    inverse_top[...] = (dot(own, top[...]) - start[...] - cross[...].astype(F32)).astype(BF)
    rest[...] = (
        two[...].astype(F32) - dot(top_t[...], inverse_top[...]) + dot(cross[...].T, top[...])
    )


def top_parts(mine, theirs, start, top, top_t, one, two):
    n, shape = len(mine), top.shape
    out = [sds(shape, BF), sds(shape, BF), sds(shape, F32)]
    return call(
        functools.partial(top_body, n), out, [scratch(shape, BF)] * 2,
        [*mine, *theirs, start, top, top_t, one, two], 6 * shape[0] ** 3,
    )


def last_body(n, *refs):
    mine, theirs, rest, out, tail_t = refs[:n], refs[n : 2 * n], *refs[2 * n :]
    p, _, c = place()
    low = mine[0].shape[0]
    for s in range(n):
        for source, t in ((mine[s], c), (theirs[s], 1 - c)):
            tail_t[block(t * n + (p ^ s), low), :] = source[...]
    out[...] = (rest[...] + tail_t[...].T.astype(F32)).astype(BF)


def last_part(mine, theirs, rest):
    return call(
        functools.partial(last_body, len(mine)), [sds(rest.shape, BF)], [scratch(rest.shape, BF)],
        [*mine, *theirs, rest], 2 * math.prod(rest.shape),
    )[0]


def finish_body(keep_one, keep_two, got, top, flags, inverse_one, inverse_two, value):
    _, _, c = place()
    half = keep_one.shape[1]
    inverse_one[:, block(c, half)] = keep_one[...]
    inverse_one[:, block(1 - c, half)] = got[:, :half].astype(BF)
    value[:, block(c, half)] = keep_two[...]
    value[:, block(1 - c, half)] = got[:, half:]
    lower = -(value[...] + dot(inverse_one[...], top[...]))
    inverse_two[...] = jnp.where(flags[...] > 0, lower, jnp.zeros_like(lower)).astype(BF)


def finish(keep_one, keep_two, got, top, flags):
    shape = (keep_one.shape[0], top.shape[1])
    return call(
        finish_body, [sds(shape, BF)] * 2, [scratch(shape, F32)],
        [keep_one, keep_two, got, top, flags], 2 * shape[0] * top.shape[0] * shape[1],
    )


def on_device(
    n, m, known_inverse, pattern, panel_one, panel_two, panel_top, structure, diag_one, diag_two
):
    row_count = known_inverse.shape[0]
    col_groups = known_inverse.shape[1]
    piece_rows = known_inverse.shape[3]
    nz = m // 2
    block_rows = row_count // BLK
    piece_blocks = piece_rows // BLK
    send = lambda x, axis, size, s: lax.ppermute(x, axis, [(k, k ^ s) for k in range(size)])
    swap = lambda x: send(x, "pcol", m, 1)
    over_z = lambda x, s: send(x, "pcol", m, 2 * s)
    over_p = lambda x, s: send(x, "prow", n, s)

    flags = structure.reshape(piece_rows, 1)
    masked_two = jnp.where(flags > 0, panel_two, jnp.zeros_like(panel_two))
    mine_one = pick(panel_one, swap(panel_one))
    mine_two = pick(masked_two, swap(masked_two))
    gather = lambda x: [x] + [over_p(x, s) for s in range(1, n)]
    gathered_one = gather(mine_one)
    gathered_two = gather(mine_two)

    shaped = known_inverse.reshape(block_rows, BLK, col_groups, piece_blocks, BLK)
    flag_table = pattern.reshape(block_rows, 1, col_groups, piece_blocks, 1)
    masked = jnp.where(flag_table > 0, shaped, jnp.zeros_like(shaped)).reshape(
        row_count, col_groups * piece_rows
    )
    others = swap(masked)
    start, top_t = start_parts(diag_one, panel_top)

    def exchange(parts):
        return [parts[0]] + [over_z(parts[s], s) for s in range(1, nz)]

    def spread(pieces):
        return [pieces[0]] + [over_p(pieces[s], s) for s in range(1, n)]

    def total(here):
        s = 1
        while s < nz:
            here = (here.astype(F32) + over_z(here, s).astype(F32)).astype(BF)
            s *= 2
        got = [here] + [over_p(here, s) for s in range(1, n)]
        return got, [swap(got[s]) for s in range(n)]

    parts_one, rows_one = product(masked, others, gathered_one, nz)
    parts_one = exchange(parts_one)
    parts_two, rows_two = product(masked, others, gathered_two, nz)
    parts_two = exchange(parts_two)
    panels = [rows_one, swap(rows_one), rows_two, swap(rows_two)]
    keep_one, give_one, *pieces_one = first_turn(parts_one, n)
    pieces_one = spread(pieces_one)
    keep_two, give, *pieces_two = second_turn(parts_two, give_one, n)
    pieces_two = spread(pieces_two)
    sums_one = sums(pieces_one, panels)
    sums_two = sums(pieces_two, panels[2:])
    corner_one, inverse_top, rest = top_parts(
        *total(sums_one), start, panel_top, top_t, diag_one, diag_two
    )
    corner_two = last_part(*total(sums_two), rest)
    inverse_one, inverse_two = finish(keep_one, keep_two, swap(give), panel_top, flags)
    return inverse_one, corner_one, inverse_top, inverse_two, corner_two


def solution(mesh):
    in_specs = (
        P("prow", None, "pcol", None),
        P("prow", None, "pcol", None),
        P(("prow", "pcol"), None),
        P(("prow", "pcol"), None),
        P(),
        P(("prow", "pcol")),
        P(),
        P(),
    )
    out_specs = (P(("prow", "pcol"), None), P(), P(), P(("prow", "pcol"), None), P())
    n, m = mesh.shape["prow"], mesh.shape["pcol"]

    def body(*args):
        return on_device(n, m, *args)

    return jax.shard_map(body, mesh=mesh, in_specs=in_specs, out_specs=out_specs, check_vma=False)
```

profile of v0, /device:TPU:0, one launch (start us, length us, event | category | flops | bytes accessed | tf_op | source)
XLA Modules:
  0.0 91.7 jit_solution(8947761738902985003)
XLA Ops:
  1.8 1.7 %bitcast_select_fusion.mine = bf16[1024,512]{1,0:T(8,128)(2,1)S(1)} fusion(pred[128,8,4,128]{3,2,1,0:T(4,128)(4,1)S(1)} %bitcast.12, bf16[128,8,4,128]{3,2,1,0:T(4,128)(2,1)} %bitcast.13), kind=kLoop, calls=%fused_computation | loop fusion | flops 524288 | bytes 2621440 | tf_op jit(solution)/shard_map/jit(_where)/select_n | solution.py:268
  4.7 1.8 %collective-permute-done.1.got = bf16[128,512]{1,0:T(8,128)(2,1)S(1)} collective-permute-done((bf16[128,512]{1,0:T(8,128)(2,1)S(1)}, bf16[128,512]{1,0:T(8,128)(2,1)S(1)}, u32[]{:S(2)}, u32[]{:S(2)}) %collective-permute-start.1) | collective-permute-done | bytes 131104 | tf_op jit(solution)/shard_map/ppermute | solution.py:253
  6.5 3.9 %collective-permute-start.4 = (bf16[256,256]{1,0:T(8,128)(2,1)S(1)}, bf16[256,256]{1,0:T(8,128)(2,1)S(1)}, u32[]{:S(2)}, u32[]{:S(2)}) collective-permute-start(bf16[256,256]{1,0:T(8,128)(2,1)S(1)} %shard_map.119.refs_0_), channel_id=1, source_target_pairs={{0,24},{8,16},{16,8},{24,0},{1,25},{9,17},{17,9},{25,1},{2,26},{10... | collective-permute-start | bytes 393224 | tf_op jit(solution)/shard_map/ppermute | solution.py:253
  11.0 2.9 %collective-permute-start.11 = (bf16[256,256]{1,0:T(8,128)(2,1)S(1)}, bf16[256,256]{1,0:T(8,128)(2,1)S(1)}, u32[]{:S(2)}, u32[]{:S(2)}) collective-permute-start(bf16[256,256]{1,0:T(8,128)(2,1)S(1)} %shard_map.122.refs_0_), channel_id=1, source_target_pairs={{0,24},{8,16},{16,8},{24,0},{1,25},{9,17},{17,9},{25,1},{2,26},{10... | collective-permute-start | bytes 393224 | tf_op jit(solution)/shard_map/ppermute | solution.py:253
  14.4 2.4 %collective-permute-start.10 = (bf16[256,256]{1,0:T(8,128)(2,1)S(1)}, bf16[256,256]{1,0:T(8,128)(2,1)S(1)}, u32[]{:S(2)}, u32[]{:S(2)}) collective-permute-start(bf16[256,256]{1,0:T(8,128)(2,1)S(1)} %shard_map.122.refs_0_), channel_id=1, source_target_pairs={{0,16},{8,24},{16,0},{24,8},{1,17},{9,25},{17,1},{25,9},{2,18},{10... | collective-permute-start | bytes 393224 | tf_op jit(solution)/shard_map/ppermute | solution.py:253
  16.8 1.6 %collective-permute-done.3.refs_2_ = bf16[256,256]{1,0:T(8,128)(2,1)S(1)} collective-permute-done((bf16[256,256]{1,0:T(8,128)(2,1)S(1)}, bf16[256,256]{1,0:T(8,128)(2,1)S(1)}, u32[]{:S(2)}, u32[]{:S(2)}) %collective-permute-start.3) | collective-permute-done | bytes 131104 | tf_op jit(solution)/shard_map/ppermute | solution.py:253
  20.5 2.1 %collective-permute-done.10.refs_2_ = bf16[256,256]{1,0:T(8,128)(2,1)S(1)} collective-permute-done((bf16[256,256]{1,0:T(8,128)(2,1)S(1)}, bf16[256,256]{1,0:T(8,128)(2,1)S(1)}, u32[]{:S(2)}, u32[]{:S(2)}) %collective-permute-start.10) | collective-permute-done | bytes 131104 | tf_op jit(solution)/shard_map/ppermute | solution.py:253
  24.4 1.6 %collective-permute-start.5 = (bf16[256,256]{1,0:T(8,128)(2,1)S(1)}, bf16[256,256]{1,0:T(8,128)(2,1)S(1)}, u32[]{:S(2)}, u32[]{:S(2)}) collective-permute-start(bf16[256,256]{1,0:T(8,128)(2,1)S(1)} %get-tuple-element.35), channel_id=1, source_target_pairs={{0,2},{1,3},{2,0},{3,1},{4,6},{5,7},{6,4},{7,5},{8,10},{9,11},{10,... | collective-permute-start | bytes 393224 | tf_op jit(solution)/shard_map/ppermute | solution.py:253
  26.0 2.6 %collective-permute-start.6 = (bf16[256,256]{1,0:T(8,128)(2,1)S(1)}, bf16[256,256]{1,0:T(8,128)(2,1)S(1)}, u32[]{:S(2)}, u32[]{:S(2)}) collective-permute-start(bf16[256,256]{1,0:T(8,128)(2,1)S(1)} %get-tuple-element.36), channel_id=1, source_target_pairs={{0,4},{1,5},{2,6},{3,7},{4,0},{5,1},{6,2},{7,3},{8,12},{9,13},{10,... | collective-permute-start | bytes 393224 | tf_op jit(solution)/shard_map/ppermute | solution.py:253
  28.8 3.6 %collective-permute-done.5.refs_1_ = bf16[256,256]{1,0:T(8,128)(2,1)S(1)} collective-permute-done((bf16[256,256]{1,0:T(8,128)(2,1)S(1)}, bf16[256,256]{1,0:T(8,128)(2,1)S(1)}, u32[]{:S(2)}, u32[]{:S(2)}) %collective-permute-start.5) | collective-permute-done | bytes 131104 | tf_op jit(solution)/shard_map/ppermute | solution.py:253
  32.5 6.5 %collective-permute-done.6.refs_2_ = bf16[256,256]{1,0:T(8,128)(2,1)S(1)} collective-permute-done((bf16[256,256]{1,0:T(8,128)(2,1)S(1)}, bf16[256,256]{1,0:T(8,128)(2,1)S(1)}, u32[]{:S(2)}, u32[]{:S(2)}) %collective-permute-start.6) | collective-permute-done | bytes 131104 | tf_op jit(solution)/shard_map/ppermute | solution.py:253
  40.8 1.9 %collective-permute-start.18 = (bf16[64,256]{1,0:T(8,128)(2,1)S(1)}, bf16[64,256]{1,0:T(8,128)(2,1)S(1)}, u32[]{:S(2)}, u32[]{:S(2)}) collective-permute-start(bf16[64,256]{1,0:T(8,128)(2,1)S(1)} %get-tuple-element.50), channel_id=1, source_target_pairs={{0,24},{8,16},{16,8},{24,0},{1,25},{9,17},{17,9},{25,1},{2,26},{10... | collective-permute-start | bytes 98312 | tf_op jit(solution)/shard_map/ppermute | solution.py:253
  43.2 2.4 %collective-permute-start.12 = (bf16[256,256]{1,0:T(8,128)(2,1)S(1)}, bf16[256,256]{1,0:T(8,128)(2,1)S(1)}, u32[]{:S(2)}, u32[]{:S(2)}) collective-permute-start(bf16[256,256]{1,0:T(8,128)(2,1)S(1)} %get-tuple-element.40), channel_id=1, source_target_pairs={{0,2},{1,3},{2,0},{3,1},{4,6},{5,7},{6,4},{7,5},{8,10},{9,11},{10,... | collective-permute-start | bytes 393224 | tf_op jit(solution)/shard_map/ppermute | solution.py:253
  45.7 2.3 %collective-permute-start.13 = (bf16[256,256]{1,0:T(8,128)(2,1)S(1)}, bf16[256,256]{1,0:T(8,128)(2,1)S(1)}, u32[]{:S(2)}, u32[]{:S(2)}) collective-permute-start(bf16[256,256]{1,0:T(8,128)(2,1)S(1)} %get-tuple-element.41), channel_id=1, source_target_pairs={{0,4},{1,5},{2,6},{3,7},{4,0},{5,1},{6,2},{7,3},{8,12},{9,13},{10,... | collective-permute-start | bytes 393224 | tf_op jit(solution)/shard_map/ppermute | solution.py:253
  50.3 6.6 %collective-permute-done.13.refs_2_ = bf16[256,256]{1,0:T(8,128)(2,1)S(1)} collective-permute-done((bf16[256,256]{1,0:T(8,128)(2,1)S(1)}, bf16[256,256]{1,0:T(8,128)(2,1)S(1)}, u32[]{:S(2)}, u32[]{:S(2)}) %collective-permute-start.13) | collective-permute-done | bytes 131104 | tf_op jit(solution)/shard_map/ppermute | solution.py:253
  59.0 1.6 %collective-permute-start.32 = (bf16[64,256]{1,0:T(8,128)(2,1)S(1)}, bf16[64,256]{1,0:T(8,128)(2,1)S(1)}, u32[]{:S(2)}, u32[]{:S(2)}) collective-permute-start(bf16[64,256]{1,0:T(8,128)(2,1)S(1)} %get-tuple-element.61), channel_id=1, source_target_pairs={{0,24},{8,16},{16,8},{24,0},{1,25},{9,17},{17,9},{25,1},{2,26},{10... | collective-permute-start | bytes 98312 | tf_op jit(solution)/shard_map/ppermute | solution.py:253
  62.3 1.5 %collective-permute-done.32.refs_3_ = bf16[64,256]{1,0:T(8,128)(2,1)S(1)} collective-permute-done((bf16[64,256]{1,0:T(8,128)(2,1)S(1)}, bf16[64,256]{1,0:T(8,128)(2,1)S(1)}, u32[]{:S(2)}, u32[]{:S(2)}) %collective-permute-start.32) | collective-permute-done | bytes 32800 | tf_op jit(solution)/shard_map/ppermute | solution.py:253
  64.1 2.1 %collective-permute-start.33 = (bf16[64,512]{1,0:T(8,128)(2,1)S(1)}, bf16[64,512]{1,0:T(8,128)(2,1)S(1)}, u32[]{:S(2)}, u32[]{:S(2)}) collective-permute-start(bf16[64,512]{1,0:T(8,128)(2,1)S(1)} %shard_map.129), channel_id=1, source_target_pairs={{0,2},{1,3},{2,0},{3,1},{4,6},{5,7},{6,4},{7,5},{8,10},{9,11},{10,... | collective-permute-start | bytes 196616 | tf_op jit(solution)/shard_map/ppermute | solution.py:253
  68.5 3.1 %collective-permute-start.34 = (bf16[64,512]{1,0:T(8,128)(2,1)S(1)}, bf16[64,512]{1,0:T(8,128)(2,1)S(1)}, u32[]{:S(2)}, u32[]{:S(2)}) collective-permute-start(bf16[64,512]{1,0:T(8,128)(2,1)S(1)} %add_convert_fusion.3), channel_id=1, source_target_pairs={{0,4},{1,5},{2,6},{3,7},{4,0},{5,1},{6,2},{7,3},{8,12},{9,13},{10,... | collective-permute-start | bytes 196616 | tf_op jit(solution)/shard_map/ppermute | solution.py:253
  71.6 2.2 %collective-permute-done.22 = bf16[64,1024]{1,0:T(8,128)(2,1)S(1)} collective-permute-done((bf16[64,1024]{1,0:T(8,128)(2,1)S(1)}, bf16[64,1024]{1,0:T(8,128)(2,1)S(1)}, u32[]{:S(2)}, u32[]{:S(2)}) %collective-permute-start.22) | collective-permute-done | bytes 131104 | tf_op jit(solution)/shard_map/ppermute | solution.py:253
  73.8 1.5 %collective-permute-start.25 = (bf16[64,1024]{1,0:T(8,128)(2,1)S(1)}, bf16[64,1024]{1,0:T(8,128)(2,1)S(1)}, u32[]{:S(2)}, u32[]{:S(2)}) collective-permute-start(bf16[64,1024]{1,0:T(8,128)(2,1)S(1)} %add_convert_fusion.refs_0_), channel_id=1, source_target_pairs={{0,24},{8,16},{16,8},{24,0},{1,25},{9,17},{17,9},{25,1},{2,26},{10... | collective-permute-start | bytes 393224 | tf_op jit(solution)/shard_map/ppermute | solution.py:253
  77.4 1.5 %collective-permute-start.37 = (bf16[64,512]{1,0:T(8,128)(2,1)S(1)}, bf16[64,512]{1,0:T(8,128)(2,1)S(1)}, u32[]{:S(2)}, u32[]{:S(2)}) collective-permute-start(bf16[64,512]{1,0:T(8,128)(2,1)S(1)} %add_convert_fusion.2.refs_0_), channel_id=1, source_target_pairs={{0,24},{8,16},{16,8},{24,0},{1,25},{9,17},{17,9},{25,1},{2,26},{10... | collective-permute-start | bytes 196616 | tf_op jit(solution)/shard_map/ppermute | solution.py:253
  80.2 2.4 %collective-permute-done.37.refs_3_ = bf16[64,512]{1,0:T(8,128)(2,1)S(1)} collective-permute-done((bf16[64,512]{1,0:T(8,128)(2,1)S(1)}, bf16[64,512]{1,0:T(8,128)(2,1)S(1)}, u32[]{:S(2)}, u32[]{:S(2)}) %collective-permute-start.37) | collective-permute-done | bytes 65568 | tf_op jit(solution)/shard_map/ppermute | solution.py:253
  89.0 1.6 %shard_map.128 = (bf16[512,512]{1,0:T(8,128)(2,1)}, bf16[512,512]{1,0:T(8,128)(2,1)}, f32[512,512]{1,0:T(8,128)S(1)}) custom-call(bf16[64,1024]{1,0:T(8,128)(2,1)S(1)} %add_convert_fusion.refs_0_, bf16[64,1024]{1,0:T(8,128)(2,1)S(1)} %collective-permute-done.23.refs_1_, bf16[64,1024]{1,0:T(8,128)(2,1)S(1)} %collective-permute-done.24.refs_2_, ...), custom_call_target="tpu_custom_call" | custom-call | flops 805306368 | bytes 6291456 | tf_op jit(solution)/shard_map/pallas_call | solution.py:31
  (95 shorter events, 29.3 us)
Async XLA Ops:
  3.5 16.1 %collective-permute-start = (bf16[1024,512]{1,0:T(8,128)(2,1)S(1)}, bf16[1024,512]{1,0:T(8,128)(2,1)S(1)}, u32[]{:S(2)}, u32[]{:S(2)}) collective-permute-start(bf16[1024,512]{1,0:T(8,128)(2,1)S(1)} %bitcast_select_fusion.mine), channel_id=1, source_target_pairs={{0,1},{1,0},{2,3},{3,2},{4,5},{5,4},{6,7},{7,6},{8,9},{9,8},{10,11... | collective-permute-start | bytes 3145736 | tf_op jit(solution)/shard_map/ppermute | solution.py:253
  4.2 6.8 %collective-permute-start.8 = (bf16[128,512]{1,0:T(8,128)(2,1)S(1)}, bf16[128,512]{1,0:T(8,128)(2,1)S(1)}, u32[]{:S(2)}, u32[]{:S(2)}) collective-permute-start(bf16[128,512]{1,0:T(8,128)(2,1)S(1)} %broadcast_select_fusion.own), channel_id=1, source_target_pairs={{0,1},{1,0},{2,3},{3,2},{4,5},{5,4},{6,7},{7,6},{8,9},{9,8},{10,11... | collective-permute-start | bytes 393224 | tf_op jit(solution)/shard_map/ppermute | solution.py:253
  6.5 7.8 %collective-permute-start.4 = (bf16[256,256]{1,0:T(8,128)(2,1)S(1)}, bf16[256,256]{1,0:T(8,128)(2,1)S(1)}, u32[]{:S(2)}, u32[]{:S(2)}) collective-permute-start(bf16[256,256]{1,0:T(8,128)(2,1)S(1)} %shard_map.119.refs_0_), channel_id=1, source_target_pairs={{0,24},{8,16},{16,8},{24,0},{1,25},{9,17},{17,9},{25,1},{2,26},{10... | collective-permute-start | bytes 393224 | tf_op jit(solution)/shard_map/ppermute | solution.py:253
  10.4 7.9 %collective-permute-start.3 = (bf16[256,256]{1,0:T(8,128)(2,1)S(1)}, bf16[256,256]{1,0:T(8,128)(2,1)S(1)}, u32[]{:S(2)}, u32[]{:S(2)}) collective-permute-start(bf16[256,256]{1,0:T(8,128)(2,1)S(1)} %shard_map.119.refs_0_), channel_id=1, source_target_pairs={{0,16},{8,24},{16,0},{24,8},{1,17},{9,25},{17,1},{25,9},{2,18},{10... | collective-permute-start | bytes 393224 | tf_op jit(solution)/shard_map/ppermute | solution.py:253
  10.9 8.7 %collective-permute-start.2 = (bf16[256,256]{1,0:T(8,128)(2,1)S(1)}, bf16[256,256]{1,0:T(8,128)(2,1)S(1)}, u32[]{:S(2)}, u32[]{:S(2)}) collective-permute-start(bf16[256,256]{1,0:T(8,128)(2,1)S(1)} %shard_map.119.refs_0_), channel_id=1, source_target_pairs={{0,8},{8,0},{16,24},{24,16},{1,9},{9,1},{17,25},{25,17},{2,10},{10... | collective-permute-start | bytes 393224 | tf_op jit(solution)/shard_map/ppermute | solution.py:253
  11.0 9.4 %collective-permute-start.11 = (bf16[256,256]{1,0:T(8,128)(2,1)S(1)}, bf16[256,256]{1,0:T(8,128)(2,1)S(1)}, u32[]{:S(2)}, u32[]{:S(2)}) collective-permute-start(bf16[256,256]{1,0:T(8,128)(2,1)S(1)} %shard_map.122.refs_0_), channel_id=1, source_target_pairs={{0,24},{8,16},{16,8},{24,0},{1,25},{9,17},{17,9},{25,1},{2,26},{10... | collective-permute-start | bytes 393224 | tf_op jit(solution)/shard_map/ppermute | solution.py:253
  14.4 8.3 %collective-permute-start.10 = (bf16[256,256]{1,0:T(8,128)(2,1)S(1)}, bf16[256,256]{1,0:T(8,128)(2,1)S(1)}, u32[]{:S(2)}, u32[]{:S(2)}) collective-permute-start(bf16[256,256]{1,0:T(8,128)(2,1)S(1)} %shard_map.122.refs_0_), channel_id=1, source_target_pairs={{0,16},{8,24},{16,0},{24,8},{1,17},{9,25},{17,1},{25,9},{2,18},{10... | collective-permute-start | bytes 393224 | tf_op jit(solution)/shard_map/ppermute | solution.py:253
  20.4 28.9 %collective-permute-start.19 = (bf16[1024,256]{1,0:T(8,128)(2,1)S(1)}, bf16[1024,256]{1,0:T(8,128)(2,1)S(1)}, u32[]{:S(2)}, u32[]{:S(2)}) collective-permute-start(bf16[1024,256]{1,0:T(8,128)(2,1)S(1)} %get-tuple-element.51.refs_4_), channel_id=1, source_target_pairs={{0,1},{1,0},{2,3},{3,2},{4,5},{5,4},{6,7},{7,6},{8,9},{9,8},{10,11... | collective-permute-start | bytes 1572872 | tf_op jit(solution)/shard_map/ppermute | solution.py:253
  24.3 25.0 %collective-permute-start.20 = (bf16[1024,256]{1,0:T(8,128)(2,1)S(1)}, bf16[1024,256]{1,0:T(8,128)(2,1)S(1)}, u32[]{:S(2)}, u32[]{:S(2)}) collective-permute-start(bf16[1024,256]{1,0:T(8,128)(2,1)S(1)} %get-tuple-element.52.refs_6_.refs_4_), channel_id=1, source_target_pairs={{0,1},{1,0},{2,3},{3,2},{4,5},{5,4},{6,7},{7,6},{8,9},{9,8},{10,11... | collective-permute-start | bytes 1572872 | tf_op jit(solution)/shard_map/ppermute | solution.py:253
  24.4 8.1 %collective-permute-start.5 = (bf16[256,256]{1,0:T(8,128)(2,1)S(1)}, bf16[256,256]{1,0:T(8,128)(2,1)S(1)}, u32[]{:S(2)}, u32[]{:S(2)}) collective-permute-start(bf16[256,256]{1,0:T(8,128)(2,1)S(1)} %get-tuple-element.35), channel_id=1, source_target_pairs={{0,2},{1,3},{2,0},{3,1},{4,6},{5,7},{6,4},{7,5},{8,10},{9,11},{10,... | collective-permute-start | bytes 393224 | tf_op jit(solution)/shard_map/ppermute | solution.py:253
  26.0 12.9 %collective-permute-start.6 = (bf16[256,256]{1,0:T(8,128)(2,1)S(1)}, bf16[256,256]{1,0:T(8,128)(2,1)S(1)}, u32[]{:S(2)}, u32[]{:S(2)}) collective-permute-start(bf16[256,256]{1,0:T(8,128)(2,1)S(1)} %get-tuple-element.36), channel_id=1, source_target_pairs={{0,4},{1,5},{2,6},{3,7},{4,0},{5,1},{6,2},{7,3},{8,12},{9,13},{10,... | collective-permute-start | bytes 393224 | tf_op jit(solution)/shard_map/ppermute | solution.py:253
  28.6 10.3 %collective-permute-start.7 = (bf16[256,256]{1,0:T(8,128)(2,1)S(1)}, bf16[256,256]{1,0:T(8,128)(2,1)S(1)}, u32[]{:S(2)}, u32[]{:S(2)}) collective-permute-start(bf16[256,256]{1,0:T(8,128)(2,1)S(1)} %get-tuple-element.37), channel_id=1, source_target_pairs={{0,6},{1,7},{2,4},{3,5},{4,2},{5,3},{6,0},{7,1},{8,14},{9,15},{10,... | collective-permute-start | bytes 393224 | tf_op jit(solution)/shard_map/ppermute | solution.py:253
  40.8 7.2 %collective-permute-start.18 = (bf16[64,256]{1,0:T(8,128)(2,1)S(1)}, bf16[64,256]{1,0:T(8,128)(2,1)S(1)}, u32[]{:S(2)}, u32[]{:S(2)}) collective-permute-start(bf16[64,256]{1,0:T(8,128)(2,1)S(1)} %get-tuple-element.50), channel_id=1, source_target_pairs={{0,24},{8,16},{16,8},{24,0},{1,25},{9,17},{17,9},{25,1},{2,26},{10... | collective-permute-start | bytes 98312 | tf_op jit(solution)/shard_map/ppermute | solution.py:253
  43.2 7.0 %collective-permute-start.12 = (bf16[256,256]{1,0:T(8,128)(2,1)S(1)}, bf16[256,256]{1,0:T(8,128)(2,1)S(1)}, u32[]{:S(2)}, u32[]{:S(2)}) collective-permute-start(bf16[256,256]{1,0:T(8,128)(2,1)S(1)} %get-tuple-element.40), channel_id=1, source_target_pairs={{0,2},{1,3},{2,0},{3,1},{4,6},{5,7},{6,4},{7,5},{8,10},{9,11},{10,... | collective-permute-start | bytes 393224 | tf_op jit(solution)/shard_map/ppermute | solution.py:253
  45.7 11.2 %collective-permute-start.13 = (bf16[256,256]{1,0:T(8,128)(2,1)S(1)}, bf16[256,256]{1,0:T(8,128)(2,1)S(1)}, u32[]{:S(2)}, u32[]{:S(2)}) collective-permute-start(bf16[256,256]{1,0:T(8,128)(2,1)S(1)} %get-tuple-element.41), channel_id=1, source_target_pairs={{0,4},{1,5},{2,6},{3,7},{4,0},{5,1},{6,2},{7,3},{8,12},{9,13},{10,... | collective-permute-start | bytes 393224 | tf_op jit(solution)/shard_map/ppermute | solution.py:253
  47.9 8.9 %collective-permute-start.14 = (bf16[256,256]{1,0:T(8,128)(2,1)S(1)}, bf16[256,256]{1,0:T(8,128)(2,1)S(1)}, u32[]{:S(2)}, u32[]{:S(2)}) collective-permute-start(bf16[256,256]{1,0:T(8,128)(2,1)S(1)} %get-tuple-element.42), channel_id=1, source_target_pairs={{0,6},{1,7},{2,4},{3,5},{4,2},{5,3},{6,0},{7,1},{8,14},{9,15},{10,... | collective-permute-start | bytes 393224 | tf_op jit(solution)/shard_map/ppermute | solution.py:253
  49.8 16.5 %collective-permute-start.21 = (bf16[64,1024]{1,0:T(8,128)(2,1)S(1)}, bf16[64,1024]{1,0:T(8,128)(2,1)S(1)}, u32[]{:S(2)}, u32[]{:S(2)}) collective-permute-start(bf16[64,1024]{1,0:T(8,128)(2,1)S(1)} %shard_map.126), channel_id=1, source_target_pairs={{0,2},{1,3},{2,0},{3,1},{4,6},{5,7},{6,4},{7,5},{8,10},{9,11},{10,... | collective-permute-start | bytes 393224 | tf_op jit(solution)/shard_map/ppermute | solution.py:253
  60.6 18.4 %collective-permute-start.15 = (f32[128,512]{1,0:T(8,128)S(1)}, f32[128,512]{1,0:T(8,128)S(1)}, u32[]{:S(2)}, u32[]{:S(2)}) collective-permute-start(f32[128,512]{1,0:T(8,128)S(1)} %get-tuple-element.45), channel_id=1, source_target_pairs={{0,1},{1,0},{2,3},{3,2},{4,5},{5,4},{6,7},{7,6},{8,9},{9,8},{10,11... | collective-permute-start | bytes 786440 | tf_op jit(solution)/shard_map/ppermute | solution.py:253
  66.3 7.5 %collective-permute-start.22 = (bf16[64,1024]{1,0:T(8,128)(2,1)S(1)}, bf16[64,1024]{1,0:T(8,128)(2,1)S(1)}, u32[]{:S(2)}, u32[]{:S(2)}) collective-permute-start(bf16[64,1024]{1,0:T(8,128)(2,1)S(1)} %add_convert_fusion.1), channel_id=1, source_target_pairs={{0,4},{1,5},{2,6},{3,7},{4,0},{5,1},{6,2},{7,3},{8,12},{9,13},{10,... | collective-permute-start | bytes 393224 | tf_op jit(solution)/shard_map/ppermute | solution.py:253
  68.5 8.9 %collective-permute-start.34 = (bf16[64,512]{1,0:T(8,128)(2,1)S(1)}, bf16[64,512]{1,0:T(8,128)(2,1)S(1)}, u32[]{:S(2)}, u32[]{:S(2)}) collective-permute-start(bf16[64,512]{1,0:T(8,128)(2,1)S(1)} %add_convert_fusion.3), channel_id=1, source_target_pairs={{0,4},{1,5},{2,6},{3,7},{4,0},{5,1},{6,2},{7,3},{8,12},{9,13},{10,... | collective-permute-start | bytes 196616 | tf_op jit(solution)/shard_map/ppermute | solution.py:253
  73.8 8.8 %collective-permute-start.25 = (bf16[64,1024]{1,0:T(8,128)(2,1)S(1)}, bf16[64,1024]{1,0:T(8,128)(2,1)S(1)}, u32[]{:S(2)}, u32[]{:S(2)}) collective-permute-start(bf16[64,1024]{1,0:T(8,128)(2,1)S(1)} %add_convert_fusion.refs_0_), channel_id=1, source_target_pairs={{0,24},{8,16},{16,8},{24,0},{1,25},{9,17},{17,9},{25,1},{2,26},{10... | collective-permute-start | bytes 393224 | tf_op jit(solution)/shard_map/ppermute | solution.py:253
  75.4 7.8 %collective-permute-start.24 = (bf16[64,1024]{1,0:T(8,128)(2,1)S(1)}, bf16[64,1024]{1,0:T(8,128)(2,1)S(1)}, u32[]{:S(2)}, u32[]{:S(2)}) collective-permute-start(bf16[64,1024]{1,0:T(8,128)(2,1)S(1)} %add_convert_fusion.refs_0_), channel_id=1, source_target_pairs={{0,16},{8,24},{16,0},{24,8},{1,17},{9,25},{17,1},{25,9},{2,18},{10... | collective-permute-start | bytes 393224 | tf_op jit(solution)/shard_map/ppermute | solution.py:253
  76.6 6.6 %collective-permute-start.23 = (bf16[64,1024]{1,0:T(8,128)(2,1)S(1)}, bf16[64,1024]{1,0:T(8,128)(2,1)S(1)}, u32[]{:S(2)}, u32[]{:S(2)}) collective-permute-start(bf16[64,1024]{1,0:T(8,128)(2,1)S(1)} %add_convert_fusion.refs_0_), channel_id=1, source_target_pairs={{0,8},{8,0},{16,24},{24,16},{1,9},{9,1},{17,25},{25,17},{2,10},{10... | collective-permute-start | bytes 393224 | tf_op jit(solution)/shard_map/ppermute | solution.py:253
  82.7 5.8 %collective-permute-start.29 = (bf16[64,1024]{1,0:T(8,128)(2,1)S(1)}, bf16[64,1024]{1,0:T(8,128)(2,1)S(1)}, u32[]{:S(2)}, u32[]{:S(2)}) collective-permute-start(bf16[64,1024]{1,0:T(8,128)(2,1)S(1)} %collective-permute-done.25.refs_3_), channel_id=1, source_target_pairs={{0,1},{1,0},{2,3},{3,2},{4,5},{5,4},{6,7},{7,6},{8,9},{9,8},{10,11... | collective-permute-start | bytes 393224 | tf_op jit(solution)/shard_map/ppermute | solution.py:253
  (24 other events, 122.4 us)
where the time goes:
time: 91.9 us; the launch traced here: 91.7 us
  starting transfers between devices  46.4 us (50%)
  waiting for transfers between devices  34.7 us (38%)
  Pallas kernels  6.63 us (7%)
  other arithmetic  2.56 us (3%)
    ppermute x42, starting transfers between devices, on_device(): lax.ppermute(x, axis, [(k, k ^ s) for k in range(size)])  46.4 us
    ppermute x42, waiting for transfers between devices, on_device(): lax.ppermute(x, axis, [(k, k ^ s) for k in range(size)])  34.7 us
    pallas_call x12, Pallas kernels, call(): pl.pallas_call(body, out_shape=out, in_specs=[VMEM] * len(args), out_spec...  6.63 us
  transfers between devices with their start and end apart: 42, of which 16 were waited for; matrix products, arithmetic and copies ran while one was open for 0% of the time, Pallas kernels for 6%

commit v1 on v0

--- a/solution.py
+++ b/solution.py
@@ -80,30 +80,56 @@
     return call(start_body, out, [], [one, top], 2 * top.shape[0] ** 3)
 
 
+def sequence(nz):
+    if nz == 1:
+        return [0]
+    stay = [2 * k for k in sequence(nz // 2)]
+    return stay + [k ^ 1 for k in stay]
+
+
 def product_body(n, nz, mine, theirs, *refs):
-    q, outs, rhs = refs[:n], refs[n : n + nz], refs[n + nz]
+    q, (stay, leave, rhs) = refs[:n], refs[n:]
     p, z, c = place()
     rows = q[0].shape[0] // 2
     depth = rhs.shape[0] // 2
     for s in range(n):
         rhs[block(p ^ s, rows), :] = q[s][:rows, :]
         rhs[pl.ds(pl.multiple_of(depth + (p ^ s) * rows, rows), rows), :] = q[s][rows:, :]
-    for s in range(nz):
-        span = block(z ^ s, 2 * rows)
-        value = dot(mine[span, :], rhs[:depth, :]) + dot(theirs[span, :], rhs[depth:, :])
-        for t in range(2):
-            outs[s][block(c ^ t, rows), :] = value[t * rows : (t + 1) * rows].astype(outs[s].dtype)
+    order = sequence(nz)
+    for k in range(nz // 2, nz):
+        emit(leave, k - nz // 2, order[k], z, c, rows, mine, theirs, rhs)
+    for k in range(nz // 2):
+        emit(stay, k, order[k], z, c, rows, mine, theirs, rhs)
+
+
+def emit(out, k, offset, z, c, rows, mine, theirs, rhs):
+    depth = rhs.shape[0] // 2
+    span = block(z ^ offset, 2 * rows)
+    value = dot(mine[span, :], rhs[:depth, :]) + dot(theirs[span, :], rhs[depth:, :])
+    for t in range(2):
+        out[block(2 * k + (c ^ t), rows), :] = value[t * rows : (t + 1) * rows].astype(out.dtype)
 
 
 def product(mine, theirs, q, nz):
-    n, shape = len(q), q[0].shape
+    n, (rows, half) = len(q), q[0].shape
     depth = mine.shape[1]
-    out = [sds(shape, F32)] + [sds(shape, BF)] * (nz - 1) + [sds((2 * depth, shape[1]), BF)]
-    *parts, rhs = call(
+    shape = (nz // 2 * rows, half)
+    out = [sds(shape, F32), sds(shape, BF), sds((2 * depth, half), BF)]
+    return call(
         functools.partial(product_body, n, nz), out, [],
-        [mine, theirs, *q], 4 * mine.shape[0] * depth * shape[1],
-    )
-    return parts, rhs
+        [mine, theirs, *q], 4 * mine.shape[0] * depth * half,
+    )
+
+
+def fold_body(held, got, stay, leave):
+    rows = stay.shape[0]
+    stay[...] = held[:rows] + got[:rows].astype(F32)
+    leave[...] = (held[rows:] + got[rows:].astype(F32)).astype(BF)
+
+
+def fold(held, got):
+    shape = (held.shape[0] // 2, held.shape[1])
+    return call(fold_body, [sds(shape, F32), sds(shape, BF)], [], [held, got], 2 * held.size)
 
 
 def first_body(n, nz, *refs):
@@ -271,8 +297,12 @@
     others = swap(masked)
     start, top_t = start_parts(diag_one, panel_top)
 
-    def exchange(parts):
-        return [parts[0]] + [over_z(parts[s], s) for s in range(1, nz)]
+    def exchange(stay, leave):
+        got, s = over_z(leave, 1), 2
+        while s < nz:
+            stay, leave = fold(stay, got)
+            got, s = over_z(leave, s), 2 * s
+        return [stay, got]
 
     def spread(pieces):
         return [pieces[0]] + [over_p(pieces[s], s) for s in range(1, n)]
@@ -285,10 +315,10 @@
         got = [here] + [over_p(here, s) for s in range(1, n)]
         return got, [swap(got[s]) for s in range(n)]
 
-    parts_one, rows_one = product(masked, others, gathered_one, nz)
-    parts_one = exchange(parts_one)
-    parts_two, rows_two = product(masked, others, gathered_two, nz)
-    parts_two = exchange(parts_two)
+    *parts_one, rows_one = product(masked, others, gathered_one, nz)
+    parts_one = exchange(*parts_one)
+    *parts_two, rows_two = product(masked, others, gathered_two, nz)
+    parts_two = exchange(*parts_two)
     panels = [rows_one, swap(rows_one), rows_two, swap(rows_two)]
     keep_one, give_one, *pieces_one = first_turn(parts_one, n)
     pieces_one = spread(pieces_one)

time: 91.9 us -> 87.8 us (0.955)
  waiting for transfers between devices: 34.7 us -> 31.2 us
    ppermute x42 -> x40, waiting for transfers between devices: 34.7 us -> 31.2 us  [on_device(): lax.ppermute(x, axis, [(k, k ^ s) for k in range(size)])]
    ppermute x42 -> x40, starting transfers between devices: 46.4 us -> 45.7 us  [on_device(): lax.ppermute(x, axis, [(k, k ^ s) for k in range(size)])]
    pallas_call x12 -> x14, Pallas kernels: 6.63 us -> 6.76 us  [call(): pl.pallas_call(body, out_shape=out, in_specs=[VMEM] * len(args), out_spec...]
  transfers between devices with their start and end apart: 42 -> 40, of which waited for: 16 -> 16; matrix products, arithmetic and copies ran while one was open for 0% -> 0% of each run, Pallas kernels for 6% -> 7%
where the time goes in v1:
time: 87.8 us; the launch traced here: 87.7 us
  starting transfers between devices  45.7 us (52%)
  waiting for transfers between devices  31.2 us (36%)
  Pallas kernels  6.76 us (8%)
  other arithmetic  2.56 us (3%)
    ppermute x40, starting transfers between devices, on_device(): lax.ppermute(x, axis, [(k, k ^ s) for k in range(size)])  45.7 us
    ppermute x40, waiting for transfers between devices, on_device(): lax.ppermute(x, axis, [(k, k ^ s) for k in range(size)])  31.2 us
    pallas_call x14, Pallas kernels, call(): pl.pallas_call(body, out_shape=out, in_specs=[VMEM] * len(args), out_spec...  6.76 us
  transfers between devices with their start and end apart: 40, of which 16 were waited for; matrix products, arithmetic and copies ran while one was open for 0% of the time, Pallas kernels for 7%

profile of v1, /device:TPU:0, one launch (start us, length us, event | category | flops | bytes accessed | tf_op | source)
XLA Modules:
  0.0 87.7 jit_solution(13515341901924465300)
XLA Ops:
  1.8 1.7 %bitcast_select_fusion.mine = bf16[1024,512]{1,0:T(8,128)(2,1)S(1)} fusion(pred[128,8,4,128]{3,2,1,0:T(4,128)(4,1)S(1)} %bitcast.12, bf16[128,8,4,128]{3,2,1,0:T(4,128)(2,1)} %bitcast.13), kind=kLoop, calls=%fused_computation | loop fusion | flops 524288 | bytes 2621440 | tf_op jit(solution)/shard_map/jit(_where)/select_n | solution.py:294
  4.7 1.8 %collective-permute-done.1.got = bf16[128,512]{1,0:T(8,128)(2,1)S(1)} collective-permute-done((bf16[128,512]{1,0:T(8,128)(2,1)S(1)}, bf16[128,512]{1,0:T(8,128)(2,1)S(1)}, u32[]{:S(2)}, u32[]{:S(2)}) %collective-permute-start.1) | collective-permute-done | bytes 131104 | tf_op jit(solution)/shard_map/ppermute | solution.py:279
  6.5 3.9 %collective-permute-start.4 = (bf16[256,256]{1,0:T(8,128)(2,1)S(1)}, bf16[256,256]{1,0:T(8,128)(2,1)S(1)}, u32[]{:S(2)}, u32[]{:S(2)}) collective-permute-start(bf16[256,256]{1,0:T(8,128)(2,1)S(1)} %shard_map.119.refs_0_), channel_id=1, source_target_pairs={{0,24},{8,16},{16,8},{24,0},{1,25},{9,17},{17,9},{25,1},{2,26},{10... | collective-permute-start | bytes 393224 | tf_op jit(solution)/shard_map/ppermute | solution.py:279
  11.0 2.9 %collective-permute-start.10 = (bf16[256,256]{1,0:T(8,128)(2,1)S(1)}, bf16[256,256]{1,0:T(8,128)(2,1)S(1)}, u32[]{:S(2)}, u32[]{:S(2)}) collective-permute-start(bf16[256,256]{1,0:T(8,128)(2,1)S(1)} %shard_map.123.refs_0_), channel_id=1, source_target_pairs={{0,24},{8,16},{16,8},{24,0},{1,25},{9,17},{17,9},{25,1},{2,26},{10... | collective-permute-start | bytes 393224 | tf_op jit(solution)/shard_map/ppermute | solution.py:279
  14.4 2.4 %collective-permute-start.9 = (bf16[256,256]{1,0:T(8,128)(2,1)S(1)}, bf16[256,256]{1,0:T(8,128)(2,1)S(1)}, u32[]{:S(2)}, u32[]{:S(2)}) collective-permute-start(bf16[256,256]{1,0:T(8,128)(2,1)S(1)} %shard_map.123.refs_0_), channel_id=1, source_target_pairs={{0,16},{8,24},{16,0},{24,8},{1,17},{9,25},{17,1},{25,9},{2,18},{10... | collective-permute-start | bytes 393224 | tf_op jit(solution)/shard_map/ppermute | solution.py:279
  16.8 1.6 %collective-permute-done.3.refs_2_ = bf16[256,256]{1,0:T(8,128)(2,1)S(1)} collective-permute-done((bf16[256,256]{1,0:T(8,128)(2,1)S(1)}, bf16[256,256]{1,0:T(8,128)(2,1)S(1)}, u32[]{:S(2)}, u32[]{:S(2)}) %collective-permute-start.3) | collective-permute-done | bytes 131104 | tf_op jit(solution)/shard_map/ppermute | solution.py:279
  20.5 2.1 %collective-permute-done.9.refs_2_ = bf16[256,256]{1,0:T(8,128)(2,1)S(1)} collective-permute-done((bf16[256,256]{1,0:T(8,128)(2,1)S(1)}, bf16[256,256]{1,0:T(8,128)(2,1)S(1)}, u32[]{:S(2)}, u32[]{:S(2)}) %collective-permute-start.9) | collective-permute-done | bytes 131104 | tf_op jit(solution)/shard_map/ppermute | solution.py:279
  24.4 1.6 %collective-permute-start.5 = (bf16[512,256]{1,0:T(8,128)(2,1)S(1)}, bf16[512,256]{1,0:T(8,128)(2,1)S(1)}, u32[]{:S(2)}, u32[]{:S(2)}) collective-permute-start(bf16[512,256]{1,0:T(8,128)(2,1)S(1)} %get-tuple-element.35), channel_id=1, source_target_pairs={{0,2},{1,3},{2,0},{3,1},{4,6},{5,7},{6,4},{7,5},{8,10},{9,11},{10,... | collective-permute-start | bytes 786440 | tf_op jit(solution)/shard_map/ppermute | solution.py:279
  26.5 7.2 %collective-permute-done.5.got = bf16[512,256]{1,0:T(8,128)(2,1)S(1)} collective-permute-done((bf16[512,256]{1,0:T(8,128)(2,1)S(1)}, bf16[512,256]{1,0:T(8,128)(2,1)S(1)}, u32[]{:S(2)}, u32[]{:S(2)}) %collective-permute-start.5) | collective-permute-done | bytes 262176 | tf_op jit(solution)/shard_map/ppermute | solution.py:279
  33.7 2.7 %collective-permute-start.6 = (bf16[256,256]{1,0:T(8,128)(2,1)S(1)}, bf16[256,256]{1,0:T(8,128)(2,1)S(1)}, u32[]{:S(2)}, u32[]{:S(2)}) collective-permute-start(bf16[256,256]{1,0:T(8,128)(2,1)S(1)} %get-tuple-element.37), channel_id=1, source_target_pairs={{0,4},{1,5},{2,6},{3,7},{4,0},{5,1},{6,2},{7,3},{8,12},{9,13},{10,... | collective-permute-start | bytes 393224 | tf_op jit(solution)/shard_map/ppermute | solution.py:279
  36.3 4.3 %collective-permute-done.6.refs_1_ = bf16[256,256]{1,0:T(8,128)(2,1)S(1)} collective-permute-done((bf16[256,256]{1,0:T(8,128)(2,1)S(1)}, bf16[256,256]{1,0:T(8,128)(2,1)S(1)}, u32[]{:S(2)}, u32[]{:S(2)}) %collective-permute-start.6) | collective-permute-done | bytes 131104 | tf_op jit(solution)/shard_map/ppermute | solution.py:279
  42.5 1.9 %collective-permute-start.16 = (bf16[64,256]{1,0:T(8,128)(2,1)S(1)}, bf16[64,256]{1,0:T(8,128)(2,1)S(1)}, u32[]{:S(2)}, u32[]{:S(2)}) collective-permute-start(bf16[64,256]{1,0:T(8,128)(2,1)S(1)} %get-tuple-element.50), channel_id=1, source_target_pairs={{0,24},{8,16},{16,8},{24,0},{1,25},{9,17},{17,9},{25,1},{2,26},{10... | collective-permute-start | bytes 98312 | tf_op jit(solution)/shard_map/ppermute | solution.py:279
  44.8 3.4 %collective-permute-start.12 = (bf16[256,256]{1,0:T(8,128)(2,1)S(1)}, bf16[256,256]{1,0:T(8,128)(2,1)S(1)}, u32[]{:S(2)}, u32[]{:S(2)}) collective-permute-start(bf16[256,256]{1,0:T(8,128)(2,1)S(1)} %get-tuple-element.42), channel_id=1, source_target_pairs={{0,4},{1,5},{2,6},{3,7},{4,0},{5,1},{6,2},{7,3},{8,12},{9,13},{10,... | collective-permute-start | bytes 393224 | tf_op jit(solution)/shard_map/ppermute | solution.py:279
  48.8 2.5 %collective-permute-start.19 = (bf16[64,1024]{1,0:T(8,128)(2,1)S(1)}, bf16[64,1024]{1,0:T(8,128)(2,1)S(1)}, u32[]{:S(2)}, u32[]{:S(2)}) collective-permute-start(bf16[64,1024]{1,0:T(8,128)(2,1)S(1)} %shard_map.128), channel_id=1, source_target_pairs={{0,2},{1,3},{2,0},{3,1},{4,6},{5,7},{6,4},{7,5},{8,10},{9,11},{10,... | collective-permute-start | bytes 393224 | tf_op jit(solution)/shard_map/ppermute | solution.py:279
  54.7 1.8 %collective-permute-start.30 = (bf16[64,256]{1,0:T(8,128)(2,1)S(1)}, bf16[64,256]{1,0:T(8,128)(2,1)S(1)}, u32[]{:S(2)}, u32[]{:S(2)}) collective-permute-start(bf16[64,256]{1,0:T(8,128)(2,1)S(1)} %get-tuple-element.61), channel_id=1, source_target_pairs={{0,24},{8,16},{16,8},{24,0},{1,25},{9,17},{17,9},{25,1},{2,26},{10... | collective-permute-start | bytes 98312 | tf_op jit(solution)/shard_map/ppermute | solution.py:279
  59.8 2.7 %collective-permute-start.31 = (bf16[64,512]{1,0:T(8,128)(2,1)S(1)}, bf16[64,512]{1,0:T(8,128)(2,1)S(1)}, u32[]{:S(2)}, u32[]{:S(2)}) collective-permute-start(bf16[64,512]{1,0:T(8,128)(2,1)S(1)} %shard_map.131), channel_id=1, source_target_pairs={{0,2},{1,3},{2,0},{3,1},{4,6},{5,7},{6,4},{7,5},{8,10},{9,11},{10,... | collective-permute-start | bytes 196616 | tf_op jit(solution)/shard_map/ppermute | solution.py:279
  62.6 1.7 %collective-permute-start.20 = (bf16[64,1024]{1,0:T(8,128)(2,1)S(1)}, bf16[64,1024]{1,0:T(8,128)(2,1)S(1)}, u32[]{:S(2)}, u32[]{:S(2)}) collective-permute-start(bf16[64,1024]{1,0:T(8,128)(2,1)S(1)} %add_convert_fusion.1), channel_id=1, source_target_pairs={{0,4},{1,5},{2,6},{3,7},{4,0},{5,1},{6,2},{7,3},{8,12},{9,13},{10,... | collective-permute-start | bytes 393224 | tf_op jit(solution)/shard_map/ppermute | solution.py:279
  64.3 1.7 %collective-permute-done.31 = bf16[64,512]{1,0:T(8,128)(2,1)S(1)} collective-permute-done((bf16[64,512]{1,0:T(8,128)(2,1)S(1)}, bf16[64,512]{1,0:T(8,128)(2,1)S(1)}, u32[]{:S(2)}, u32[]{:S(2)}) %collective-permute-start.31) | collective-permute-done | bytes 65568 | tf_op jit(solution)/shard_map/ppermute | solution.py:279
  67.0 2.7 %collective-permute-done.20 = bf16[64,1024]{1,0:T(8,128)(2,1)S(1)} collective-permute-done((bf16[64,1024]{1,0:T(8,128)(2,1)S(1)}, bf16[64,1024]{1,0:T(8,128)(2,1)S(1)}, u32[]{:S(2)}, u32[]{:S(2)}) %collective-permute-start.20) | collective-permute-done | bytes 131104 | tf_op jit(solution)/shard_map/ppermute | solution.py:279
  69.8 1.6 %collective-permute-start.23 = (bf16[64,1024]{1,0:T(8,128)(2,1)S(1)}, bf16[64,1024]{1,0:T(8,128)(2,1)S(1)}, u32[]{:S(2)}, u32[]{:S(2)}) collective-permute-start(bf16[64,1024]{1,0:T(8,128)(2,1)S(1)} %add_convert_fusion.refs_0_), channel_id=1, source_target_pairs={{0,24},{8,16},{16,8},{24,0},{1,25},{9,17},{17,9},{25,1},{2,26},{10... | collective-permute-start | bytes 393224 | tf_op jit(solution)/shard_map/ppermute | solution.py:279
  73.4 1.6 %collective-permute-start.35 = (bf16[64,512]{1,0:T(8,128)(2,1)S(1)}, bf16[64,512]{1,0:T(8,128)(2,1)S(1)}, u32[]{:S(2)}, u32[]{:S(2)}) collective-permute-start(bf16[64,512]{1,0:T(8,128)(2,1)S(1)} %add_convert_fusion.2.refs_0_), channel_id=1, source_target_pairs={{0,24},{8,16},{16,8},{24,0},{1,25},{9,17},{17,9},{25,1},{2,26},{10... | collective-permute-start | bytes 196616 | tf_op jit(solution)/shard_map/ppermute | solution.py:279
  76.4 2.2 %collective-permute-done.35.refs_3_ = bf16[64,512]{1,0:T(8,128)(2,1)S(1)} collective-permute-done((bf16[64,512]{1,0:T(8,128)(2,1)S(1)}, bf16[64,512]{1,0:T(8,128)(2,1)S(1)}, u32[]{:S(2)}, u32[]{:S(2)}) %collective-permute-start.35) | collective-permute-done | bytes 65568 | tf_op jit(solution)/shard_map/ppermute | solution.py:279
  79.7 1.5 %collective-permute-start.33 = (bf16[64,512]{1,0:T(8,128)(2,1)S(1)}, bf16[64,512]{1,0:T(8,128)(2,1)S(1)}, u32[]{:S(2)}, u32[]{:S(2)}) collective-permute-start(bf16[64,512]{1,0:T(8,128)(2,1)S(1)} %add_convert_fusion.2.refs_0_), channel_id=1, source_target_pairs={{0,8},{8,0},{16,24},{24,16},{1,9},{9,1},{17,25},{25,17},{2,10},{10... | collective-permute-start | bytes 196616 | tf_op jit(solution)/shard_map/ppermute | solution.py:279
  85.0 1.6 %shard_map.130 = (bf16[512,512]{1,0:T(8,128)(2,1)}, bf16[512,512]{1,0:T(8,128)(2,1)}, f32[512,512]{1,0:T(8,128)S(1)}) custom-call(bf16[64,1024]{1,0:T(8,128)(2,1)S(1)} %add_convert_fusion.refs_0_, bf16[64,1024]{1,0:T(8,128)(2,1)S(1)} %collective-permute-done.21.refs_1_, bf16[64,1024]{1,0:T(8,128)(2,1)S(1)} %collective-permute-done.22.refs_2_, ...), custom_call_target="tpu_custom_call" | custom-call | flops 805306368 | bytes 6291456 | tf_op jit(solution)/shard_map/pallas_call | solution.py:31
  (93 shorter events, 27.5 us)
Async XLA Ops:
  3.5 16.1 %collective-permute-start = (bf16[1024,512]{1,0:T(8,128)(2,1)S(1)}, bf16[1024,512]{1,0:T(8,128)(2,1)S(1)}, u32[]{:S(2)}, u32[]{:S(2)}) collective-permute-start(bf16[1024,512]{1,0:T(8,128)(2,1)S(1)} %bitcast_select_fusion.mine), channel_id=1, source_target_pairs={{0,1},{1,0},{2,3},{3,2},{4,5},{5,4},{6,7},{7,6},{8,9},{9,8},{10,11... | collective-permute-start | bytes 3145736 | tf_op jit(solution)/shard_map/ppermute | solution.py:279
  4.2 6.8 %collective-permute-start.7 = (bf16[128,512]{1,0:T(8,128)(2,1)S(1)}, bf16[128,512]{1,0:T(8,128)(2,1)S(1)}, u32[]{:S(2)}, u32[]{:S(2)}) collective-permute-start(bf16[128,512]{1,0:T(8,128)(2,1)S(1)} %broadcast_select_fusion.own), channel_id=1, source_target_pairs={{0,1},{1,0},{2,3},{3,2},{4,5},{5,4},{6,7},{7,6},{8,9},{9,8},{10,11... | collective-permute-start | bytes 393224 | tf_op jit(solution)/shard_map/ppermute | solution.py:279
  6.5 7.8 %collective-permute-start.4 = (bf16[256,256]{1,0:T(8,128)(2,1)S(1)}, bf16[256,256]{1,0:T(8,128)(2,1)S(1)}, u32[]{:S(2)}, u32[]{:S(2)}) collective-permute-start(bf16[256,256]{1,0:T(8,128)(2,1)S(1)} %shard_map.119.refs_0_), channel_id=1, source_target_pairs={{0,24},{8,16},{16,8},{24,0},{1,25},{9,17},{17,9},{25,1},{2,26},{10... | collective-permute-start | bytes 393224 | tf_op jit(solution)/shard_map/ppermute | solution.py:279
  10.4 7.9 %collective-permute-start.3 = (bf16[256,256]{1,0:T(8,128)(2,1)S(1)}, bf16[256,256]{1,0:T(8,128)(2,1)S(1)}, u32[]{:S(2)}, u32[]{:S(2)}) collective-permute-start(bf16[256,256]{1,0:T(8,128)(2,1)S(1)} %shard_map.119.refs_0_), channel_id=1, source_target_pairs={{0,16},{8,24},{16,0},{24,8},{1,17},{9,25},{17,1},{25,9},{2,18},{10... | collective-permute-start | bytes 393224 | tf_op jit(solution)/shard_map/ppermute | solution.py:279
  10.9 8.7 %collective-permute-start.2 = (bf16[256,256]{1,0:T(8,128)(2,1)S(1)}, bf16[256,256]{1,0:T(8,128)(2,1)S(1)}, u32[]{:S(2)}, u32[]{:S(2)}) collective-permute-start(bf16[256,256]{1,0:T(8,128)(2,1)S(1)} %shard_map.119.refs_0_), channel_id=1, source_target_pairs={{0,8},{8,0},{16,24},{24,16},{1,9},{9,1},{17,25},{25,17},{2,10},{10... | collective-permute-start | bytes 393224 | tf_op jit(solution)/shard_map/ppermute | solution.py:279
  11.0 9.4 %collective-permute-start.10 = (bf16[256,256]{1,0:T(8,128)(2,1)S(1)}, bf16[256,256]{1,0:T(8,128)(2,1)S(1)}, u32[]{:S(2)}, u32[]{:S(2)}) collective-permute-start(bf16[256,256]{1,0:T(8,128)(2,1)S(1)} %shard_map.123.refs_0_), channel_id=1, source_target_pairs={{0,24},{8,16},{16,8},{24,0},{1,25},{9,17},{17,9},{25,1},{2,26},{10... | collective-permute-start | bytes 393224 | tf_op jit(solution)/shard_map/ppermute | solution.py:279
  14.4 8.3 %collective-permute-start.9 = (bf16[256,256]{1,0:T(8,128)(2,1)S(1)}, bf16[256,256]{1,0:T(8,128)(2,1)S(1)}, u32[]{:S(2)}, u32[]{:S(2)}) collective-permute-start(bf16[256,256]{1,0:T(8,128)(2,1)S(1)} %shard_map.123.refs_0_), channel_id=1, source_target_pairs={{0,16},{8,24},{16,0},{24,8},{1,17},{9,25},{17,1},{25,9},{2,18},{10... | collective-permute-start | bytes 393224 | tf_op jit(solution)/shard_map/ppermute | solution.py:279
  20.4 27.9 %collective-permute-start.17 = (bf16[1024,256]{1,0:T(8,128)(2,1)S(1)}, bf16[1024,256]{1,0:T(8,128)(2,1)S(1)}, u32[]{:S(2)}, u32[]{:S(2)}) collective-permute-start(bf16[1024,256]{1,0:T(8,128)(2,1)S(1)} %get-tuple-element.51.refs_4_), channel_id=1, source_target_pairs={{0,1},{1,0},{2,3},{3,2},{4,5},{5,4},{6,7},{7,6},{8,9},{9,8},{10,11... | collective-permute-start | bytes 1572872 | tf_op jit(solution)/shard_map/ppermute | solution.py:279
  24.3 23.9 %collective-permute-start.18 = (bf16[1024,256]{1,0:T(8,128)(2,1)S(1)}, bf16[1024,256]{1,0:T(8,128)(2,1)S(1)}, u32[]{:S(2)}, u32[]{:S(2)}) collective-permute-start(bf16[1024,256]{1,0:T(8,128)(2,1)S(1)} %get-tuple-element.52.refs_6_.refs_4_), channel_id=1, source_target_pairs={{0,1},{1,0},{2,3},{3,2},{4,5},{5,4},{6,7},{7,6},{8,9},{9,8},{10,11... | collective-permute-start | bytes 1572872 | tf_op jit(solution)/shard_map/ppermute | solution.py:279
  24.4 9.2 %collective-permute-start.5 = (bf16[512,256]{1,0:T(8,128)(2,1)S(1)}, bf16[512,256]{1,0:T(8,128)(2,1)S(1)}, u32[]{:S(2)}, u32[]{:S(2)}) collective-permute-start(bf16[512,256]{1,0:T(8,128)(2,1)S(1)} %get-tuple-element.35), channel_id=1, source_target_pairs={{0,2},{1,3},{2,0},{3,1},{4,6},{5,7},{6,4},{7,5},{8,10},{9,11},{10,... | collective-permute-start | bytes 786440 | tf_op jit(solution)/shard_map/ppermute | solution.py:279
  26.0 16.5 %collective-permute-start.11 = (bf16[512,256]{1,0:T(8,128)(2,1)S(1)}, bf16[512,256]{1,0:T(8,128)(2,1)S(1)}, u32[]{:S(2)}, u32[]{:S(2)}) collective-permute-start(bf16[512,256]{1,0:T(8,128)(2,1)S(1)} %get-tuple-element.40), channel_id=1, source_target_pairs={{0,2},{1,3},{2,0},{3,1},{4,6},{5,7},{6,4},{7,5},{8,10},{9,11},{10,... | collective-permute-start | bytes 786440 | tf_op jit(solution)/shard_map/ppermute | solution.py:279
  33.7 7.0 %collective-permute-start.6 = (bf16[256,256]{1,0:T(8,128)(2,1)S(1)}, bf16[256,256]{1,0:T(8,128)(2,1)S(1)}, u32[]{:S(2)}, u32[]{:S(2)}) collective-permute-start(bf16[256,256]{1,0:T(8,128)(2,1)S(1)} %get-tuple-element.37), channel_id=1, source_target_pairs={{0,4},{1,5},{2,6},{3,7},{4,0},{5,1},{6,2},{7,3},{8,12},{9,13},{10,... | collective-permute-start | bytes 393224 | tf_op jit(solution)/shard_map/ppermute | solution.py:279
  42.2 6.1 %collective-permute-start.15 = (bf16[64,256]{1,0:T(8,128)(2,1)S(1)}, bf16[64,256]{1,0:T(8,128)(2,1)S(1)}, u32[]{:S(2)}, u32[]{:S(2)}) collective-permute-start(bf16[64,256]{1,0:T(8,128)(2,1)S(1)} %get-tuple-element.49), channel_id=1, source_target_pairs={{0,16},{8,24},{16,0},{24,8},{1,17},{9,25},{17,1},{25,9},{2,18},{10... | collective-permute-start | bytes 98312 | tf_op jit(solution)/shard_map/ppermute | solution.py:279
  42.5 5.8 %collective-permute-start.16 = (bf16[64,256]{1,0:T(8,128)(2,1)S(1)}, bf16[64,256]{1,0:T(8,128)(2,1)S(1)}, u32[]{:S(2)}, u32[]{:S(2)}) collective-permute-start(bf16[64,256]{1,0:T(8,128)(2,1)S(1)} %get-tuple-element.50), channel_id=1, source_target_pairs={{0,24},{8,16},{16,8},{24,0},{1,25},{9,17},{17,9},{25,1},{2,26},{10... | collective-permute-start | bytes 98312 | tf_op jit(solution)/shard_map/ppermute | solution.py:279
  44.8 8.0 %collective-permute-start.12 = (bf16[256,256]{1,0:T(8,128)(2,1)S(1)}, bf16[256,256]{1,0:T(8,128)(2,1)S(1)}, u32[]{:S(2)}, u32[]{:S(2)}) collective-permute-start(bf16[256,256]{1,0:T(8,128)(2,1)S(1)} %get-tuple-element.42), channel_id=1, source_target_pairs={{0,4},{1,5},{2,6},{3,7},{4,0},{5,1},{6,2},{7,3},{8,12},{9,13},{10,... | collective-permute-start | bytes 393224 | tf_op jit(solution)/shard_map/ppermute | solution.py:279
  48.8 13.7 %collective-permute-start.19 = (bf16[64,1024]{1,0:T(8,128)(2,1)S(1)}, bf16[64,1024]{1,0:T(8,128)(2,1)S(1)}, u32[]{:S(2)}, u32[]{:S(2)}) collective-permute-start(bf16[64,1024]{1,0:T(8,128)(2,1)S(1)} %shard_map.128), channel_id=1, source_target_pairs={{0,2},{1,3},{2,0},{3,1},{4,6},{5,7},{6,4},{7,5},{8,10},{9,11},{10,... | collective-permute-start | bytes 393224 | tf_op jit(solution)/shard_map/ppermute | solution.py:279
  56.5 18.5 %collective-permute-start.13 = (f32[128,512]{1,0:T(8,128)S(1)}, f32[128,512]{1,0:T(8,128)S(1)}, u32[]{:S(2)}, u32[]{:S(2)}) collective-permute-start(f32[128,512]{1,0:T(8,128)S(1)} %get-tuple-element.45), channel_id=1, source_target_pairs={{0,1},{1,0},{2,3},{3,2},{4,5},{5,4},{6,7},{7,6},{8,9},{9,8},{10,11... | collective-permute-start | bytes 786440 | tf_op jit(solution)/shard_map/ppermute | solution.py:279
  59.8 6.2 %collective-permute-start.31 = (bf16[64,512]{1,0:T(8,128)(2,1)S(1)}, bf16[64,512]{1,0:T(8,128)(2,1)S(1)}, u32[]{:S(2)}, u32[]{:S(2)}) collective-permute-start(bf16[64,512]{1,0:T(8,128)(2,1)S(1)} %shard_map.131), channel_id=1, source_target_pairs={{0,2},{1,3},{2,0},{3,1},{4,6},{5,7},{6,4},{7,5},{8,10},{9,11},{10,... | collective-permute-start | bytes 196616 | tf_op jit(solution)/shard_map/ppermute | solution.py:279
  62.6 7.2 %collective-permute-start.20 = (bf16[64,1024]{1,0:T(8,128)(2,1)S(1)}, bf16[64,1024]{1,0:T(8,128)(2,1)S(1)}, u32[]{:S(2)}, u32[]{:S(2)}) collective-permute-start(bf16[64,1024]{1,0:T(8,128)(2,1)S(1)} %add_convert_fusion.1), channel_id=1, source_target_pairs={{0,4},{1,5},{2,6},{3,7},{4,0},{5,1},{6,2},{7,3},{8,12},{9,13},{10,... | collective-permute-start | bytes 393224 | tf_op jit(solution)/shard_map/ppermute | solution.py:279
  66.1 7.3 %collective-permute-start.32 = (bf16[64,512]{1,0:T(8,128)(2,1)S(1)}, bf16[64,512]{1,0:T(8,128)(2,1)S(1)}, u32[]{:S(2)}, u32[]{:S(2)}) collective-permute-start(bf16[64,512]{1,0:T(8,128)(2,1)S(1)} %add_convert_fusion.3), channel_id=1, source_target_pairs={{0,4},{1,5},{2,6},{3,7},{4,0},{5,1},{6,2},{7,3},{8,12},{9,13},{10,... | collective-permute-start | bytes 196616 | tf_op jit(solution)/shard_map/ppermute | solution.py:279
  69.8 8.8 %collective-permute-start.23 = (bf16[64,1024]{1,0:T(8,128)(2,1)S(1)}, bf16[64,1024]{1,0:T(8,128)(2,1)S(1)}, u32[]{:S(2)}, u32[]{:S(2)}) collective-permute-start(bf16[64,1024]{1,0:T(8,128)(2,1)S(1)} %add_convert_fusion.refs_0_), channel_id=1, source_target_pairs={{0,24},{8,16},{16,8},{24,0},{1,25},{9,17},{17,9},{25,1},{2,26},{10... | collective-permute-start | bytes 393224 | tf_op jit(solution)/shard_map/ppermute | solution.py:279
  71.4 7.7 %collective-permute-start.22 = (bf16[64,1024]{1,0:T(8,128)(2,1)S(1)}, bf16[64,1024]{1,0:T(8,128)(2,1)S(1)}, u32[]{:S(2)}, u32[]{:S(2)}) collective-permute-start(bf16[64,1024]{1,0:T(8,128)(2,1)S(1)} %add_convert_fusion.refs_0_), channel_id=1, source_target_pairs={{0,16},{8,24},{16,0},{24,8},{1,17},{9,25},{17,1},{25,9},{2,18},{10... | collective-permute-start | bytes 393224 | tf_op jit(solution)/shard_map/ppermute | solution.py:279
  72.8 6.4 %collective-permute-start.21 = (bf16[64,1024]{1,0:T(8,128)(2,1)S(1)}, bf16[64,1024]{1,0:T(8,128)(2,1)S(1)}, u32[]{:S(2)}, u32[]{:S(2)}) collective-permute-start(bf16[64,1024]{1,0:T(8,128)(2,1)S(1)} %add_convert_fusion.refs_0_), channel_id=1, source_target_pairs={{0,8},{8,0},{16,24},{24,16},{1,9},{9,1},{17,25},{25,17},{2,10},{10... | collective-permute-start | bytes 393224 | tf_op jit(solution)/shard_map/ppermute | solution.py:279
  78.6 5.8 %collective-permute-start.27 = (bf16[64,1024]{1,0:T(8,128)(2,1)S(1)}, bf16[64,1024]{1,0:T(8,128)(2,1)S(1)}, u32[]{:S(2)}, u32[]{:S(2)}) collective-permute-start(bf16[64,1024]{1,0:T(8,128)(2,1)S(1)} %collective-permute-done.23.refs_3_), channel_id=1, source_target_pairs={{0,1},{1,0},{2,3},{3,2},{4,5},{5,4},{6,7},{7,6},{8,9},{9,8},{10,11... | collective-permute-start | bytes 393224 | tf_op jit(solution)/shard_map/ppermute | solution.py:279
  (22 other events, 112.2 us)

commit v2 on v1

--- a/solution.py
+++ b/solution.py
@@ -70,6 +70,41 @@
     return call(pick_body, [sds((2 * rows, width // 2), BF)], [], [own, got], 0)[0]
 
 
+def split_body(own, near, far):
+    _, _, c = place()
+    half = near.shape[1]
+    near[...] = own[:, block(c, half)]
+    far[...] = own[:, block(1 - c, half)]
+
+
+def split(own):
+    shape = (own.shape[0], own.shape[1] // 2)
+    return call(split_body, [sds(shape, BF)] * 2, [], [own], 0)
+
+
+def kept_rows(flags, values):
+    rows = values.shape[0]
+    mask = jnp.broadcast_to(flags.astype(F32), (rows, rows)).T > 0
+    mask = jnp.concatenate([mask.astype(F32)] * (values.shape[1] // rows), axis=1)
+    return jnp.where(mask > 0, values, jnp.zeros_like(values))
+
+
+def keep_body(flags, values, out):
+    out[...] = kept_rows(flags[...], values[...].astype(F32)).astype(BF)
+
+
+def keep(flags, values):
+    return call(keep_body, [sds(values.shape, BF)], [], [flags, values], values.size)[0]
+
+
+def add_body(one, two, out):
+    out[...] = (one[...].astype(F32) + two[...].astype(F32)).astype(out.dtype)
+
+
+def add(one, two):
+    return call(add_body, [sds(one.shape, BF)], [], [one, two], one.size)[0]
+
+
 def start_body(one, top, start, top_t):
     start[...] = dot(one[...], top[...])
     top_t[...] = top[...].T
@@ -88,13 +123,14 @@
 
 
 def product_body(n, nz, mine, theirs, *refs):
-    q, (stay, leave, rhs) = refs[:n], refs[n:]
+    near, far, (stay, leave, rhs) = refs[:n], refs[n:-3], refs[-3:]
     p, z, c = place()
-    rows = q[0].shape[0] // 2
     depth = rhs.shape[0] // 2
-    for s in range(n):
-        rhs[block(p ^ s, rows), :] = q[s][:rows, :]
-        rhs[pl.ds(pl.multiple_of(depth + (p ^ s) * rows, rows), rows), :] = q[s][rows:, :]
+    rows = depth // n
+    for s in range(n):
+        other = far[s][...] if far else near[s][rows:, :]
+        rhs[block(p ^ s, rows), :] = near[s][:rows, :]
+        rhs[pl.ds(pl.multiple_of(depth + (p ^ s) * rows, rows), rows), :] = other
     order = sequence(nz)
     for k in range(nz // 2, nz):
         emit(leave, k - nz // 2, order[k], z, c, rows, mine, theirs, rhs)
@@ -110,14 +146,15 @@
         out[block(2 * k + (c ^ t), rows), :] = value[t * rows : (t + 1) * rows].astype(out.dtype)
 
 
-def product(mine, theirs, q, nz):
-    n, (rows, half) = len(q), q[0].shape
+def product(mine, theirs, near, far, nz):
+    n, half = len(near), near[0].shape[1]
     depth = mine.shape[1]
+    rows = 2 * depth // n
     shape = (nz // 2 * rows, half)
     out = [sds(shape, F32), sds(shape, BF), sds((2 * depth, half), BF)]
     return call(
         functools.partial(product_body, n, nz), out, [],
-        [mine, theirs, *q], 4 * mine.shape[0] * depth * half,
+        [mine, theirs, *near, *far], 4 * mine.shape[0] * depth * half,
     )
 
 
@@ -256,7 +293,7 @@
     value[:, block(c, half)] = keep_two[...]
     value[:, block(1 - c, half)] = got[:, half:]
     lower = -(value[...] + dot(inverse_one[...], top[...]))
-    inverse_two[...] = jnp.where(flags[...] > 0, lower, jnp.zeros_like(lower)).astype(BF)
+    inverse_two[...] = kept_rows(flags[...], lower).astype(BF)
 
 
 def finish(keep_one, keep_two, got, top, flags):
@@ -281,13 +318,18 @@
     over_z = lambda x, s: send(x, "pcol", m, 2 * s)
     over_p = lambda x, s: send(x, "prow", n, s)
 
-    flags = structure.reshape(piece_rows, 1)
-    masked_two = jnp.where(flags > 0, panel_two, jnp.zeros_like(panel_two))
-    mine_one = pick(panel_one, swap(panel_one))
+    across = lambda x, s: lax.ppermute(
+        x, ("prow", "pcol"),
+        [(k * m + j, (k ^ s) * m + (j ^ 1)) for k in range(n) for j in range(m)],
+    )
+
+    flags = structure.reshape(1, piece_rows)
+    own_one, other_one = split(panel_one)
+    near_one = [own_one] + [over_p(own_one, s) for s in range(1, n)]
+    far_one = [across(other_one, s) for s in range(n)]
+    masked_two = keep(flags, panel_two)
     mine_two = pick(masked_two, swap(masked_two))
-    gather = lambda x: [x] + [over_p(x, s) for s in range(1, n)]
-    gathered_one = gather(mine_one)
-    gathered_two = gather(mine_two)
+    near_two = [mine_two] + [over_p(mine_two, s) for s in range(1, n)]
 
     shaped = known_inverse.reshape(block_rows, BLK, col_groups, piece_blocks, BLK)
     flag_table = pattern.reshape(block_rows, 1, col_groups, piece_blocks, 1)
@@ -310,14 +352,14 @@
     def total(here):
         s = 1
         while s < nz:
-            here = (here.astype(F32) + over_z(here, s).astype(F32)).astype(BF)
+            here = add(here, over_z(here, s))
             s *= 2
         got = [here] + [over_p(here, s) for s in range(1, n)]
         return got, [swap(got[s]) for s in range(n)]
 
-    *parts_one, rows_one = product(masked, others, gathered_one, nz)
+    *parts_one, rows_one = product(masked, others, near_one, far_one, nz)
     parts_one = exchange(*parts_one)
-    *parts_two, rows_two = product(masked, others, gathered_two, nz)
+    *parts_two, rows_two = product(masked, others, near_two, [], nz)
     parts_two = exchange(*parts_two)
     panels = [rows_one, swap(rows_one), rows_two, swap(rows_two)]
     keep_one, give_one, *pieces_one = first_turn(parts_one, n)

time: 87.8 us -> 90.6 us (1.032)
  waiting for transfers between devices: 31.2 us -> 33.5 us
    ppermute x0 -> x4, starting transfers between devices: none -> 2.92 us  [on_device(): lax.ppermute(x, ('prow', 'pcol'), [(k * m + j, (k ^ s) * m + (j ^ 1)) for...]
    ppermute x40 -> x39, starting transfers between devices: 45.7 us -> 43.1 us  [on_device(): lax.ppermute(x, axis, [(k, k ^ s) for k in range(size)])]
    ppermute x0 -> x4, waiting for transfers between devices: none -> 1.26 us  [on_device(): lax.ppermute(x, ('prow', 'pcol'), [(k * m + j, (k ^ s) * m + (j ^ 1)) for...]
    ppermute x40 -> x39, waiting for transfers between devices: 31.2 us -> 32.2 us  [on_device(): lax.ppermute(x, axis, [(k, k ^ s) for k in range(size)])]
    pallas_call x14 -> x19, Pallas kernels: 6.76 us -> 6.95 us  [call(): pl.pallas_call(body, out_shape=out, in_specs=[VMEM] * len(args), out_spec...]
  transfers between devices with their start and end apart: 40 -> 43, of which waited for: 16 -> 17; matrix products, arithmetic and copies ran while one was open for 0% -> 0% of each run, Pallas kernels for 7% -> 7%
where the time goes in v2:
time: 90.6 us; the launch traced here: 90.4 us
  starting transfers between devices  46 us (51%)
  waiting for transfers between devices  33.5 us (37%)
  Pallas kernels  6.95 us (8%)
  other arithmetic  2.33 us (3%)
    ppermute x39, starting transfers between devices, on_device(): lax.ppermute(x, axis, [(k, k ^ s) for k in range(size)])  43.1 us
    ppermute x39, waiting for transfers between devices, on_device(): lax.ppermute(x, axis, [(k, k ^ s) for k in range(size)])  32.2 us
    pallas_call x19, Pallas kernels, call(): pl.pallas_call(body, out_shape=out, in_specs=[VMEM] * len(args), out_spec...  6.95 us
    ppermute x4, starting transfers between devices, on_device(): lax.ppermute(x, ('prow', 'pcol'), [(k * m + j, (k ^ s) * m + (j ^ 1)) for...  2.92 us
  transfers between devices with their start and end apart: 43, of which 17 were waited for; matrix products, arithmetic and copies ran while one was open for 0% of the time, Pallas kernels for 7%

profile of v2, /device:TPU:0, one launch (start us, length us, event | category | flops | bytes accessed | tf_op | source)
XLA Modules:
  0.0 90.4 jit_solution(11842796081258159988)
XLA Ops:
  1.8 1.6 %bitcast_select_fusion.mine = bf16[1024,512]{1,0:T(8,128)(2,1)S(1)} fusion(pred[128,8,4,128]{3,2,1,0:T(4,128)(4,1)S(1)} %bitcast.14, bf16[128,8,4,128]{3,2,1,0:T(4,128)(2,1)} %bitcast.15), kind=kLoop, calls=%fused_computation | loop fusion | flops 524288 | bytes 2621440 | tf_op jit(solution)/shard_map/jit(_where)/select_n | solution.py:336
  5.0 4.0 %collective-permute-start.3 = (bf16[128,256]{1,0:T(8,128)(2,1)S(1)}, bf16[128,256]{1,0:T(8,128)(2,1)S(1)}, u32[]{:S(2)}, u32[]{:S(2)}) collective-permute-start(bf16[128,256]{1,0:T(8,128)(2,1)S(1)} %get-tuple-element.36.refs_0_), channel_id=1, source_target_pairs={{0,24},{8,16},{16,8},{24,0},{1,25},{9,17},{17,9},{25,1},{2,26},{10... | collective-permute-start | bytes 196616 | tf_op jit(solution)/shard_map/ppermute | solution.py:316
  9.6 1.6 %collective-permute-done.3.refs_3_ = bf16[128,256]{1,0:T(8,128)(2,1)S(1)} collective-permute-done((bf16[128,256]{1,0:T(8,128)(2,1)S(1)}, bf16[128,256]{1,0:T(8,128)(2,1)S(1)}, u32[]{:S(2)}, u32[]{:S(2)}) %collective-permute-start.3) | collective-permute-done | bytes 65568 | tf_op jit(solution)/shard_map/ppermute | solution.py:316
  14.8 1.7 %collective-permute-start.13 = (bf16[256,256]{1,0:T(8,128)(2,1)S(1)}, bf16[256,256]{1,0:T(8,128)(2,1)S(1)}, u32[]{:S(2)}, u32[]{:S(2)}) collective-permute-start(bf16[256,256]{1,0:T(8,128)(2,1)S(1)} %shard_map.124.refs_0_), channel_id=1, source_target_pairs={{0,24},{8,16},{16,8},{24,0},{1,25},{9,17},{17,9},{25,1},{2,26},{10... | collective-permute-start | bytes 393224 | tf_op jit(solution)/shard_map/ppermute | solution.py:316
  16.6 1.6 %collective-permute-start.12 = (bf16[256,256]{1,0:T(8,128)(2,1)S(1)}, bf16[256,256]{1,0:T(8,128)(2,1)S(1)}, u32[]{:S(2)}, u32[]{:S(2)}) collective-permute-start(bf16[256,256]{1,0:T(8,128)(2,1)S(1)} %shard_map.124.refs_0_), channel_id=1, source_target_pairs={{0,16},{8,24},{16,0},{24,8},{1,17},{9,25},{17,1},{25,9},{2,18},{10... | collective-permute-start | bytes 393224 | tf_op jit(solution)/shard_map/ppermute | solution.py:316
  18.2 1.6 %collective-permute-start.11 = (bf16[256,256]{1,0:T(8,128)(2,1)S(1)}, bf16[256,256]{1,0:T(8,128)(2,1)S(1)}, u32[]{:S(2)}, u32[]{:S(2)}) collective-permute-start(bf16[256,256]{1,0:T(8,128)(2,1)S(1)} %shard_map.124.refs_0_), channel_id=1, source_target_pairs={{0,8},{8,0},{16,24},{24,16},{1,9},{9,1},{17,25},{25,17},{2,10},{10... | collective-permute-start | bytes 393224 | tf_op jit(solution)/shard_map/ppermute | solution.py:316
  22.3 2.7 %collective-permute-done.12.refs_2_ = bf16[256,256]{1,0:T(8,128)(2,1)S(1)} collective-permute-done((bf16[256,256]{1,0:T(8,128)(2,1)S(1)}, bf16[256,256]{1,0:T(8,128)(2,1)S(1)}, u32[]{:S(2)}, u32[]{:S(2)}) %collective-permute-start.12) | collective-permute-done | bytes 131104 | tf_op jit(solution)/shard_map/ppermute | solution.py:316
  26.0 1.6 %collective-permute-start.8 = (bf16[512,256]{1,0:T(8,128)(2,1)S(1)}, bf16[512,256]{1,0:T(8,128)(2,1)S(1)}, u32[]{:S(2)}, u32[]{:S(2)}) collective-permute-start(bf16[512,256]{1,0:T(8,128)(2,1)S(1)} %get-tuple-element.39), channel_id=1, source_target_pairs={{0,2},{1,3},{2,0},{3,1},{4,6},{5,7},{6,4},{7,5},{8,10},{9,11},{10,... | collective-permute-start | bytes 786440 | tf_op jit(solution)/shard_map/ppermute | solution.py:316
  28.0 7.1 %collective-permute-done.8.got = bf16[512,256]{1,0:T(8,128)(2,1)S(1)} collective-permute-done((bf16[512,256]{1,0:T(8,128)(2,1)S(1)}, bf16[512,256]{1,0:T(8,128)(2,1)S(1)}, u32[]{:S(2)}, u32[]{:S(2)}) %collective-permute-start.8) | collective-permute-done | bytes 262176 | tf_op jit(solution)/shard_map/ppermute | solution.py:316
  35.2 2.7 %collective-permute-start.9 = (bf16[256,256]{1,0:T(8,128)(2,1)S(1)}, bf16[256,256]{1,0:T(8,128)(2,1)S(1)}, u32[]{:S(2)}, u32[]{:S(2)}) collective-permute-start(bf16[256,256]{1,0:T(8,128)(2,1)S(1)} %get-tuple-element.41), channel_id=1, source_target_pairs={{0,4},{1,5},{2,6},{3,7},{4,0},{5,1},{6,2},{7,3},{8,12},{9,13},{10,... | collective-permute-start | bytes 393224 | tf_op jit(solution)/shard_map/ppermute | solution.py:316
  37.9 4.3 %collective-permute-done.9.refs_1_ = bf16[256,256]{1,0:T(8,128)(2,1)S(1)} collective-permute-done((bf16[256,256]{1,0:T(8,128)(2,1)S(1)}, bf16[256,256]{1,0:T(8,128)(2,1)S(1)}, u32[]{:S(2)}, u32[]{:S(2)}) %collective-permute-start.9) | collective-permute-done | bytes 131104 | tf_op jit(solution)/shard_map/ppermute | solution.py:316
  44.2 1.7 %collective-permute-start.19 = (bf16[64,256]{1,0:T(8,128)(2,1)S(1)}, bf16[64,256]{1,0:T(8,128)(2,1)S(1)}, u32[]{:S(2)}, u32[]{:S(2)}) collective-permute-start(bf16[64,256]{1,0:T(8,128)(2,1)S(1)} %get-tuple-element.54), channel_id=1, source_target_pairs={{0,24},{8,16},{16,8},{24,0},{1,25},{9,17},{17,9},{25,1},{2,26},{10... | collective-permute-start | bytes 98312 | tf_op jit(solution)/shard_map/ppermute | solution.py:316
  46.3 3.4 %collective-permute-start.15 = (bf16[256,256]{1,0:T(8,128)(2,1)S(1)}, bf16[256,256]{1,0:T(8,128)(2,1)S(1)}, u32[]{:S(2)}, u32[]{:S(2)}) collective-permute-start(bf16[256,256]{1,0:T(8,128)(2,1)S(1)} %get-tuple-element.46), channel_id=1, source_target_pairs={{0,4},{1,5},{2,6},{3,7},{4,0},{5,1},{6,2},{7,3},{8,12},{9,13},{10,... | collective-permute-start | bytes 393224 | tf_op jit(solution)/shard_map/ppermute | solution.py:316
  50.2 2.8 %collective-permute-start.22 = (bf16[64,1024]{1,0:T(8,128)(2,1)S(1)}, bf16[64,1024]{1,0:T(8,128)(2,1)S(1)}, u32[]{:S(2)}, u32[]{:S(2)}) collective-permute-start(bf16[64,1024]{1,0:T(8,128)(2,1)S(1)} %shard_map.129.one), channel_id=1, source_target_pairs={{0,2},{1,3},{2,0},{3,1},{4,6},{5,7},{6,4},{7,5},{8,10},{9,11},{10,... | collective-permute-start | bytes 393224 | tf_op jit(solution)/shard_map/ppermute | solution.py:316
  54.4 1.6 %collective-permute-done.22.two = bf16[64,1024]{1,0:T(8,128)(2,1)S(1)} collective-permute-done((bf16[64,1024]{1,0:T(8,128)(2,1)S(1)}, bf16[64,1024]{1,0:T(8,128)(2,1)S(1)}, u32[]{:S(2)}, u32[]{:S(2)}) %collective-permute-start.22) | collective-permute-done | bytes 131104 | tf_op jit(solution)/shard_map/ppermute | solution.py:316
  56.0 2.4 %collective-permute-start.23 = (bf16[64,1024]{1,0:T(8,128)(2,1)S(1)}, bf16[64,1024]{1,0:T(8,128)(2,1)S(1)}, u32[]{:S(2)}, u32[]{:S(2)}) collective-permute-start(bf16[64,1024]{1,0:T(8,128)(2,1)S(1)} %shard_map.130.one), channel_id=1, source_target_pairs={{0,4},{1,5},{2,6},{3,7},{4,0},{5,1},{6,2},{7,3},{8,12},{9,13},{10,... | collective-permute-start | bytes 393224 | tf_op jit(solution)/shard_map/ppermute | solution.py:316
  63.6 1.8 %collective-permute-done.33.refs_3_ = bf16[64,256]{1,0:T(8,128)(2,1)S(1)} collective-permute-done((bf16[64,256]{1,0:T(8,128)(2,1)S(1)}, bf16[64,256]{1,0:T(8,128)(2,1)S(1)}, u32[]{:S(2)}, u32[]{:S(2)}) %collective-permute-start.33) | collective-permute-done | bytes 32800 | tf_op jit(solution)/shard_map/ppermute | solution.py:316
  65.8 2.1 %collective-permute-start.34 = (bf16[64,512]{1,0:T(8,128)(2,1)S(1)}, bf16[64,512]{1,0:T(8,128)(2,1)S(1)}, u32[]{:S(2)}, u32[]{:S(2)}) collective-permute-start(bf16[64,512]{1,0:T(8,128)(2,1)S(1)} %shard_map.134.one), channel_id=1, source_target_pairs={{0,2},{1,3},{2,0},{3,1},{4,6},{5,7},{6,4},{7,5},{8,10},{9,11},{10,... | collective-permute-start | bytes 196616 | tf_op jit(solution)/shard_map/ppermute | solution.py:316
  67.9 2.9 %collective-permute-done.34.two = bf16[64,512]{1,0:T(8,128)(2,1)S(1)} collective-permute-done((bf16[64,512]{1,0:T(8,128)(2,1)S(1)}, bf16[64,512]{1,0:T(8,128)(2,1)S(1)}, u32[]{:S(2)}, u32[]{:S(2)}) %collective-permute-start.34) | collective-permute-done | bytes 65568 | tf_op jit(solution)/shard_map/ppermute | solution.py:316
  74.5 1.5 %collective-permute-done.35.two = bf16[64,512]{1,0:T(8,128)(2,1)S(1)} collective-permute-done((bf16[64,512]{1,0:T(8,128)(2,1)S(1)}, bf16[64,512]{1,0:T(8,128)(2,1)S(1)}, u32[]{:S(2)}, u32[]{:S(2)}) %collective-permute-start.35) | collective-permute-done | bytes 65568 | tf_op jit(solution)/shard_map/ppermute | solution.py:316
  76.7 2.1 %collective-permute-start.37 = (bf16[64,512]{1,0:T(8,128)(2,1)S(1)}, bf16[64,512]{1,0:T(8,128)(2,1)S(1)}, u32[]{:S(2)}, u32[]{:S(2)}) collective-permute-start(bf16[64,512]{1,0:T(8,128)(2,1)S(1)} %shard_map.136.refs_0_), channel_id=1, source_target_pairs={{0,16},{8,24},{16,0},{24,8},{1,17},{9,25},{17,1},{25,9},{2,18},{10... | collective-permute-start | bytes 196616 | tf_op jit(solution)/shard_map/ppermute | solution.py:316
  78.8 2.6 %collective-permute-done.38.refs_3_ = bf16[64,512]{1,0:T(8,128)(2,1)S(1)} collective-permute-done((bf16[64,512]{1,0:T(8,128)(2,1)S(1)}, bf16[64,512]{1,0:T(8,128)(2,1)S(1)}, u32[]{:S(2)}, u32[]{:S(2)}) %collective-permute-start.38) | collective-permute-done | bytes 65568 | tf_op jit(solution)/shard_map/ppermute | solution.py:316
  85.0 1.7 %collective-permute-done.36.refs_1_ = bf16[64,512]{1,0:T(8,128)(2,1)S(1)} collective-permute-done((bf16[64,512]{1,0:T(8,128)(2,1)S(1)}, bf16[64,512]{1,0:T(8,128)(2,1)S(1)}, u32[]{:S(2)}, u32[]{:S(2)}) %collective-permute-start.36) | collective-permute-done | bytes 65568 | tf_op jit(solution)/shard_map/ppermute | solution.py:316
  87.8 1.6 %shard_map.133 = (bf16[512,512]{1,0:T(8,128)(2,1)}, bf16[512,512]{1,0:T(8,128)(2,1)}, f32[512,512]{1,0:T(8,128)S(1)}) custom-call(bf16[64,1024]{1,0:T(8,128)(2,1)S(1)} %shard_map.131.refs_0_, bf16[64,1024]{1,0:T(8,128)(2,1)S(1)} %collective-permute-done.24.refs_1_, bf16[64,1024]{1,0:T(8,128)(2,1)S(1)} %collective-permute-done.25.refs_2_, ...), custom_call_target="tpu_custom_call" | custom-call | flops 805306368 | bytes 6291456 | tf_op jit(solution)/shard_map/pallas_call | solution.py:31
  (97 shorter events, 30.8 us)
Async XLA Ops:
  3.4 17.6 %collective-permute-start = (bf16[1024,512]{1,0:T(8,128)(2,1)S(1)}, bf16[1024,512]{1,0:T(8,128)(2,1)S(1)}, u32[]{:S(2)}, u32[]{:S(2)}) collective-permute-start(bf16[1024,512]{1,0:T(8,128)(2,1)S(1)} %bitcast_select_fusion.mine), channel_id=1, source_target_pairs={{0,1},{1,0},{2,3},{3,2},{4,5},{5,4},{6,7},{7,6},{8,9},{9,8},{10,11... | collective-permute-start | bytes 3145736 | tf_op jit(solution)/shard_map/ppermute | solution.py:316
  4.2 10.4 %collective-permute-start.10 = (bf16[128,512]{1,0:T(8,128)(2,1)S(1)}, bf16[128,512]{1,0:T(8,128)(2,1)S(1)}, u32[]{:S(2)}, u32[]{:S(2)}) collective-permute-start(bf16[128,512]{1,0:T(8,128)(2,1)S(1)} %shard_map.123.own), channel_id=1, source_target_pairs={{0,1},{1,0},{2,3},{3,2},{4,5},{5,4},{6,7},{7,6},{8,9},{9,8},{10,11... | collective-permute-start | bytes 393224 | tf_op jit(solution)/shard_map/ppermute | solution.py:316
  5.0 6.2 %collective-permute-start.3 = (bf16[128,256]{1,0:T(8,128)(2,1)S(1)}, bf16[128,256]{1,0:T(8,128)(2,1)S(1)}, u32[]{:S(2)}, u32[]{:S(2)}) collective-permute-start(bf16[128,256]{1,0:T(8,128)(2,1)S(1)} %get-tuple-element.36.refs_0_), channel_id=1, source_target_pairs={{0,24},{8,16},{16,8},{24,0},{1,25},{9,17},{17,9},{25,1},{2,26},{10... | collective-permute-start | bytes 196616 | tf_op jit(solution)/shard_map/ppermute | solution.py:316
  14.8 7.4 %collective-permute-start.13 = (bf16[256,256]{1,0:T(8,128)(2,1)S(1)}, bf16[256,256]{1,0:T(8,128)(2,1)S(1)}, u32[]{:S(2)}, u32[]{:S(2)}) collective-permute-start(bf16[256,256]{1,0:T(8,128)(2,1)S(1)} %shard_map.124.refs_0_), channel_id=1, source_target_pairs={{0,24},{8,16},{16,8},{24,0},{1,25},{9,17},{17,9},{25,1},{2,26},{10... | collective-permute-start | bytes 393224 | tf_op jit(solution)/shard_map/ppermute | solution.py:316
  16.6 8.5 %collective-permute-start.12 = (bf16[256,256]{1,0:T(8,128)(2,1)S(1)}, bf16[256,256]{1,0:T(8,128)(2,1)S(1)}, u32[]{:S(2)}, u32[]{:S(2)}) collective-permute-start(bf16[256,256]{1,0:T(8,128)(2,1)S(1)} %shard_map.124.refs_0_), channel_id=1, source_target_pairs={{0,16},{8,24},{16,0},{24,8},{1,17},{9,25},{17,1},{25,9},{2,18},{10... | collective-permute-start | bytes 393224 | tf_op jit(solution)/shard_map/ppermute | solution.py:316
  18.2 6.8 %collective-permute-start.11 = (bf16[256,256]{1,0:T(8,128)(2,1)S(1)}, bf16[256,256]{1,0:T(8,128)(2,1)S(1)}, u32[]{:S(2)}, u32[]{:S(2)}) collective-permute-start(bf16[256,256]{1,0:T(8,128)(2,1)S(1)} %shard_map.124.refs_0_), channel_id=1, source_target_pairs={{0,8},{8,0},{16,24},{24,16},{1,9},{9,1},{17,25},{25,17},{2,10},{10... | collective-permute-start | bytes 393224 | tf_op jit(solution)/shard_map/ppermute | solution.py:316
  21.8 27.9 %collective-permute-start.20 = (bf16[1024,256]{1,0:T(8,128)(2,1)S(1)}, bf16[1024,256]{1,0:T(8,128)(2,1)S(1)}, u32[]{:S(2)}, u32[]{:S(2)}) collective-permute-start(bf16[1024,256]{1,0:T(8,128)(2,1)S(1)} %get-tuple-element.55.refs_4_), channel_id=1, source_target_pairs={{0,1},{1,0},{2,3},{3,2},{4,5},{5,4},{6,7},{7,6},{8,9},{9,8},{10,11... | collective-permute-start | bytes 1572872 | tf_op jit(solution)/shard_map/ppermute | solution.py:316
  25.8 24.0 %collective-permute-start.21 = (bf16[1024,256]{1,0:T(8,128)(2,1)S(1)}, bf16[1024,256]{1,0:T(8,128)(2,1)S(1)}, u32[]{:S(2)}, u32[]{:S(2)}) collective-permute-start(bf16[1024,256]{1,0:T(8,128)(2,1)S(1)} %get-tuple-element.56.refs_6_.refs_4_), channel_id=1, source_target_pairs={{0,1},{1,0},{2,3},{3,2},{4,5},{5,4},{6,7},{7,6},{8,9},{9,8},{10,11... | collective-permute-start | bytes 1572872 | tf_op jit(solution)/shard_map/ppermute | solution.py:316
  26.0 9.2 %collective-permute-start.8 = (bf16[512,256]{1,0:T(8,128)(2,1)S(1)}, bf16[512,256]{1,0:T(8,128)(2,1)S(1)}, u32[]{:S(2)}, u32[]{:S(2)}) collective-permute-start(bf16[512,256]{1,0:T(8,128)(2,1)S(1)} %get-tuple-element.39), channel_id=1, source_target_pairs={{0,2},{1,3},{2,0},{3,1},{4,6},{5,7},{6,4},{7,5},{8,10},{9,11},{10,... | collective-permute-start | bytes 786440 | tf_op jit(solution)/shard_map/ppermute | solution.py:316
  27.6 16.6 %collective-permute-start.14 = (bf16[512,256]{1,0:T(8,128)(2,1)S(1)}, bf16[512,256]{1,0:T(8,128)(2,1)S(1)}, u32[]{:S(2)}, u32[]{:S(2)}) collective-permute-start(bf16[512,256]{1,0:T(8,128)(2,1)S(1)} %get-tuple-element.44), channel_id=1, source_target_pairs={{0,2},{1,3},{2,0},{3,1},{4,6},{5,7},{6,4},{7,5},{8,10},{9,11},{10,... | collective-permute-start | bytes 786440 | tf_op jit(solution)/shard_map/ppermute | solution.py:316
  35.2 7.0 %collective-permute-start.9 = (bf16[256,256]{1,0:T(8,128)(2,1)S(1)}, bf16[256,256]{1,0:T(8,128)(2,1)S(1)}, u32[]{:S(2)}, u32[]{:S(2)}) collective-permute-start(bf16[256,256]{1,0:T(8,128)(2,1)S(1)} %get-tuple-element.41), channel_id=1, source_target_pairs={{0,4},{1,5},{2,6},{3,7},{4,0},{5,1},{6,2},{7,3},{8,12},{9,13},{10,... | collective-permute-start | bytes 393224 | tf_op jit(solution)/shard_map/ppermute | solution.py:316
  43.5 6.2 %collective-permute-start.18 = (bf16[64,256]{1,0:T(8,128)(2,1)S(1)}, bf16[64,256]{1,0:T(8,128)(2,1)S(1)}, u32[]{:S(2)}, u32[]{:S(2)}) collective-permute-start(bf16[64,256]{1,0:T(8,128)(2,1)S(1)} %get-tuple-element.53), channel_id=1, source_target_pairs={{0,16},{8,24},{16,0},{24,8},{1,17},{9,25},{17,1},{25,9},{2,18},{10... | collective-permute-start | bytes 98312 | tf_op jit(solution)/shard_map/ppermute | solution.py:316
  44.2 5.6 %collective-permute-start.19 = (bf16[64,256]{1,0:T(8,128)(2,1)S(1)}, bf16[64,256]{1,0:T(8,128)(2,1)S(1)}, u32[]{:S(2)}, u32[]{:S(2)}) collective-permute-start(bf16[64,256]{1,0:T(8,128)(2,1)S(1)} %get-tuple-element.54), channel_id=1, source_target_pairs={{0,24},{8,16},{16,8},{24,0},{1,25},{9,17},{17,9},{25,1},{2,26},{10... | collective-permute-start | bytes 98312 | tf_op jit(solution)/shard_map/ppermute | solution.py:316
  46.3 7.9 %collective-permute-start.15 = (bf16[256,256]{1,0:T(8,128)(2,1)S(1)}, bf16[256,256]{1,0:T(8,128)(2,1)S(1)}, u32[]{:S(2)}, u32[]{:S(2)}) collective-permute-start(bf16[256,256]{1,0:T(8,128)(2,1)S(1)} %get-tuple-element.46), channel_id=1, source_target_pairs={{0,4},{1,5},{2,6},{3,7},{4,0},{5,1},{6,2},{7,3},{8,12},{9,13},{10,... | collective-permute-start | bytes 393224 | tf_op jit(solution)/shard_map/ppermute | solution.py:316
  50.2 5.8 %collective-permute-start.22 = (bf16[64,1024]{1,0:T(8,128)(2,1)S(1)}, bf16[64,1024]{1,0:T(8,128)(2,1)S(1)}, u32[]{:S(2)}, u32[]{:S(2)}) collective-permute-start(bf16[64,1024]{1,0:T(8,128)(2,1)S(1)} %shard_map.129.one), channel_id=1, source_target_pairs={{0,2},{1,3},{2,0},{3,1},{4,6},{5,7},{6,4},{7,5},{8,10},{9,11},{10,... | collective-permute-start | bytes 393224 | tf_op jit(solution)/shard_map/ppermute | solution.py:316
  54.4 22.3 %collective-permute-start.16 = (f32[128,512]{1,0:T(8,128)S(1)}, f32[128,512]{1,0:T(8,128)S(1)}, u32[]{:S(2)}, u32[]{:S(2)}) collective-permute-start(f32[128,512]{1,0:T(8,128)S(1)} %get-tuple-element.49), channel_id=1, source_target_pairs={{0,1},{1,0},{2,3},{3,2},{4,5},{5,4},{6,7},{7,6},{8,9},{9,8},{10,11... | collective-permute-start | bytes 786440 | tf_op jit(solution)/shard_map/ppermute | solution.py:316
  56.0 14.9 %collective-permute-start.23 = (bf16[64,1024]{1,0:T(8,128)(2,1)S(1)}, bf16[64,1024]{1,0:T(8,128)(2,1)S(1)}, u32[]{:S(2)}, u32[]{:S(2)}) collective-permute-start(bf16[64,1024]{1,0:T(8,128)(2,1)S(1)} %shard_map.130.one), channel_id=1, source_target_pairs={{0,4},{1,5},{2,6},{3,7},{4,0},{5,1},{6,2},{7,3},{8,12},{9,13},{10,... | collective-permute-start | bytes 393224 | tf_op jit(solution)/shard_map/ppermute | solution.py:316
  71.0 10.5 %collective-permute-start.26 = (bf16[64,1024]{1,0:T(8,128)(2,1)S(1)}, bf16[64,1024]{1,0:T(8,128)(2,1)S(1)}, u32[]{:S(2)}, u32[]{:S(2)}) collective-permute-start(bf16[64,1024]{1,0:T(8,128)(2,1)S(1)} %shard_map.131.refs_0_), channel_id=1, source_target_pairs={{0,24},{8,16},{16,8},{24,0},{1,25},{9,17},{17,9},{25,1},{2,26},{10... | collective-permute-start | bytes 393224 | tf_op jit(solution)/shard_map/ppermute | solution.py:316
  72.2 9.7 %collective-permute-start.25 = (bf16[64,1024]{1,0:T(8,128)(2,1)S(1)}, bf16[64,1024]{1,0:T(8,128)(2,1)S(1)}, u32[]{:S(2)}, u32[]{:S(2)}) collective-permute-start(bf16[64,1024]{1,0:T(8,128)(2,1)S(1)} %shard_map.131.refs_0_), channel_id=1, source_target_pairs={{0,16},{8,24},{16,0},{24,8},{1,17},{9,25},{17,1},{25,9},{2,18},{10... | collective-permute-start | bytes 393224 | tf_op jit(solution)/shard_map/ppermute | solution.py:316
  73.7 8.3 %collective-permute-start.24 = (bf16[64,1024]{1,0:T(8,128)(2,1)S(1)}, bf16[64,1024]{1,0:T(8,128)(2,1)S(1)}, u32[]{:S(2)}, u32[]{:S(2)}) collective-permute-start(bf16[64,1024]{1,0:T(8,128)(2,1)S(1)} %shard_map.131.refs_0_), channel_id=1, source_target_pairs={{0,8},{8,0},{16,24},{24,16},{1,9},{9,1},{17,25},{25,17},{2,10},{10... | collective-permute-start | bytes 393224 | tf_op jit(solution)/shard_map/ppermute | solution.py:316
  76.7 5.7 %collective-permute-start.37 = (bf16[64,512]{1,0:T(8,128)(2,1)S(1)}, bf16[64,512]{1,0:T(8,128)(2,1)S(1)}, u32[]{:S(2)}, u32[]{:S(2)}) collective-permute-start(bf16[64,512]{1,0:T(8,128)(2,1)S(1)} %shard_map.136.refs_0_), channel_id=1, source_target_pairs={{0,16},{8,24},{16,0},{24,8},{1,17},{9,25},{17,1},{25,9},{2,18},{10... | collective-permute-start | bytes 196616 | tf_op jit(solution)/shard_map/ppermute | solution.py:316
  81.4 5.8 %collective-permute-start.30 = (bf16[64,1024]{1,0:T(8,128)(2,1)S(1)}, bf16[64,1024]{1,0:T(8,128)(2,1)S(1)}, u32[]{:S(2)}, u32[]{:S(2)}) collective-permute-start(bf16[64,1024]{1,0:T(8,128)(2,1)S(1)} %collective-permute-done.26.refs_3_), channel_id=1, source_target_pairs={{0,1},{1,0},{2,3},{3,2},{4,5},{5,4},{6,7},{7,6},{8,9},{9,8},{10,11... | collective-permute-start | bytes 393224 | tf_op jit(solution)/shard_map/ppermute | solution.py:316
  81.9 5.4 %collective-permute-start.29 = (bf16[64,1024]{1,0:T(8,128)(2,1)S(1)}, bf16[64,1024]{1,0:T(8,128)(2,1)S(1)}, u32[]{:S(2)}, u32[]{:S(2)}) collective-permute-start(bf16[64,1024]{1,0:T(8,128)(2,1)S(1)} %collective-permute-done.25.refs_2_), channel_id=1, source_target_pairs={{0,1},{1,0},{2,3},{3,2},{4,5},{5,4},{6,7},{7,6},{8,9},{9,8},{10,11... | collective-permute-start | bytes 393224 | tf_op jit(solution)/shard_map/ppermute | solution.py:316
  82.0 5.7 %collective-permute-start.28 = (bf16[64,1024]{1,0:T(8,128)(2,1)S(1)}, bf16[64,1024]{1,0:T(8,128)(2,1)S(1)}, u32[]{:S(2)}, u32[]{:S(2)}) collective-permute-start(bf16[64,1024]{1,0:T(8,128)(2,1)S(1)} %collective-permute-done.24.refs_1_), channel_id=1, source_target_pairs={{0,1},{1,0},{2,3},{3,2},{4,5},{5,4},{6,7},{7,6},{8,9},{9,8},{10,11... | collective-permute-start | bytes 393224 | tf_op jit(solution)/shard_map/ppermute | solution.py:316
  (25 other events, 121.5 us)

commit v3 on v1

--- a/solution.py
+++ b/solution.py
@@ -70,6 +70,29 @@
     return call(pick_body, [sds((2 * rows, width // 2), BF)], [], [own, got], 0)[0]
 
 
+def kept_rows(flags, values):
+    rows = values.shape[0]
+    mask = jnp.broadcast_to(flags.astype(F32), (rows, rows)).T > 0
+    mask = jnp.concatenate([mask.astype(F32)] * (values.shape[1] // rows), axis=1)
+    return jnp.where(mask > 0, values, jnp.zeros_like(values))
+
+
+def keep_body(flags, values, out):
+    out[...] = kept_rows(flags[...], values[...].astype(F32)).astype(BF)
+
+
+def keep(flags, values):
+    return call(keep_body, [sds(values.shape, BF)], [], [flags, values], values.size)[0]
+
+
+def add_body(one, two, out):
+    out[...] = (one[...].astype(F32) + two[...].astype(F32)).astype(out.dtype)
+
+
+def add(one, two):
+    return call(add_body, [sds(one.shape, BF)], [], [one, two], one.size)[0]
+
+
 def start_body(one, top, start, top_t):
     start[...] = dot(one[...], top[...])
     top_t[...] = top[...].T
@@ -90,8 +113,8 @@
 def product_body(n, nz, mine, theirs, *refs):
     q, (stay, leave, rhs) = refs[:n], refs[n:]
     p, z, c = place()
-    rows = q[0].shape[0] // 2
     depth = rhs.shape[0] // 2
+    rows = depth // n
     for s in range(n):
         rhs[block(p ^ s, rows), :] = q[s][:rows, :]
         rhs[pl.ds(pl.multiple_of(depth + (p ^ s) * rows, rows), rows), :] = q[s][rows:, :]
@@ -203,17 +226,23 @@
     )[0]
 
 
-def top_body(n, *refs):
-    mine, theirs = refs[:n], refs[n : 2 * n]
-    start, top, top_t, one, two = refs[2 * n : 2 * n + 5]
-    corner, inverse_top, rest, own_t, cross = refs[2 * n + 5 :]
-    p, _, c = place()
-    low, width = mine[0].shape[0], own_t.shape[1]
-    for s in range(n):
-        for source, t in ((mine[s], c), (theirs[s], 1 - c)):
-            rows = block(t * n + (p ^ s), low)
-            own_t[rows, :] = source[:, :width]
-            cross[rows, :] = source[:, width:]
+def stack_body(n, *refs):
+    p, _, _ = place()
+    for s in range(n):
+        refs[n][block(p ^ s, refs[s].shape[0]), :] = refs[s][...]
+
+
+def stack(parts):
+    n, (low, width) = len(parts), parts[0].shape
+    return call(functools.partial(stack_body, n), [sds((n * low, width), BF)], [], parts, 0)[0]
+
+
+def top_body(mine, theirs, start, top, top_t, one, two, corner, inverse_top, rest, own_t, cross):
+    _, _, c = place()
+    half, width = mine.shape[0], own_t.shape[1]
+    for source, t in ((mine, c), (theirs, 1 - c)):
+        own_t[block(t, half), :] = source[:, :width]
+        cross[block(t, half), :] = source[:, width:]
     own = own_t[...].T
     corner[...] = (one[...].astype(F32) - own.astype(F32)).astype(BF)
     inverse_top[...] = (dot(own, top[...]) - start[...] - cross[...].astype(F32)).astype(BF)
@@ -223,28 +252,26 @@
 
 
 def top_parts(mine, theirs, start, top, top_t, one, two):
-    n, shape = len(mine), top.shape
+    shape = top.shape
     out = [sds(shape, BF), sds(shape, BF), sds(shape, F32)]
     return call(
-        functools.partial(top_body, n), out, [scratch(shape, BF)] * 2,
-        [*mine, *theirs, start, top, top_t, one, two], 6 * shape[0] ** 3,
-    )
-
-
-def last_body(n, *refs):
-    mine, theirs, rest, out, tail_t = refs[:n], refs[n : 2 * n], *refs[2 * n :]
-    p, _, c = place()
-    low = mine[0].shape[0]
-    for s in range(n):
-        for source, t in ((mine[s], c), (theirs[s], 1 - c)):
-            tail_t[block(t * n + (p ^ s), low), :] = source[...]
+        top_body, out, [scratch(shape, BF)] * 2,
+        [mine, theirs, start, top, top_t, one, two], 6 * shape[0] ** 3,
+    )
+
+
+def last_body(mine, theirs, rest, out, tail_t):
+    _, _, c = place()
+    half = mine.shape[0]
+    for source, t in ((mine, c), (theirs, 1 - c)):
+        tail_t[block(t, half), :] = source[...]
     out[...] = (rest[...] + tail_t[...].T.astype(F32)).astype(BF)
 
 
 def last_part(mine, theirs, rest):
     return call(
-        functools.partial(last_body, len(mine)), [sds(rest.shape, BF)], [scratch(rest.shape, BF)],
-        [*mine, *theirs, rest], 2 * math.prod(rest.shape),
+        last_body, [sds(rest.shape, BF)], [scratch(rest.shape, BF)],
+        [mine, theirs, rest], 2 * math.prod(rest.shape),
     )[0]
 
 
@@ -256,7 +283,7 @@
     value[:, block(c, half)] = keep_two[...]
     value[:, block(1 - c, half)] = got[:, half:]
     lower = -(value[...] + dot(inverse_one[...], top[...]))
-    inverse_two[...] = jnp.where(flags[...] > 0, lower, jnp.zeros_like(lower)).astype(BF)
+    inverse_two[...] = kept_rows(flags[...], lower).astype(BF)
 
 
 def finish(keep_one, keep_two, got, top, flags):
@@ -281,12 +308,12 @@
     over_z = lambda x, s: send(x, "pcol", m, 2 * s)
     over_p = lambda x, s: send(x, "prow", n, s)
 
-    flags = structure.reshape(piece_rows, 1)
-    masked_two = jnp.where(flags > 0, panel_two, jnp.zeros_like(panel_two))
+    flags = structure.reshape(1, piece_rows)
+    gather = lambda x: [x] + [over_p(x, s) for s in range(1, n)]
     mine_one = pick(panel_one, swap(panel_one))
+    gathered_one = gather(mine_one)
+    masked_two = keep(flags, panel_two)
     mine_two = pick(masked_two, swap(masked_two))
-    gather = lambda x: [x] + [over_p(x, s) for s in range(1, n)]
-    gathered_one = gather(mine_one)
     gathered_two = gather(mine_two)
 
     shaped = known_inverse.reshape(block_rows, BLK, col_groups, piece_blocks, BLK)
@@ -310,10 +337,10 @@
     def total(here):
         s = 1
         while s < nz:
-            here = (here.astype(F32) + over_z(here, s).astype(F32)).astype(BF)
+            here = add(here, over_z(here, s))
             s *= 2
-        got = [here] + [over_p(here, s) for s in range(1, n)]
-        return got, [swap(got[s]) for s in range(n)]
+        held = stack([here] + [over_p(here, s) for s in range(1, n)])
+        return held, swap(held)
 
     *parts_one, rows_one = product(masked, others, gathered_one, nz)
     parts_one = exchange(*parts_one)

time: 87.8 us -> 103 us (1.17)
  waiting for transfers between devices: 31.2 us -> 57.3 us
  starting transfers between devices: 45.7 us -> 34.9 us
    ppermute x40 -> x34, waiting for transfers between devices: 31.2 us -> 57.3 us  [on_device(): lax.ppermute(x, axis, [(k, k ^ s) for k in range(size)])]
    ppermute x40 -> x34, starting transfers between devices: 45.7 us -> 34.9 us  [on_device(): lax.ppermute(x, axis, [(k, k ^ s) for k in range(size)])]
    pallas_call x14 -> x21, Pallas kernels: 6.76 us -> 6.92 us  [call(): pl.pallas_call(body, out_shape=out, in_specs=[VMEM] * len(args), out_spec...]
  transfers between devices with their start and end apart: 40 -> 34, of which waited for: 16 -> 24; matrix products, arithmetic and copies ran while one was open for 0% -> 0% of each run, Pallas kernels for 7% -> 5%
where the time goes in v3:
time: 103 us
  waiting for transfers between devices  57.3 us (56%)
  starting transfers between devices  34.9 us (34%)
  Pallas kernels  6.92 us (7%)
  other arithmetic  2.33 us (2%)
    ppermute x34, waiting for transfers between devices, on_device(): lax.ppermute(x, axis, [(k, k ^ s) for k in range(size)])  57.3 us
    ppermute x34, starting transfers between devices, on_device(): lax.ppermute(x, axis, [(k, k ^ s) for k in range(size)])  34.9 us
    pallas_call x21, Pallas kernels, call(): pl.pallas_call(body, out_shape=out, in_specs=[VMEM] * len(args), out_spec...  6.92 us
  transfers between devices with their start and end apart: 34, of which 24 were waited for; matrix products, arithmetic and copies ran while one was open for 0% of the time, Pallas kernels for 5%

profile of v3, /device:TPU:0, one launch (start us, length us, event | category | flops | bytes accessed | tf_op | source)
XLA Modules:
  0.0 102.9 jit_solution(5975244941358632379)
XLA Ops:
  1.8 1.6 %bitcast_select_fusion.mine = bf16[1024,512]{1,0:T(8,128)(2,1)S(1)} fusion(pred[128,8,4,128]{3,2,1,0:T(4,128)(4,1)S(1)} %bitcast.14, bf16[128,8,4,128]{3,2,1,0:T(4,128)(2,1)} %bitcast.15), kind=kLoop, calls=%fused_computation | loop fusion | flops 524288 | bytes 2621440 | tf_op jit(solution)/shard_map/jit(_where)/select_n | solution.py:321
  4.8 1.7 %collective-permute-done.1.got = bf16[128,512]{1,0:T(8,128)(2,1)S(1)} collective-permute-done((bf16[128,512]{1,0:T(8,128)(2,1)S(1)}, bf16[128,512]{1,0:T(8,128)(2,1)S(1)}, u32[]{:S(2)}, u32[]{:S(2)}) %collective-permute-start.1) | collective-permute-done | bytes 131104 | tf_op jit(solution)/shard_map/ppermute | solution.py:306
  6.5 3.9 %collective-permute-start.4 = (bf16[256,256]{1,0:T(8,128)(2,1)S(1)}, bf16[256,256]{1,0:T(8,128)(2,1)S(1)}, u32[]{:S(2)}, u32[]{:S(2)}) collective-permute-start(bf16[256,256]{1,0:T(8,128)(2,1)S(1)} %shard_map.119.refs_0_), channel_id=1, source_target_pairs={{0,24},{8,16},{16,8},{24,0},{1,25},{9,17},{17,9},{25,1},{2,26},{10... | collective-permute-start | bytes 393224 | tf_op jit(solution)/shard_map/ppermute | solution.py:306
  11.0 2.9 %collective-permute-start.10 = (bf16[256,256]{1,0:T(8,128)(2,1)S(1)}, bf16[256,256]{1,0:T(8,128)(2,1)S(1)}, u32[]{:S(2)}, u32[]{:S(2)}) collective-permute-start(bf16[256,256]{1,0:T(8,128)(2,1)S(1)} %shard_map.124.refs_0_), channel_id=1, source_target_pairs={{0,24},{8,16},{16,8},{24,0},{1,25},{9,17},{17,9},{25,1},{2,26},{10... | collective-permute-start | bytes 393224 | tf_op jit(solution)/shard_map/ppermute | solution.py:306
  14.3 2.4 %collective-permute-start.9 = (bf16[256,256]{1,0:T(8,128)(2,1)S(1)}, bf16[256,256]{1,0:T(8,128)(2,1)S(1)}, u32[]{:S(2)}, u32[]{:S(2)}) collective-permute-start(bf16[256,256]{1,0:T(8,128)(2,1)S(1)} %shard_map.124.refs_0_), channel_id=1, source_target_pairs={{0,16},{8,24},{16,0},{24,8},{1,17},{9,25},{17,1},{25,9},{2,18},{10... | collective-permute-start | bytes 393224 | tf_op jit(solution)/shard_map/ppermute | solution.py:306
  16.7 1.6 %collective-permute-done.3.refs_2_ = bf16[256,256]{1,0:T(8,128)(2,1)S(1)} collective-permute-done((bf16[256,256]{1,0:T(8,128)(2,1)S(1)}, bf16[256,256]{1,0:T(8,128)(2,1)S(1)}, u32[]{:S(2)}, u32[]{:S(2)}) %collective-permute-start.3) | collective-permute-done | bytes 131104 | tf_op jit(solution)/shard_map/ppermute | solution.py:306
  20.5 2.1 %collective-permute-done.9.refs_2_ = bf16[256,256]{1,0:T(8,128)(2,1)S(1)} collective-permute-done((bf16[256,256]{1,0:T(8,128)(2,1)S(1)}, bf16[256,256]{1,0:T(8,128)(2,1)S(1)}, u32[]{:S(2)}, u32[]{:S(2)}) %collective-permute-start.9) | collective-permute-done | bytes 131104 | tf_op jit(solution)/shard_map/ppermute | solution.py:306
  24.4 1.6 %collective-permute-start.5 = (bf16[512,256]{1,0:T(8,128)(2,1)S(1)}, bf16[512,256]{1,0:T(8,128)(2,1)S(1)}, u32[]{:S(2)}, u32[]{:S(2)}) collective-permute-start(bf16[512,256]{1,0:T(8,128)(2,1)S(1)} %get-tuple-element.35), channel_id=1, source_target_pairs={{0,2},{1,3},{2,0},{3,1},{4,6},{5,7},{6,4},{7,5},{8,10},{9,11},{10,... | collective-permute-start | bytes 786440 | tf_op jit(solution)/shard_map/ppermute | solution.py:306
  26.0 7.1 %collective-permute-done.5.got = bf16[512,256]{1,0:T(8,128)(2,1)S(1)} collective-permute-done((bf16[512,256]{1,0:T(8,128)(2,1)S(1)}, bf16[512,256]{1,0:T(8,128)(2,1)S(1)}, u32[]{:S(2)}, u32[]{:S(2)}) %collective-permute-start.5) | collective-permute-done | bytes 262176 | tf_op jit(solution)/shard_map/ppermute | solution.py:306
  33.1 2.7 %collective-permute-start.6 = (bf16[256,256]{1,0:T(8,128)(2,1)S(1)}, bf16[256,256]{1,0:T(8,128)(2,1)S(1)}, u32[]{:S(2)}, u32[]{:S(2)}) collective-permute-start(bf16[256,256]{1,0:T(8,128)(2,1)S(1)} %get-tuple-element.37), channel_id=1, source_target_pairs={{0,4},{1,5},{2,6},{3,7},{4,0},{5,1},{6,2},{7,3},{8,12},{9,13},{10,... | collective-permute-start | bytes 393224 | tf_op jit(solution)/shard_map/ppermute | solution.py:306
  35.8 6.1 %collective-permute-done.6.refs_1_ = bf16[256,256]{1,0:T(8,128)(2,1)S(1)} collective-permute-done((bf16[256,256]{1,0:T(8,128)(2,1)S(1)}, bf16[256,256]{1,0:T(8,128)(2,1)S(1)}, u32[]{:S(2)}, u32[]{:S(2)}) %collective-permute-start.6) | collective-permute-done | bytes 131104 | tf_op jit(solution)/shard_map/ppermute | solution.py:306
  43.7 1.9 %collective-permute-start.16 = (bf16[64,256]{1,0:T(8,128)(2,1)S(1)}, bf16[64,256]{1,0:T(8,128)(2,1)S(1)}, u32[]{:S(2)}, u32[]{:S(2)}) collective-permute-start(bf16[64,256]{1,0:T(8,128)(2,1)S(1)} %get-tuple-element.50), channel_id=1, source_target_pairs={{0,24},{8,16},{16,8},{24,0},{1,25},{9,17},{17,9},{25,1},{2,26},{10... | collective-permute-start | bytes 98312 | tf_op jit(solution)/shard_map/ppermute | solution.py:306
  51.1 5.0 %collective-permute-done.19.two = bf16[64,1024]{1,0:T(8,128)(2,1)S(1)} collective-permute-done((bf16[64,1024]{1,0:T(8,128)(2,1)S(1)}, bf16[64,1024]{1,0:T(8,128)(2,1)S(1)}, u32[]{:S(2)}, u32[]{:S(2)}) %collective-permute-start.19) | collective-permute-done | bytes 131104 | tf_op jit(solution)/shard_map/ppermute | solution.py:306
  57.6 6.0 %collective-permute-done.20.two = bf16[64,1024]{1,0:T(8,128)(2,1)S(1)} collective-permute-done((bf16[64,1024]{1,0:T(8,128)(2,1)S(1)}, bf16[64,1024]{1,0:T(8,128)(2,1)S(1)}, u32[]{:S(2)}, u32[]{:S(2)}) %collective-permute-start.20) | collective-permute-done | bytes 131104 | tf_op jit(solution)/shard_map/ppermute | solution.py:306
  63.6 1.9 %collective-permute-start.23 = (bf16[64,1024]{1,0:T(8,128)(2,1)S(1)}, bf16[64,1024]{1,0:T(8,128)(2,1)S(1)}, u32[]{:S(2)}, u32[]{:S(2)}) collective-permute-start(bf16[64,1024]{1,0:T(8,128)(2,1)S(1)} %shard_map.131.refs_0_), channel_id=1, source_target_pairs={{0,24},{8,16},{16,8},{24,0},{1,25},{9,17},{17,9},{25,1},{2,26},{10... | collective-permute-start | bytes 393224 | tf_op jit(solution)/shard_map/ppermute | solution.py:306
  67.3 2.3 %collective-permute-done.23.refs_3_ = bf16[64,1024]{1,0:T(8,128)(2,1)S(1)} collective-permute-done((bf16[64,1024]{1,0:T(8,128)(2,1)S(1)}, bf16[64,1024]{1,0:T(8,128)(2,1)S(1)}, u32[]{:S(2)}, u32[]{:S(2)}) %collective-permute-start.23) | collective-permute-done | bytes 131104 | tf_op jit(solution)/shard_map/ppermute | solution.py:306
  71.8 2.4 %collective-permute-done.12.refs_1_ = bf16[256,256]{1,0:T(8,128)(2,1)S(1)} collective-permute-done((bf16[256,256]{1,0:T(8,128)(2,1)S(1)}, bf16[256,256]{1,0:T(8,128)(2,1)S(1)}, u32[]{:S(2)}, u32[]{:S(2)}) %collective-permute-start.12) | collective-permute-done | bytes 131104 | tf_op jit(solution)/shard_map/ppermute | solution.py:306
  74.4 1.7 %collective-permute-start.25 = (bf16[64,256]{1,0:T(8,128)(2,1)S(1)}, bf16[64,256]{1,0:T(8,128)(2,1)S(1)}, u32[]{:S(2)}, u32[]{:S(2)}) collective-permute-start(bf16[64,256]{1,0:T(8,128)(2,1)S(1)} %get-tuple-element.59), channel_id=1, source_target_pairs={{0,8},{8,0},{16,24},{24,16},{1,9},{9,1},{17,25},{25,17},{2,10},{10... | collective-permute-start | bytes 98312 | tf_op jit(solution)/shard_map/ppermute | solution.py:306
  78.3 1.6 %collective-permute-done.26.refs_2_ = bf16[64,256]{1,0:T(8,128)(2,1)S(1)} collective-permute-done((bf16[64,256]{1,0:T(8,128)(2,1)S(1)}, bf16[64,256]{1,0:T(8,128)(2,1)S(1)}, u32[]{:S(2)}, u32[]{:S(2)}) %collective-permute-start.26) | collective-permute-done | bytes 32800 | tf_op jit(solution)/shard_map/ppermute | solution.py:306
  80.0 1.7 %collective-permute-done.27.refs_3_ = bf16[64,256]{1,0:T(8,128)(2,1)S(1)} collective-permute-done((bf16[64,256]{1,0:T(8,128)(2,1)S(1)}, bf16[64,256]{1,0:T(8,128)(2,1)S(1)}, u32[]{:S(2)}, u32[]{:S(2)}) %collective-permute-start.27) | collective-permute-done | bytes 32800 | tf_op jit(solution)/shard_map/ppermute | solution.py:306
  82.1 4.7 %collective-permute-done.28.two = bf16[64,512]{1,0:T(8,128)(2,1)S(1)} collective-permute-done((bf16[64,512]{1,0:T(8,128)(2,1)S(1)}, bf16[64,512]{1,0:T(8,128)(2,1)S(1)}, u32[]{:S(2)}, u32[]{:S(2)}) %collective-permute-start.28) | collective-permute-done | bytes 65568 | tf_op jit(solution)/shard_map/ppermute | solution.py:306
  87.0 5.1 %collective-permute-done.29.two = bf16[64,512]{1,0:T(8,128)(2,1)S(1)} collective-permute-done((bf16[64,512]{1,0:T(8,128)(2,1)S(1)}, bf16[64,512]{1,0:T(8,128)(2,1)S(1)}, u32[]{:S(2)}, u32[]{:S(2)}) %collective-permute-start.29) | collective-permute-done | bytes 65568 | tf_op jit(solution)/shard_map/ppermute | solution.py:306
  95.7 1.7 %collective-permute-done.32.refs_3_ = bf16[64,512]{1,0:T(8,128)(2,1)S(1)} collective-permute-done((bf16[64,512]{1,0:T(8,128)(2,1)S(1)}, bf16[64,512]{1,0:T(8,128)(2,1)S(1)}, u32[]{:S(2)}, u32[]{:S(2)}) %collective-permute-start.32) | collective-permute-done | bytes 65568 | tf_op jit(solution)/shard_map/ppermute | solution.py:306
  100.4 1.5 %shard_map.134 = (bf16[512,512]{1,0:T(8,128)(2,1)}, bf16[512,512]{1,0:T(8,128)(2,1)}, f32[512,512]{1,0:T(8,128)S(1)}) custom-call(bf16[256,1024]{1,0:T(8,128)(2,1)S(1)} %shard_map.132.mine, bf16[256,1024]{1,0:T(8,128)(2,1)S(1)} %collective-permute-done.24.theirs, f32[512,512]{1,0:T(8,128)S(1)} %get-tuple-element.53.start, bf16[512,512]{1,0:T(8,128)(2,1)S(1)} %copy-done, ...), custom_call_target="tpu_custom_call" | custom-call | flops 805306368 | bytes 6291456 | tf_op jit(solution)/shard_map/pallas_call | solution.py:31
  (81 shorter events, 30.7 us)
Async XLA Ops:
  3.4 16.1 %collective-permute-start = (bf16[1024,512]{1,0:T(8,128)(2,1)S(1)}, bf16[1024,512]{1,0:T(8,128)(2,1)S(1)}, u32[]{:S(2)}, u32[]{:S(2)}) collective-permute-start(bf16[1024,512]{1,0:T(8,128)(2,1)S(1)} %bitcast_select_fusion.mine), channel_id=1, source_target_pairs={{0,1},{1,0},{2,3},{3,2},{4,5},{5,4},{6,7},{7,6},{8,9},{9,8},{10,11... | collective-permute-start | bytes 3145736 | tf_op jit(solution)/shard_map/ppermute | solution.py:306
  4.2 6.8 %collective-permute-start.7 = (bf16[128,512]{1,0:T(8,128)(2,1)S(1)}, bf16[128,512]{1,0:T(8,128)(2,1)S(1)}, u32[]{:S(2)}, u32[]{:S(2)}) collective-permute-start(bf16[128,512]{1,0:T(8,128)(2,1)S(1)} %shard_map.123.own), channel_id=1, source_target_pairs={{0,1},{1,0},{2,3},{3,2},{4,5},{5,4},{6,7},{7,6},{8,9},{9,8},{10,11... | collective-permute-start | bytes 393224 | tf_op jit(solution)/shard_map/ppermute | solution.py:306
  6.5 7.8 %collective-permute-start.4 = (bf16[256,256]{1,0:T(8,128)(2,1)S(1)}, bf16[256,256]{1,0:T(8,128)(2,1)S(1)}, u32[]{:S(2)}, u32[]{:S(2)}) collective-permute-start(bf16[256,256]{1,0:T(8,128)(2,1)S(1)} %shard_map.119.refs_0_), channel_id=1, source_target_pairs={{0,24},{8,16},{16,8},{24,0},{1,25},{9,17},{17,9},{25,1},{2,26},{10... | collective-permute-start | bytes 393224 | tf_op jit(solution)/shard_map/ppermute | solution.py:306
  10.4 7.9 %collective-permute-start.3 = (bf16[256,256]{1,0:T(8,128)(2,1)S(1)}, bf16[256,256]{1,0:T(8,128)(2,1)S(1)}, u32[]{:S(2)}, u32[]{:S(2)}) collective-permute-start(bf16[256,256]{1,0:T(8,128)(2,1)S(1)} %shard_map.119.refs_0_), channel_id=1, source_target_pairs={{0,16},{8,24},{16,0},{24,8},{1,17},{9,25},{17,1},{25,9},{2,18},{10... | collective-permute-start | bytes 393224 | tf_op jit(solution)/shard_map/ppermute | solution.py:306
  10.9 8.7 %collective-permute-start.2 = (bf16[256,256]{1,0:T(8,128)(2,1)S(1)}, bf16[256,256]{1,0:T(8,128)(2,1)S(1)}, u32[]{:S(2)}, u32[]{:S(2)}) collective-permute-start(bf16[256,256]{1,0:T(8,128)(2,1)S(1)} %shard_map.119.refs_0_), channel_id=1, source_target_pairs={{0,8},{8,0},{16,24},{24,16},{1,9},{9,1},{17,25},{25,17},{2,10},{10... | collective-permute-start | bytes 393224 | tf_op jit(solution)/shard_map/ppermute | solution.py:306
  11.0 9.4 %collective-permute-start.10 = (bf16[256,256]{1,0:T(8,128)(2,1)S(1)}, bf16[256,256]{1,0:T(8,128)(2,1)S(1)}, u32[]{:S(2)}, u32[]{:S(2)}) collective-permute-start(bf16[256,256]{1,0:T(8,128)(2,1)S(1)} %shard_map.124.refs_0_), channel_id=1, source_target_pairs={{0,24},{8,16},{16,8},{24,0},{1,25},{9,17},{17,9},{25,1},{2,26},{10... | collective-permute-start | bytes 393224 | tf_op jit(solution)/shard_map/ppermute | solution.py:306
  14.3 8.3 %collective-permute-start.9 = (bf16[256,256]{1,0:T(8,128)(2,1)S(1)}, bf16[256,256]{1,0:T(8,128)(2,1)S(1)}, u32[]{:S(2)}, u32[]{:S(2)}) collective-permute-start(bf16[256,256]{1,0:T(8,128)(2,1)S(1)} %shard_map.124.refs_0_), channel_id=1, source_target_pairs={{0,16},{8,24},{16,0},{24,8},{1,17},{9,25},{17,1},{25,9},{2,18},{10... | collective-permute-start | bytes 393224 | tf_op jit(solution)/shard_map/ppermute | solution.py:306
  18.3 5.2 %collective-permute-start.8 = (bf16[256,256]{1,0:T(8,128)(2,1)S(1)}, bf16[256,256]{1,0:T(8,128)(2,1)S(1)}, u32[]{:S(2)}, u32[]{:S(2)}) collective-permute-start(bf16[256,256]{1,0:T(8,128)(2,1)S(1)} %shard_map.124.refs_0_), channel_id=1, source_target_pairs={{0,8},{8,0},{16,24},{24,16},{1,9},{9,1},{17,25},{25,17},{2,10},{10... | collective-permute-start | bytes 393224 | tf_op jit(solution)/shard_map/ppermute | solution.py:306
  20.4 28.1 %collective-permute-start.17 = (bf16[1024,256]{1,0:T(8,128)(2,1)S(1)}, bf16[1024,256]{1,0:T(8,128)(2,1)S(1)}, u32[]{:S(2)}, u32[]{:S(2)}) collective-permute-start(bf16[1024,256]{1,0:T(8,128)(2,1)S(1)} %get-tuple-element.51.refs_4_), channel_id=1, source_target_pairs={{0,1},{1,0},{2,3},{3,2},{4,5},{5,4},{6,7},{7,6},{8,9},{9,8},{10,11... | collective-permute-start | bytes 1572872 | tf_op jit(solution)/shard_map/ppermute | solution.py:306
  24.3 24.2 %collective-permute-start.18 = (bf16[1024,256]{1,0:T(8,128)(2,1)S(1)}, bf16[1024,256]{1,0:T(8,128)(2,1)S(1)}, u32[]{:S(2)}, u32[]{:S(2)}) collective-permute-start(bf16[1024,256]{1,0:T(8,128)(2,1)S(1)} %get-tuple-element.52.refs_6_.refs_4_), channel_id=1, source_target_pairs={{0,1},{1,0},{2,3},{3,2},{4,5},{5,4},{6,7},{7,6},{8,9},{9,8},{10,11... | collective-permute-start | bytes 1572872 | tf_op jit(solution)/shard_map/ppermute | solution.py:306
  24.4 8.7 %collective-permute-start.5 = (bf16[512,256]{1,0:T(8,128)(2,1)S(1)}, bf16[512,256]{1,0:T(8,128)(2,1)S(1)}, u32[]{:S(2)}, u32[]{:S(2)}) collective-permute-start(bf16[512,256]{1,0:T(8,128)(2,1)S(1)} %get-tuple-element.35), channel_id=1, source_target_pairs={{0,2},{1,3},{2,0},{3,1},{4,6},{5,7},{6,4},{7,5},{8,10},{9,11},{10,... | collective-permute-start | bytes 786440 | tf_op jit(solution)/shard_map/ppermute | solution.py:306
  33.1 8.7 %collective-permute-start.6 = (bf16[256,256]{1,0:T(8,128)(2,1)S(1)}, bf16[256,256]{1,0:T(8,128)(2,1)S(1)}, u32[]{:S(2)}, u32[]{:S(2)}) collective-permute-start(bf16[256,256]{1,0:T(8,128)(2,1)S(1)} %get-tuple-element.37), channel_id=1, source_target_pairs={{0,4},{1,5},{2,6},{3,7},{4,0},{5,1},{6,2},{7,3},{8,12},{9,13},{10,... | collective-permute-start | bytes 393224 | tf_op jit(solution)/shard_map/ppermute | solution.py:306
  43.7 4.8 %collective-permute-start.16 = (bf16[64,256]{1,0:T(8,128)(2,1)S(1)}, bf16[64,256]{1,0:T(8,128)(2,1)S(1)}, u32[]{:S(2)}, u32[]{:S(2)}) collective-permute-start(bf16[64,256]{1,0:T(8,128)(2,1)S(1)} %get-tuple-element.50), channel_id=1, source_target_pairs={{0,24},{8,16},{16,8},{24,0},{1,25},{9,17},{17,9},{25,1},{2,26},{10... | collective-permute-start | bytes 98312 | tf_op jit(solution)/shard_map/ppermute | solution.py:306
  49.0 7.1 %collective-permute-start.19 = (bf16[64,1024]{1,0:T(8,128)(2,1)S(1)}, bf16[64,1024]{1,0:T(8,128)(2,1)S(1)}, u32[]{:S(2)}, u32[]{:S(2)}) collective-permute-start(bf16[64,1024]{1,0:T(8,128)(2,1)S(1)} %shard_map.129.one), channel_id=1, source_target_pairs={{0,2},{1,3},{2,0},{3,1},{4,6},{5,7},{6,4},{7,5},{8,10},{9,11},{10,... | collective-permute-start | bytes 393224 | tf_op jit(solution)/shard_map/ppermute | solution.py:306
  49.7 17.4 %collective-permute-start.11 = (bf16[512,256]{1,0:T(8,128)(2,1)S(1)}, bf16[512,256]{1,0:T(8,128)(2,1)S(1)}, u32[]{:S(2)}, u32[]{:S(2)}) collective-permute-start(bf16[512,256]{1,0:T(8,128)(2,1)S(1)} %get-tuple-element.40), channel_id=1, source_target_pairs={{0,2},{1,3},{2,0},{3,1},{4,6},{5,7},{6,4},{7,5},{8,10},{9,11},{10,... | collective-permute-start | bytes 786440 | tf_op jit(solution)/shard_map/ppermute | solution.py:306
  56.1 7.5 %collective-permute-start.20 = (bf16[64,1024]{1,0:T(8,128)(2,1)S(1)}, bf16[64,1024]{1,0:T(8,128)(2,1)S(1)}, u32[]{:S(2)}, u32[]{:S(2)}) collective-permute-start(bf16[64,1024]{1,0:T(8,128)(2,1)S(1)} %shard_map.130.one), channel_id=1, source_target_pairs={{0,4},{1,5},{2,6},{3,7},{4,0},{5,1},{6,2},{7,3},{8,12},{9,13},{10,... | collective-permute-start | bytes 393224 | tf_op jit(solution)/shard_map/ppermute | solution.py:306
  63.6 6.0 %collective-permute-start.23 = (bf16[64,1024]{1,0:T(8,128)(2,1)S(1)}, bf16[64,1024]{1,0:T(8,128)(2,1)S(1)}, u32[]{:S(2)}, u32[]{:S(2)}) collective-permute-start(bf16[64,1024]{1,0:T(8,128)(2,1)S(1)} %shard_map.131.refs_0_), channel_id=1, source_target_pairs={{0,24},{8,16},{16,8},{24,0},{1,25},{9,17},{17,9},{25,1},{2,26},{10... | collective-permute-start | bytes 393224 | tf_op jit(solution)/shard_map/ppermute | solution.py:306
  65.6 5.4 %collective-permute-start.22 = (bf16[64,1024]{1,0:T(8,128)(2,1)S(1)}, bf16[64,1024]{1,0:T(8,128)(2,1)S(1)}, u32[]{:S(2)}, u32[]{:S(2)}) collective-permute-start(bf16[64,1024]{1,0:T(8,128)(2,1)S(1)} %shard_map.131.refs_0_), channel_id=1, source_target_pairs={{0,16},{8,24},{16,0},{24,8},{1,17},{9,25},{17,1},{25,9},{2,18},{10... | collective-permute-start | bytes 393224 | tf_op jit(solution)/shard_map/ppermute | solution.py:306
  66.7 5.0 %collective-permute-start.21 = (bf16[64,1024]{1,0:T(8,128)(2,1)S(1)}, bf16[64,1024]{1,0:T(8,128)(2,1)S(1)}, u32[]{:S(2)}, u32[]{:S(2)}) collective-permute-start(bf16[64,1024]{1,0:T(8,128)(2,1)S(1)} %shard_map.131.refs_0_), channel_id=1, source_target_pairs={{0,8},{8,0},{16,24},{24,16},{1,9},{9,1},{17,25},{25,17},{2,10},{10... | collective-permute-start | bytes 393224 | tf_op jit(solution)/shard_map/ppermute | solution.py:306
  67.2 7.0 %collective-permute-start.12 = (bf16[256,256]{1,0:T(8,128)(2,1)S(1)}, bf16[256,256]{1,0:T(8,128)(2,1)S(1)}, u32[]{:S(2)}, u32[]{:S(2)}) collective-permute-start(bf16[256,256]{1,0:T(8,128)(2,1)S(1)} %get-tuple-element.42), channel_id=1, source_target_pairs={{0,4},{1,5},{2,6},{3,7},{4,0},{5,1},{6,2},{7,3},{8,12},{9,13},{10,... | collective-permute-start | bytes 393224 | tf_op jit(solution)/shard_map/ppermute | solution.py:306
  71.7 28.5 %collective-permute-start.24 = (bf16[256,1024]{1,0:T(8,128)(2,1)S(1)}, bf16[256,1024]{1,0:T(8,128)(2,1)S(1)}, u32[]{:S(2)}, u32[]{:S(2)}) collective-permute-start(bf16[256,1024]{1,0:T(8,128)(2,1)S(1)} %shard_map.132.mine), channel_id=1, source_target_pairs={{0,1},{1,0},{2,3},{3,2},{4,5},{5,4},{6,7},{7,6},{8,9},{9,8},{10,11... | collective-permute-start | bytes 1572872 | tf_op jit(solution)/shard_map/ppermute | solution.py:306
  86.9 5.2 %collective-permute-start.29 = (bf16[64,512]{1,0:T(8,128)(2,1)S(1)}, bf16[64,512]{1,0:T(8,128)(2,1)S(1)}, u32[]{:S(2)}, u32[]{:S(2)}) collective-permute-start(bf16[64,512]{1,0:T(8,128)(2,1)S(1)} %shard_map.136.one), channel_id=1, source_target_pairs={{0,4},{1,5},{2,6},{3,7},{4,0},{5,1},{6,2},{7,3},{8,12},{9,13},{10,... | collective-permute-start | bytes 196616 | tf_op jit(solution)/shard_map/ppermute | solution.py:306
  86.9 12.4 %collective-permute-start.13 = (f32[128,512]{1,0:T(8,128)S(1)}, f32[128,512]{1,0:T(8,128)S(1)}, u32[]{:S(2)}, u32[]{:S(2)}) collective-permute-start(f32[128,512]{1,0:T(8,128)S(1)} %get-tuple-element.45), channel_id=1, source_target_pairs={{0,1},{1,0},{2,3},{3,2},{4,5},{5,4},{6,7},{7,6},{8,9},{9,8},{10,11... | collective-permute-start | bytes 786440 | tf_op jit(solution)/shard_map/ppermute | solution.py:306
  92.1 5.3 %collective-permute-start.32 = (bf16[64,512]{1,0:T(8,128)(2,1)S(1)}, bf16[64,512]{1,0:T(8,128)(2,1)S(1)}, u32[]{:S(2)}, u32[]{:S(2)}) collective-permute-start(bf16[64,512]{1,0:T(8,128)(2,1)S(1)} %shard_map.137.refs_0_), channel_id=1, source_target_pairs={{0,24},{8,16},{16,8},{24,0},{1,25},{9,17},{17,9},{25,1},{2,26},{10... | collective-permute-start | bytes 196616 | tf_op jit(solution)/shard_map/ppermute | solution.py:306
  (16 other events, 80.4 us)

commit v4 on v3

--- a/solution.py
+++ b/solution.py
@@ -39,10 +39,8 @@
     )(*args)
 
 
-def tree(parts):
-    while len(parts) > 1:
-        parts = [parts[k] + parts[k + 1] for k in range(0, len(parts), 2)]
-    return parts[0]
+def total_of(parts):
+    return sum(part[...].astype(F32) for part in parts)
 
 
 def dot(a, b):
@@ -89,8 +87,8 @@
     out[...] = (one[...].astype(F32) + two[...].astype(F32)).astype(out.dtype)
 
 
-def add(one, two):
-    return call(add_body, [sds(one.shape, BF)], [], [one, two], one.size)[0]
+def add(one, two, kind=BF):
+    return call(add_body, [sds(one.shape, kind)], [], [one, two], one.size)[0]
 
 
 def start_body(one, top, start, top_t):
@@ -111,18 +109,16 @@
 
 
 def product_body(n, nz, mine, theirs, *refs):
-    q, (stay, leave, rhs) = refs[:n], refs[n:]
+    q, (*outs, rhs) = refs[:n], refs[n:]
     p, z, c = place()
     depth = rhs.shape[0] // 2
     rows = depth // n
     for s in range(n):
         rhs[block(p ^ s, rows), :] = q[s][:rows, :]
         rhs[pl.ds(pl.multiple_of(depth + (p ^ s) * rows, rows), rows), :] = q[s][rows:, :]
-    order = sequence(nz)
-    for k in range(nz // 2, nz):
-        emit(leave, k - nz // 2, order[k], z, c, rows, mine, theirs, rhs)
-    for k in range(nz // 2):
-        emit(stay, k, order[k], z, c, rows, mine, theirs, rhs)
+    order, size = sequence(nz), nz // 4
+    for k in reversed(range(nz)):
+        emit(outs[k // size], k % size, order[k], z, c, rows, mine, theirs, rhs)
 
 
 def emit(out, k, offset, z, c, rows, mine, theirs, rhs):
@@ -136,23 +132,12 @@
 def product(mine, theirs, q, nz):
     n, (rows, half) = len(q), q[0].shape
     depth = mine.shape[1]
-    shape = (nz // 2 * rows, half)
-    out = [sds(shape, F32), sds(shape, BF), sds((2 * depth, half), BF)]
+    shape = (nz // 4 * rows, half)
+    out = [sds(shape, F32)] * 2 + [sds(shape, BF)] * 2 + [sds((2 * depth, half), BF)]
     return call(
         functools.partial(product_body, n, nz), out, [],
         [mine, theirs, *q], 4 * mine.shape[0] * depth * half,
     )
-
-
-def fold_body(held, got, stay, leave):
-    rows = stay.shape[0]
-    stay[...] = held[:rows] + got[:rows].astype(F32)
-    leave[...] = (held[rows:] + got[rows:].astype(F32)).astype(BF)
-
-
-def fold(held, got):
-    shape = (held.shape[0] // 2, held.shape[1])
-    return call(fold_body, [sds(shape, F32), sds(shape, BF)], [], [held, got], 2 * held.size)
 
 
 def first_body(n, nz, *refs):
@@ -160,7 +145,7 @@
     keep, give, outs, turned = refs[nz], refs[nz + 1], refs[nz + 2 : nz + 2 + n], refs[nz + 2 + n]
     p, _, _ = place()
     rows = keep.shape[0]
-    inverse = -tree([parts[s][...].astype(F32) for s in range(nz)])
+    inverse = -total_of(parts)
     keep[...] = inverse[:rows].astype(BF)
     give[...] = inverse[rows:].astype(BF)
     turned[...] = inverse.T
@@ -173,7 +158,7 @@
     keep, give, outs, turned = refs[nz + 1], refs[nz + 2], refs[nz + 3 : nz + 3 + n], refs[nz + 3 + n]
     p, _, _ = place()
     rows, half = keep.shape
-    value = tree([parts[s][...].astype(F32) for s in range(nz)])
+    value = total_of(parts)
     keep[...] = value[:rows]
     give[:, :half] = give_one[...].astype(F32)
     give[:, half:] = value[rows:]
@@ -318,18 +303,26 @@
 
     shaped = known_inverse.reshape(block_rows, BLK, col_groups, piece_blocks, BLK)
     flag_table = pattern.reshape(block_rows, 1, col_groups, piece_blocks, 1)
-    masked = jnp.where(flag_table > 0, shaped, jnp.zeros_like(shaped)).reshape(
+    kept = jnp.broadcast_to(flag_table > 0, shaped.shape)
+    masked = jnp.where(kept, shaped, jnp.zeros_like(shaped)).reshape(
         row_count, col_groups * piece_rows
     )
     others = swap(masked)
     start, top_t = start_parts(diag_one, panel_top)
 
-    def exchange(stay, leave):
-        got, s = over_z(leave, 1), 2
-        while s < nz:
-            stay, leave = fold(stay, got)
-            got, s = over_z(leave, s), 2 * s
-        return [stay, got]
+    def exchange(keep_held, go_held, keep_leave, go_leave):
+        s, count = 1, nz // 4
+        while True:
+            go_got = over_z(go_leave, s)
+            keep_got = over_z(keep_leave, s)
+            s *= 2
+            leave = add(go_held, go_got)
+            if count == 1:
+                return [keep_held, keep_got, over_z(leave, s)]
+            held = add(keep_held, keep_got, F32)
+            keep_held, go_held = jnp.split(held, 2)
+            keep_leave, go_leave = jnp.split(leave, 2)
+            count //= 2
 
     def spread(pieces):
         return [pieces[0]] + [over_p(pieces[s], s) for s in range(1, n)]

time: 103 us -> 99.9 us (0.970)
  waiting for transfers between devices: 57.3 us -> 47.3 us
  starting transfers between devices: 34.9 us -> 41.7 us
    ppermute x34 -> x36, waiting for transfers between devices: 57.3 us -> 47.3 us  [on_device(): lax.ppermute(x, axis, [(k, k ^ s) for k in range(size)])]
    ppermute x34 -> x36, starting transfers between devices: 34.9 us -> 41.7 us  [on_device(): lax.ppermute(x, axis, [(k, k ^ s) for k in range(size)])]
  transfers between devices with their start and end apart: 34 -> 36, of which waited for: 24 -> 23; matrix products, arithmetic and copies ran while one was open for 0% -> 0% of each run, Pallas kernels for 5% -> 5%
where the time goes in v4:
time: 99.9 us; the launch traced here: 99.6 us
  waiting for transfers between devices  47.3 us (47%)
  starting transfers between devices  41.7 us (42%)
  Pallas kernels  6.84 us (7%)
  other arithmetic  2.33 us (2%)
    ppermute x36, waiting for transfers between devices, on_device(): lax.ppermute(x, axis, [(k, k ^ s) for k in range(size)])  47.3 us
    ppermute x36, starting transfers between devices, on_device(): lax.ppermute(x, axis, [(k, k ^ s) for k in range(size)])  41.7 us
    pallas_call x21, Pallas kernels, call(): pl.pallas_call(body, out_shape=out, in_specs=[VMEM] * len(args), out_spec...  6.84 us
  transfers between devices with their start and end apart: 36, of which 23 were waited for; matrix products, arithmetic and copies ran while one was open for 0% of the time, Pallas kernels for 5%

profile of v4, /device:TPU:0, one launch (start us, length us, event | category | flops | bytes accessed | tf_op | source)
XLA Modules:
  0.0 99.6 jit_solution(18415217233988385812)
XLA Ops:
  1.8 1.6 %bitcast_select_fusion.mine = bf16[1024,512]{1,0:T(8,128)(2,1)S(1)} fusion(pred[128,8,4,128]{3,2,1,0:T(4,128)(4,1)S(1)} %bitcast.14, bf16[128,8,4,128]{3,2,1,0:T(4,128)(2,1)} %bitcast.15), kind=kLoop, calls=%fused_computation | loop fusion | flops 524288 | bytes 2621440 | tf_op jit(solution)/shard_map/jit(_where)/select_n | solution.py:307
  4.8 1.7 %collective-permute-done.1.got = bf16[128,512]{1,0:T(8,128)(2,1)S(1)} collective-permute-done((bf16[128,512]{1,0:T(8,128)(2,1)S(1)}, bf16[128,512]{1,0:T(8,128)(2,1)S(1)}, u32[]{:S(2)}, u32[]{:S(2)}) %collective-permute-start.1) | collective-permute-done | bytes 131104 | tf_op jit(solution)/shard_map/ppermute | solution.py:291
  6.5 3.9 %collective-permute-start.4 = (bf16[256,256]{1,0:T(8,128)(2,1)S(1)}, bf16[256,256]{1,0:T(8,128)(2,1)S(1)}, u32[]{:S(2)}, u32[]{:S(2)}) collective-permute-start(bf16[256,256]{1,0:T(8,128)(2,1)S(1)} %shard_map.119.refs_0_), channel_id=1, source_target_pairs={{0,24},{8,16},{16,8},{24,0},{1,25},{9,17},{17,9},{25,1},{2,26},{10... | collective-permute-start | bytes 393224 | tf_op jit(solution)/shard_map/ppermute | solution.py:291
  11.0 2.9 %collective-permute-start.11 = (bf16[256,256]{1,0:T(8,128)(2,1)S(1)}, bf16[256,256]{1,0:T(8,128)(2,1)S(1)}, u32[]{:S(2)}, u32[]{:S(2)}) collective-permute-start(bf16[256,256]{1,0:T(8,128)(2,1)S(1)} %shard_map.124.refs_0_), channel_id=1, source_target_pairs={{0,24},{8,16},{16,8},{24,0},{1,25},{9,17},{17,9},{25,1},{2,26},{10... | collective-permute-start | bytes 393224 | tf_op jit(solution)/shard_map/ppermute | solution.py:291
  14.3 2.4 %collective-permute-start.10 = (bf16[256,256]{1,0:T(8,128)(2,1)S(1)}, bf16[256,256]{1,0:T(8,128)(2,1)S(1)}, u32[]{:S(2)}, u32[]{:S(2)}) collective-permute-start(bf16[256,256]{1,0:T(8,128)(2,1)S(1)} %shard_map.124.refs_0_), channel_id=1, source_target_pairs={{0,16},{8,24},{16,0},{24,8},{1,17},{9,25},{17,1},{25,9},{2,18},{10... | collective-permute-start | bytes 393224 | tf_op jit(solution)/shard_map/ppermute | solution.py:291
  20.4 2.2 %collective-permute-done.10.refs_2_ = bf16[256,256]{1,0:T(8,128)(2,1)S(1)} collective-permute-done((bf16[256,256]{1,0:T(8,128)(2,1)S(1)}, bf16[256,256]{1,0:T(8,128)(2,1)S(1)}, u32[]{:S(2)}, u32[]{:S(2)}) %collective-permute-start.10) | collective-permute-done | bytes 131104 | tf_op jit(solution)/shard_map/ppermute | solution.py:291
  24.3 1.6 %collective-permute-start.6 = (bf16[256,256]{1,0:T(8,128)(2,1)S(1)}, bf16[256,256]{1,0:T(8,128)(2,1)S(1)}, u32[]{:S(2)}, u32[]{:S(2)}) collective-permute-start(bf16[256,256]{1,0:T(8,128)(2,1)S(1)} %get-tuple-element.37), channel_id=1, source_target_pairs={{0,2},{1,3},{2,0},{3,1},{4,6},{5,7},{6,4},{7,5},{8,10},{9,11},{10,... | collective-permute-start | bytes 393224 | tf_op jit(solution)/shard_map/ppermute | solution.py:291
  26.4 4.3 %collective-permute-done.6.two = bf16[256,256]{1,0:T(8,128)(2,1)S(1)} collective-permute-done((bf16[256,256]{1,0:T(8,128)(2,1)S(1)}, bf16[256,256]{1,0:T(8,128)(2,1)S(1)}, u32[]{:S(2)}, u32[]{:S(2)}) %collective-permute-start.6) | collective-permute-done | bytes 131104 | tf_op jit(solution)/shard_map/ppermute | solution.py:291
  30.8 2.7 %collective-permute-start.7 = (bf16[256,256]{1,0:T(8,128)(2,1)S(1)}, bf16[256,256]{1,0:T(8,128)(2,1)S(1)}, u32[]{:S(2)}, u32[]{:S(2)}) collective-permute-start(bf16[256,256]{1,0:T(8,128)(2,1)S(1)} %shard_map.121), channel_id=1, source_target_pairs={{0,4},{1,5},{2,6},{3,7},{4,0},{5,1},{6,2},{7,3},{8,12},{9,13},{10,... | collective-permute-start | bytes 393224 | tf_op jit(solution)/shard_map/ppermute | solution.py:291
  33.5 5.7 %collective-permute-done.7.refs_2_ = bf16[256,256]{1,0:T(8,128)(2,1)S(1)} collective-permute-done((bf16[256,256]{1,0:T(8,128)(2,1)S(1)}, bf16[256,256]{1,0:T(8,128)(2,1)S(1)}, u32[]{:S(2)}, u32[]{:S(2)}) %collective-permute-start.7) | collective-permute-done | bytes 131104 | tf_op jit(solution)/shard_map/ppermute | solution.py:291
  41.0 1.9 %collective-permute-start.18 = (bf16[64,256]{1,0:T(8,128)(2,1)S(1)}, bf16[64,256]{1,0:T(8,128)(2,1)S(1)}, u32[]{:S(2)}, u32[]{:S(2)}) collective-permute-start(bf16[64,256]{1,0:T(8,128)(2,1)S(1)} %get-tuple-element.50), channel_id=1, source_target_pairs={{0,24},{8,16},{16,8},{24,0},{1,25},{9,17},{17,9},{25,1},{2,26},{10... | collective-permute-start | bytes 98312 | tf_op jit(solution)/shard_map/ppermute | solution.py:291
  46.9 4.4 %collective-permute-done.21.two = bf16[64,1024]{1,0:T(8,128)(2,1)S(1)} collective-permute-done((bf16[64,1024]{1,0:T(8,128)(2,1)S(1)}, bf16[64,1024]{1,0:T(8,128)(2,1)S(1)}, u32[]{:S(2)}, u32[]{:S(2)}) %collective-permute-start.21) | collective-permute-done | bytes 131104 | tf_op jit(solution)/shard_map/ppermute | solution.py:291
  51.4 2.0 %collective-permute-start.22 = (bf16[64,1024]{1,0:T(8,128)(2,1)S(1)}, bf16[64,1024]{1,0:T(8,128)(2,1)S(1)}, u32[]{:S(2)}, u32[]{:S(2)}) collective-permute-start(bf16[64,1024]{1,0:T(8,128)(2,1)S(1)} %shard_map.130.one), channel_id=1, source_target_pairs={{0,4},{1,5},{2,6},{3,7},{4,0},{5,1},{6,2},{7,3},{8,12},{9,13},{10,... | collective-permute-start | bytes 393224 | tf_op jit(solution)/shard_map/ppermute | solution.py:291
  53.3 2.2 %collective-permute-start.13 = (bf16[256,256]{1,0:T(8,128)(2,1)S(1)}, bf16[256,256]{1,0:T(8,128)(2,1)S(1)}, u32[]{:S(2)}, u32[]{:S(2)}) collective-permute-start(bf16[256,256]{1,0:T(8,128)(2,1)S(1)} %get-tuple-element.42), channel_id=1, source_target_pairs={{0,2},{1,3},{2,0},{3,1},{4,6},{5,7},{6,4},{7,5},{8,10},{9,11},{10,... | collective-permute-start | bytes 393224 | tf_op jit(solution)/shard_map/ppermute | solution.py:291
  55.6 3.2 %collective-permute-done.22.two = bf16[64,1024]{1,0:T(8,128)(2,1)S(1)} collective-permute-done((bf16[64,1024]{1,0:T(8,128)(2,1)S(1)}, bf16[64,1024]{1,0:T(8,128)(2,1)S(1)}, u32[]{:S(2)}, u32[]{:S(2)}) %collective-permute-start.22) | collective-permute-done | bytes 131104 | tf_op jit(solution)/shard_map/ppermute | solution.py:291
  58.8 2.0 %collective-permute-start.25 = (bf16[64,1024]{1,0:T(8,128)(2,1)S(1)}, bf16[64,1024]{1,0:T(8,128)(2,1)S(1)}, u32[]{:S(2)}, u32[]{:S(2)}) collective-permute-start(bf16[64,1024]{1,0:T(8,128)(2,1)S(1)} %shard_map.131.refs_0_), channel_id=1, source_target_pairs={{0,24},{8,16},{16,8},{24,0},{1,25},{9,17},{17,9},{25,1},{2,26},{10... | collective-permute-start | bytes 393224 | tf_op jit(solution)/shard_map/ppermute | solution.py:291
  63.1 2.7 %collective-permute-start.14 = (bf16[256,256]{1,0:T(8,128)(2,1)S(1)}, bf16[256,256]{1,0:T(8,128)(2,1)S(1)}, u32[]{:S(2)}, u32[]{:S(2)}) collective-permute-start(bf16[256,256]{1,0:T(8,128)(2,1)S(1)} %shard_map.126), channel_id=1, source_target_pairs={{0,4},{1,5},{2,6},{3,7},{4,0},{5,1},{6,2},{7,3},{8,12},{9,13},{10,... | collective-permute-start | bytes 393224 | tf_op jit(solution)/shard_map/ppermute | solution.py:291
  67.5 1.9 %collective-permute-done.12.refs_1_ = bf16[256,256]{1,0:T(8,128)(2,1)S(1)} collective-permute-done((bf16[256,256]{1,0:T(8,128)(2,1)S(1)}, bf16[256,256]{1,0:T(8,128)(2,1)S(1)}, u32[]{:S(2)}, u32[]{:S(2)}) %collective-permute-start.12) | collective-permute-done | bytes 131104 | tf_op jit(solution)/shard_map/ppermute | solution.py:291
  69.6 2.7 %collective-permute-start.27 = (bf16[64,256]{1,0:T(8,128)(2,1)S(1)}, bf16[64,256]{1,0:T(8,128)(2,1)S(1)}, u32[]{:S(2)}, u32[]{:S(2)}) collective-permute-start(bf16[64,256]{1,0:T(8,128)(2,1)S(1)} %get-tuple-element.59), channel_id=1, source_target_pairs={{0,8},{8,0},{16,24},{24,16},{1,9},{9,1},{17,25},{25,17},{2,10},{10... | collective-permute-start | bytes 98312 | tf_op jit(solution)/shard_map/ppermute | solution.py:291
  74.1 2.0 %collective-permute-done.28.refs_2_ = bf16[64,256]{1,0:T(8,128)(2,1)S(1)} collective-permute-done((bf16[64,256]{1,0:T(8,128)(2,1)S(1)}, bf16[64,256]{1,0:T(8,128)(2,1)S(1)}, u32[]{:S(2)}, u32[]{:S(2)}) %collective-permute-start.28) | collective-permute-done | bytes 32800 | tf_op jit(solution)/shard_map/ppermute | solution.py:291
  76.2 1.7 %collective-permute-done.29.refs_3_ = bf16[64,256]{1,0:T(8,128)(2,1)S(1)} collective-permute-done((bf16[64,256]{1,0:T(8,128)(2,1)S(1)}, bf16[64,256]{1,0:T(8,128)(2,1)S(1)}, u32[]{:S(2)}, u32[]{:S(2)}) %collective-permute-start.29) | collective-permute-done | bytes 32800 | tf_op jit(solution)/shard_map/ppermute | solution.py:291
  78.6 4.6 %collective-permute-done.30.two = bf16[64,512]{1,0:T(8,128)(2,1)S(1)} collective-permute-done((bf16[64,512]{1,0:T(8,128)(2,1)S(1)}, bf16[64,512]{1,0:T(8,128)(2,1)S(1)}, u32[]{:S(2)}, u32[]{:S(2)}) %collective-permute-start.30) | collective-permute-done | bytes 65568 | tf_op jit(solution)/shard_map/ppermute | solution.py:291
  84.1 4.3 %collective-permute-done.31.two = bf16[64,512]{1,0:T(8,128)(2,1)S(1)} collective-permute-done((bf16[64,512]{1,0:T(8,128)(2,1)S(1)}, bf16[64,512]{1,0:T(8,128)(2,1)S(1)}, u32[]{:S(2)}, u32[]{:S(2)}) %collective-permute-start.31) | collective-permute-done | bytes 65568 | tf_op jit(solution)/shard_map/ppermute | solution.py:291
  92.0 1.7 %collective-permute-done.34.refs_3_ = bf16[64,512]{1,0:T(8,128)(2,1)S(1)} collective-permute-done((bf16[64,512]{1,0:T(8,128)(2,1)S(1)}, bf16[64,512]{1,0:T(8,128)(2,1)S(1)}, u32[]{:S(2)}, u32[]{:S(2)}) %collective-permute-start.34) | collective-permute-done | bytes 65568 | tf_op jit(solution)/shard_map/ppermute | solution.py:291
  (85 shorter events, 32.5 us)
Async XLA Ops:
  3.4 16.1 %collective-permute-start = (bf16[1024,512]{1,0:T(8,128)(2,1)S(1)}, bf16[1024,512]{1,0:T(8,128)(2,1)S(1)}, u32[]{:S(2)}, u32[]{:S(2)}) collective-permute-start(bf16[1024,512]{1,0:T(8,128)(2,1)S(1)} %bitcast_select_fusion.mine), channel_id=1, source_target_pairs={{0,1},{1,0},{2,3},{3,2},{4,5},{5,4},{6,7},{7,6},{8,9},{9,8},{10,11... | collective-permute-start | bytes 3145736 | tf_op jit(solution)/shard_map/ppermute | solution.py:291
  4.2 6.8 %collective-permute-start.8 = (bf16[128,512]{1,0:T(8,128)(2,1)S(1)}, bf16[128,512]{1,0:T(8,128)(2,1)S(1)}, u32[]{:S(2)}, u32[]{:S(2)}) collective-permute-start(bf16[128,512]{1,0:T(8,128)(2,1)S(1)} %shard_map.123.own), channel_id=1, source_target_pairs={{0,1},{1,0},{2,3},{3,2},{4,5},{5,4},{6,7},{7,6},{8,9},{9,8},{10,11... | collective-permute-start | bytes 393224 | tf_op jit(solution)/shard_map/ppermute | solution.py:291
  6.5 7.8 %collective-permute-start.4 = (bf16[256,256]{1,0:T(8,128)(2,1)S(1)}, bf16[256,256]{1,0:T(8,128)(2,1)S(1)}, u32[]{:S(2)}, u32[]{:S(2)}) collective-permute-start(bf16[256,256]{1,0:T(8,128)(2,1)S(1)} %shard_map.119.refs_0_), channel_id=1, source_target_pairs={{0,24},{8,16},{16,8},{24,0},{1,25},{9,17},{17,9},{25,1},{2,26},{10... | collective-permute-start | bytes 393224 | tf_op jit(solution)/shard_map/ppermute | solution.py:291
  10.4 7.9 %collective-permute-start.3 = (bf16[256,256]{1,0:T(8,128)(2,1)S(1)}, bf16[256,256]{1,0:T(8,128)(2,1)S(1)}, u32[]{:S(2)}, u32[]{:S(2)}) collective-permute-start(bf16[256,256]{1,0:T(8,128)(2,1)S(1)} %shard_map.119.refs_0_), channel_id=1, source_target_pairs={{0,16},{8,24},{16,0},{24,8},{1,17},{9,25},{17,1},{25,9},{2,18},{10... | collective-permute-start | bytes 393224 | tf_op jit(solution)/shard_map/ppermute | solution.py:291
  10.9 8.7 %collective-permute-start.2 = (bf16[256,256]{1,0:T(8,128)(2,1)S(1)}, bf16[256,256]{1,0:T(8,128)(2,1)S(1)}, u32[]{:S(2)}, u32[]{:S(2)}) collective-permute-start(bf16[256,256]{1,0:T(8,128)(2,1)S(1)} %shard_map.119.refs_0_), channel_id=1, source_target_pairs={{0,8},{8,0},{16,24},{24,16},{1,9},{9,1},{17,25},{25,17},{2,10},{10... | collective-permute-start | bytes 393224 | tf_op jit(solution)/shard_map/ppermute | solution.py:291
  11.0 9.4 %collective-permute-start.11 = (bf16[256,256]{1,0:T(8,128)(2,1)S(1)}, bf16[256,256]{1,0:T(8,128)(2,1)S(1)}, u32[]{:S(2)}, u32[]{:S(2)}) collective-permute-start(bf16[256,256]{1,0:T(8,128)(2,1)S(1)} %shard_map.124.refs_0_), channel_id=1, source_target_pairs={{0,24},{8,16},{16,8},{24,0},{1,25},{9,17},{17,9},{25,1},{2,26},{10... | collective-permute-start | bytes 393224 | tf_op jit(solution)/shard_map/ppermute | solution.py:291
  14.3 8.3 %collective-permute-start.10 = (bf16[256,256]{1,0:T(8,128)(2,1)S(1)}, bf16[256,256]{1,0:T(8,128)(2,1)S(1)}, u32[]{:S(2)}, u32[]{:S(2)}) collective-permute-start(bf16[256,256]{1,0:T(8,128)(2,1)S(1)} %shard_map.124.refs_0_), channel_id=1, source_target_pairs={{0,16},{8,24},{16,0},{24,8},{1,17},{9,25},{17,1},{25,9},{2,18},{10... | collective-permute-start | bytes 393224 | tf_op jit(solution)/shard_map/ppermute | solution.py:291
  18.3 5.2 %collective-permute-start.9 = (bf16[256,256]{1,0:T(8,128)(2,1)S(1)}, bf16[256,256]{1,0:T(8,128)(2,1)S(1)}, u32[]{:S(2)}, u32[]{:S(2)}) collective-permute-start(bf16[256,256]{1,0:T(8,128)(2,1)S(1)} %shard_map.124.refs_0_), channel_id=1, source_target_pairs={{0,8},{8,0},{16,24},{24,16},{1,9},{9,1},{17,25},{25,17},{2,10},{10... | collective-permute-start | bytes 393224 | tf_op jit(solution)/shard_map/ppermute | solution.py:291
  20.3 25.4 %collective-permute-start.19 = (bf16[1024,256]{1,0:T(8,128)(2,1)S(1)}, bf16[1024,256]{1,0:T(8,128)(2,1)S(1)}, u32[]{:S(2)}, u32[]{:S(2)}) collective-permute-start(bf16[1024,256]{1,0:T(8,128)(2,1)S(1)} %get-tuple-element.51.refs_4_), channel_id=1, source_target_pairs={{0,1},{1,0},{2,3},{3,2},{4,5},{5,4},{6,7},{7,6},{8,9},{9,8},{10,11... | collective-permute-start | bytes 1572872 | tf_op jit(solution)/shard_map/ppermute | solution.py:291
  24.3 21.5 %collective-permute-start.20 = (bf16[1024,256]{1,0:T(8,128)(2,1)S(1)}, bf16[1024,256]{1,0:T(8,128)(2,1)S(1)}, u32[]{:S(2)}, u32[]{:S(2)}) collective-permute-start(bf16[1024,256]{1,0:T(8,128)(2,1)S(1)} %get-tuple-element.52.refs_6_.refs_4_), channel_id=1, source_target_pairs={{0,1},{1,0},{2,3},{3,2},{4,5},{5,4},{6,7},{7,6},{8,9},{9,8},{10,11... | collective-permute-start | bytes 1572872 | tf_op jit(solution)/shard_map/ppermute | solution.py:291
  24.3 6.4 %collective-permute-start.6 = (bf16[256,256]{1,0:T(8,128)(2,1)S(1)}, bf16[256,256]{1,0:T(8,128)(2,1)S(1)}, u32[]{:S(2)}, u32[]{:S(2)}) collective-permute-start(bf16[256,256]{1,0:T(8,128)(2,1)S(1)} %get-tuple-element.37), channel_id=1, source_target_pairs={{0,2},{1,3},{2,0},{3,1},{4,6},{5,7},{6,4},{7,5},{8,10},{9,11},{10,... | collective-permute-start | bytes 393224 | tf_op jit(solution)/shard_map/ppermute | solution.py:291
  26.0 7.5 %collective-permute-start.5 = (bf16[256,256]{1,0:T(8,128)(2,1)S(1)}, bf16[256,256]{1,0:T(8,128)(2,1)S(1)}, u32[]{:S(2)}, u32[]{:S(2)}) collective-permute-start(bf16[256,256]{1,0:T(8,128)(2,1)S(1)} %get-tuple-element.35), channel_id=1, source_target_pairs={{0,2},{1,3},{2,0},{3,1},{4,6},{5,7},{6,4},{7,5},{8,10},{9,11},{10,... | collective-permute-start | bytes 393224 | tf_op jit(solution)/shard_map/ppermute | solution.py:291
  30.8 8.3 %collective-permute-start.7 = (bf16[256,256]{1,0:T(8,128)(2,1)S(1)}, bf16[256,256]{1,0:T(8,128)(2,1)S(1)}, u32[]{:S(2)}, u32[]{:S(2)}) collective-permute-start(bf16[256,256]{1,0:T(8,128)(2,1)S(1)} %shard_map.121), channel_id=1, source_target_pairs={{0,4},{1,5},{2,6},{3,7},{4,0},{5,1},{6,2},{7,3},{8,12},{9,13},{10,... | collective-permute-start | bytes 393224 | tf_op jit(solution)/shard_map/ppermute | solution.py:291
  51.4 7.4 %collective-permute-start.22 = (bf16[64,1024]{1,0:T(8,128)(2,1)S(1)}, bf16[64,1024]{1,0:T(8,128)(2,1)S(1)}, u32[]{:S(2)}, u32[]{:S(2)}) collective-permute-start(bf16[64,1024]{1,0:T(8,128)(2,1)S(1)} %shard_map.130.one), channel_id=1, source_target_pairs={{0,4},{1,5},{2,6},{3,7},{4,0},{5,1},{6,2},{7,3},{8,12},{9,13},{10,... | collective-permute-start | bytes 393224 | tf_op jit(solution)/shard_map/ppermute | solution.py:291
  53.3 9.7 %collective-permute-start.13 = (bf16[256,256]{1,0:T(8,128)(2,1)S(1)}, bf16[256,256]{1,0:T(8,128)(2,1)S(1)}, u32[]{:S(2)}, u32[]{:S(2)}) collective-permute-start(bf16[256,256]{1,0:T(8,128)(2,1)S(1)} %get-tuple-element.42), channel_id=1, source_target_pairs={{0,2},{1,3},{2,0},{3,1},{4,6},{5,7},{6,4},{7,5},{8,10},{9,11},{10,... | collective-permute-start | bytes 393224 | tf_op jit(solution)/shard_map/ppermute | solution.py:291
  58.8 6.9 %collective-permute-start.25 = (bf16[64,1024]{1,0:T(8,128)(2,1)S(1)}, bf16[64,1024]{1,0:T(8,128)(2,1)S(1)}, u32[]{:S(2)}, u32[]{:S(2)}) collective-permute-start(bf16[64,1024]{1,0:T(8,128)(2,1)S(1)} %shard_map.131.refs_0_), channel_id=1, source_target_pairs={{0,24},{8,16},{16,8},{24,0},{1,25},{9,17},{17,9},{25,1},{2,26},{10... | collective-permute-start | bytes 393224 | tf_op jit(solution)/shard_map/ppermute | solution.py:291
  60.8 5.4 %collective-permute-start.24 = (bf16[64,1024]{1,0:T(8,128)(2,1)S(1)}, bf16[64,1024]{1,0:T(8,128)(2,1)S(1)}, u32[]{:S(2)}, u32[]{:S(2)}) collective-permute-start(bf16[64,1024]{1,0:T(8,128)(2,1)S(1)} %shard_map.131.refs_0_), channel_id=1, source_target_pairs={{0,16},{8,24},{16,0},{24,8},{1,17},{9,25},{17,1},{25,9},{2,18},{10... | collective-permute-start | bytes 393224 | tf_op jit(solution)/shard_map/ppermute | solution.py:291
  62.1 5.3 %collective-permute-start.23 = (bf16[64,1024]{1,0:T(8,128)(2,1)S(1)}, bf16[64,1024]{1,0:T(8,128)(2,1)S(1)}, u32[]{:S(2)}, u32[]{:S(2)}) collective-permute-start(bf16[64,1024]{1,0:T(8,128)(2,1)S(1)} %shard_map.131.refs_0_), channel_id=1, source_target_pairs={{0,8},{8,0},{16,24},{24,16},{1,9},{9,1},{17,25},{25,17},{2,10},{10... | collective-permute-start | bytes 393224 | tf_op jit(solution)/shard_map/ppermute | solution.py:291
  63.0 6.4 %collective-permute-start.12 = (bf16[256,256]{1,0:T(8,128)(2,1)S(1)}, bf16[256,256]{1,0:T(8,128)(2,1)S(1)}, u32[]{:S(2)}, u32[]{:S(2)}) collective-permute-start(bf16[256,256]{1,0:T(8,128)(2,1)S(1)} %get-tuple-element.40), channel_id=1, source_target_pairs={{0,2},{1,3},{2,0},{3,1},{4,6},{5,7},{6,4},{7,5},{8,10},{9,11},{10,... | collective-permute-start | bytes 393224 | tf_op jit(solution)/shard_map/ppermute | solution.py:291
  63.1 6.3 %collective-permute-start.14 = (bf16[256,256]{1,0:T(8,128)(2,1)S(1)}, bf16[256,256]{1,0:T(8,128)(2,1)S(1)}, u32[]{:S(2)}, u32[]{:S(2)}) collective-permute-start(bf16[256,256]{1,0:T(8,128)(2,1)S(1)} %shard_map.126), channel_id=1, source_target_pairs={{0,4},{1,5},{2,6},{3,7},{4,0},{5,1},{6,2},{7,3},{8,12},{9,13},{10,... | collective-permute-start | bytes 393224 | tf_op jit(solution)/shard_map/ppermute | solution.py:291
  67.5 29.5 %collective-permute-start.26 = (bf16[256,1024]{1,0:T(8,128)(2,1)S(1)}, bf16[256,1024]{1,0:T(8,128)(2,1)S(1)}, u32[]{:S(2)}, u32[]{:S(2)}) collective-permute-start(bf16[256,1024]{1,0:T(8,128)(2,1)S(1)} %shard_map.132.mine), channel_id=1, source_target_pairs={{0,1},{1,0},{2,3},{3,2},{4,5},{5,4},{6,7},{7,6},{8,9},{9,8},{10,11... | collective-permute-start | bytes 1572872 | tf_op jit(solution)/shard_map/ppermute | solution.py:291
  83.2 5.2 %collective-permute-start.31 = (bf16[64,512]{1,0:T(8,128)(2,1)S(1)}, bf16[64,512]{1,0:T(8,128)(2,1)S(1)}, u32[]{:S(2)}, u32[]{:S(2)}) collective-permute-start(bf16[64,512]{1,0:T(8,128)(2,1)S(1)} %shard_map.136.one), channel_id=1, source_target_pairs={{0,4},{1,5},{2,6},{3,7},{4,0},{5,1},{6,2},{7,3},{8,12},{9,13},{10,... | collective-permute-start | bytes 196616 | tf_op jit(solution)/shard_map/ppermute | solution.py:291
  84.1 12.0 %collective-permute-start.15 = (f32[128,512]{1,0:T(8,128)S(1)}, f32[128,512]{1,0:T(8,128)S(1)}, u32[]{:S(2)}, u32[]{:S(2)}) collective-permute-start(f32[128,512]{1,0:T(8,128)S(1)} %get-tuple-element.45), channel_id=1, source_target_pairs={{0,1},{1,0},{2,3},{3,2},{4,5},{5,4},{6,7},{7,6},{8,9},{9,8},{10,11... | collective-permute-start | bytes 786440 | tf_op jit(solution)/shard_map/ppermute | solution.py:291
  88.4 5.3 %collective-permute-start.34 = (bf16[64,512]{1,0:T(8,128)(2,1)S(1)}, bf16[64,512]{1,0:T(8,128)(2,1)S(1)}, u32[]{:S(2)}, u32[]{:S(2)}) collective-permute-start(bf16[64,512]{1,0:T(8,128)(2,1)S(1)} %shard_map.137.refs_0_), channel_id=1, source_target_pairs={{0,24},{8,16},{16,8},{24,0},{1,25},{9,17},{17,9},{25,1},{2,26},{10... | collective-permute-start | bytes 196616 | tf_op jit(solution)/shard_map/ppermute | solution.py:291
  (18 other events, 92.0 us)

commit v5 on v4

--- a/solution.py
+++ b/solution.py
@@ -83,6 +83,18 @@
     return call(keep_body, [sds(values.shape, BF)], [], [flags, values], values.size)[0]
 
 
+def tree_body(*refs):
+    parts, out = [ref[...].astype(F32) for ref in refs[:-1]], refs[-1]
+    while len(parts) > 1:
+        parts = [parts[k] + parts[k + 1] for k in range(0, len(parts), 2)]
+    out[...] = parts[0].astype(BF)
+
+
+def tree(parts):
+    one = parts[0]
+    return call(tree_body, [sds(one.shape, BF)], [], parts, len(parts) * one.size)[0]
+
+
 def add_body(one, two, out):
     out[...] = (one[...].astype(F32) + two[...].astype(F32)).astype(out.dtype)
 
@@ -303,8 +315,7 @@
 
     shaped = known_inverse.reshape(block_rows, BLK, col_groups, piece_blocks, BLK)
     flag_table = pattern.reshape(block_rows, 1, col_groups, piece_blocks, 1)
-    kept = jnp.broadcast_to(flag_table > 0, shaped.shape)
-    masked = jnp.where(kept, shaped, jnp.zeros_like(shaped)).reshape(
+    masked = jnp.where(flag_table > 0, shaped, jnp.zeros_like(shaped)).reshape(
         row_count, col_groups * piece_rows
     )
     others = swap(masked)
@@ -327,11 +338,12 @@
     def spread(pieces):
         return [pieces[0]] + [over_p(pieces[s], s) for s in range(1, n)]
 
-    def total(here):
-        s = 1
-        while s < nz:
-            here = add(here, over_z(here, s))
-            s *= 2
+    def doubled(here):
+        for k in range(nz.bit_length() - 1):
+            here = add(here, over_z(here, 2**k))
+        return here
+
+    def spread_out(here):
         held = stack([here] + [over_p(here, s) for s in range(1, n)])
         return held, swap(held)
 
@@ -347,9 +359,10 @@
     sums_one = sums(pieces_one, panels)
     sums_two = sums(pieces_two, panels[2:])
     corner_one, inverse_top, rest = top_parts(
-        *total(sums_one), start, panel_top, top_t, diag_one, diag_two
-    )
-    corner_two = last_part(*total(sums_two), rest)
+        *spread_out(doubled(sums_one)), start, panel_top, top_t, diag_one, diag_two
+    )
+    sums_two = tree([sums_two] + [over_z(sums_two, s) for s in range(1, nz)])
+    corner_two = last_part(*spread_out(sums_two), rest)
     inverse_one, inverse_two = finish(keep_one, keep_two, swap(give), panel_top, flags)
     return inverse_one, corner_one, inverse_top, inverse_two, corner_two
 

time: 99.9 us -> 104 us (1.041)
  waiting for transfers between devices: 47.3 us -> 50.4 us
    ppermute x36 -> x37, waiting for transfers between devices: 47.3 us -> 50.4 us  [on_device(): lax.ppermute(x, axis, [(k, k ^ s) for k in range(size)])]
    ppermute x36 -> x37, starting transfers between devices: 41.7 us -> 42.3 us  [on_device(): lax.ppermute(x, axis, [(k, k ^ s) for k in range(size)])]
    pallas_call x21 -> x20, Pallas kernels: 6.84 us -> 6.83 us  [call(): pl.pallas_call(body, out_shape=out, in_specs=[VMEM] * len(args), out_spec...]
  transfers between devices with their start and end apart: 36 -> 37, of which waited for: 23 -> 26; matrix products, arithmetic and copies ran while one was open for 0% -> 0% of each run, Pallas kernels for 5% -> 5%
where the time goes in v5:
time: 104 us; the launch traced here: 103 us
  waiting for transfers between devices  50.4 us (48%)
  starting transfers between devices  42.3 us (41%)
  Pallas kernels  6.83 us (7%)
  other arithmetic  2.33 us (2%)
    ppermute x37, waiting for transfers between devices, on_device(): lax.ppermute(x, axis, [(k, k ^ s) for k in range(size)])  50.4 us
    ppermute x37, starting transfers between devices, on_device(): lax.ppermute(x, axis, [(k, k ^ s) for k in range(size)])  42.3 us
    pallas_call x20, Pallas kernels, call(): pl.pallas_call(body, out_shape=out, in_specs=[VMEM] * len(args), out_spec...  6.83 us
  transfers between devices with their start and end apart: 37, of which 26 were waited for; matrix products, arithmetic and copies ran while one was open for 0% of the time, Pallas kernels for 5%

profile of v5, /device:TPU:0, one launch (start us, length us, event | category | flops | bytes accessed | tf_op | source)
XLA Modules:
  0.0 103.4 jit_solution(3680568574049809519)
XLA Ops:
  1.8 1.6 %bitcast_select_fusion.mine = bf16[1024,512]{1,0:T(8,128)(2,1)S(1)} fusion(pred[128,8,4,128]{3,2,1,0:T(4,128)(4,1)S(1)} %bitcast.14, bf16[128,8,4,128]{3,2,1,0:T(4,128)(2,1)} %bitcast.15), kind=kLoop, calls=%fused_computation | loop fusion | flops 524288 | bytes 2621440 | tf_op jit(solution)/shard_map/jit(_where)/select_n | solution.py:318
  4.8 1.7 %collective-permute-done.1.got = bf16[128,512]{1,0:T(8,128)(2,1)S(1)} collective-permute-done((bf16[128,512]{1,0:T(8,128)(2,1)S(1)}, bf16[128,512]{1,0:T(8,128)(2,1)S(1)}, u32[]{:S(2)}, u32[]{:S(2)}) %collective-permute-start.1) | collective-permute-done | bytes 131104 | tf_op jit(solution)/shard_map/ppermute | solution.py:303
  6.5 3.9 %collective-permute-start.4 = (bf16[256,256]{1,0:T(8,128)(2,1)S(1)}, bf16[256,256]{1,0:T(8,128)(2,1)S(1)}, u32[]{:S(2)}, u32[]{:S(2)}) collective-permute-start(bf16[256,256]{1,0:T(8,128)(2,1)S(1)} %shard_map.119.refs_0_), channel_id=1, source_target_pairs={{0,24},{8,16},{16,8},{24,0},{1,25},{9,17},{17,9},{25,1},{2,26},{10... | collective-permute-start | bytes 393224 | tf_op jit(solution)/shard_map/ppermute | solution.py:303
  11.0 2.9 %collective-permute-start.11 = (bf16[256,256]{1,0:T(8,128)(2,1)S(1)}, bf16[256,256]{1,0:T(8,128)(2,1)S(1)}, u32[]{:S(2)}, u32[]{:S(2)}) collective-permute-start(bf16[256,256]{1,0:T(8,128)(2,1)S(1)} %shard_map.124.refs_0_), channel_id=1, source_target_pairs={{0,24},{8,16},{16,8},{24,0},{1,25},{9,17},{17,9},{25,1},{2,26},{10... | collective-permute-start | bytes 393224 | tf_op jit(solution)/shard_map/ppermute | solution.py:303
  14.3 2.4 %collective-permute-start.10 = (bf16[256,256]{1,0:T(8,128)(2,1)S(1)}, bf16[256,256]{1,0:T(8,128)(2,1)S(1)}, u32[]{:S(2)}, u32[]{:S(2)}) collective-permute-start(bf16[256,256]{1,0:T(8,128)(2,1)S(1)} %shard_map.124.refs_0_), channel_id=1, source_target_pairs={{0,16},{8,24},{16,0},{24,8},{1,17},{9,25},{17,1},{25,9},{2,18},{10... | collective-permute-start | bytes 393224 | tf_op jit(solution)/shard_map/ppermute | solution.py:303
  20.4 2.2 %collective-permute-done.10.refs_2_ = bf16[256,256]{1,0:T(8,128)(2,1)S(1)} collective-permute-done((bf16[256,256]{1,0:T(8,128)(2,1)S(1)}, bf16[256,256]{1,0:T(8,128)(2,1)S(1)}, u32[]{:S(2)}, u32[]{:S(2)}) %collective-permute-start.10) | collective-permute-done | bytes 131104 | tf_op jit(solution)/shard_map/ppermute | solution.py:303
  24.3 1.6 %collective-permute-start.6 = (bf16[256,256]{1,0:T(8,128)(2,1)S(1)}, bf16[256,256]{1,0:T(8,128)(2,1)S(1)}, u32[]{:S(2)}, u32[]{:S(2)}) collective-permute-start(bf16[256,256]{1,0:T(8,128)(2,1)S(1)} %get-tuple-element.37), channel_id=1, source_target_pairs={{0,2},{1,3},{2,0},{3,1},{4,6},{5,7},{6,4},{7,5},{8,10},{9,11},{10,... | collective-permute-start | bytes 393224 | tf_op jit(solution)/shard_map/ppermute | solution.py:303
  26.4 4.3 %collective-permute-done.6.two = bf16[256,256]{1,0:T(8,128)(2,1)S(1)} collective-permute-done((bf16[256,256]{1,0:T(8,128)(2,1)S(1)}, bf16[256,256]{1,0:T(8,128)(2,1)S(1)}, u32[]{:S(2)}, u32[]{:S(2)}) %collective-permute-start.6) | collective-permute-done | bytes 131104 | tf_op jit(solution)/shard_map/ppermute | solution.py:303
  30.8 2.7 %collective-permute-start.7 = (bf16[256,256]{1,0:T(8,128)(2,1)S(1)}, bf16[256,256]{1,0:T(8,128)(2,1)S(1)}, u32[]{:S(2)}, u32[]{:S(2)}) collective-permute-start(bf16[256,256]{1,0:T(8,128)(2,1)S(1)} %shard_map.121), channel_id=1, source_target_pairs={{0,4},{1,5},{2,6},{3,7},{4,0},{5,1},{6,2},{7,3},{8,12},{9,13},{10,... | collective-permute-start | bytes 393224 | tf_op jit(solution)/shard_map/ppermute | solution.py:303
  33.5 5.7 %collective-permute-done.7.refs_2_ = bf16[256,256]{1,0:T(8,128)(2,1)S(1)} collective-permute-done((bf16[256,256]{1,0:T(8,128)(2,1)S(1)}, bf16[256,256]{1,0:T(8,128)(2,1)S(1)}, u32[]{:S(2)}, u32[]{:S(2)}) %collective-permute-start.7) | collective-permute-done | bytes 131104 | tf_op jit(solution)/shard_map/ppermute | solution.py:303
  41.0 1.9 %collective-permute-start.18 = (bf16[64,256]{1,0:T(8,128)(2,1)S(1)}, bf16[64,256]{1,0:T(8,128)(2,1)S(1)}, u32[]{:S(2)}, u32[]{:S(2)}) collective-permute-start(bf16[64,256]{1,0:T(8,128)(2,1)S(1)} %get-tuple-element.50), channel_id=1, source_target_pairs={{0,24},{8,16},{16,8},{24,0},{1,25},{9,17},{17,9},{25,1},{2,26},{10... | collective-permute-start | bytes 98312 | tf_op jit(solution)/shard_map/ppermute | solution.py:303
  46.9 4.4 %collective-permute-done.21.two = bf16[64,1024]{1,0:T(8,128)(2,1)S(1)} collective-permute-done((bf16[64,1024]{1,0:T(8,128)(2,1)S(1)}, bf16[64,1024]{1,0:T(8,128)(2,1)S(1)}, u32[]{:S(2)}, u32[]{:S(2)}) %collective-permute-start.21) | collective-permute-done | bytes 131104 | tf_op jit(solution)/shard_map/ppermute | solution.py:303
  51.4 2.0 %collective-permute-start.22 = (bf16[64,1024]{1,0:T(8,128)(2,1)S(1)}, bf16[64,1024]{1,0:T(8,128)(2,1)S(1)}, u32[]{:S(2)}, u32[]{:S(2)}) collective-permute-start(bf16[64,1024]{1,0:T(8,128)(2,1)S(1)} %shard_map.130.one), channel_id=1, source_target_pairs={{0,4},{1,5},{2,6},{3,7},{4,0},{5,1},{6,2},{7,3},{8,12},{9,13},{10,... | collective-permute-start | bytes 393224 | tf_op jit(solution)/shard_map/ppermute | solution.py:303
  53.3 5.4 %collective-permute-done.22.two = bf16[64,1024]{1,0:T(8,128)(2,1)S(1)} collective-permute-done((bf16[64,1024]{1,0:T(8,128)(2,1)S(1)}, bf16[64,1024]{1,0:T(8,128)(2,1)S(1)}, u32[]{:S(2)}, u32[]{:S(2)}) %collective-permute-start.22) | collective-permute-done | bytes 131104 | tf_op jit(solution)/shard_map/ppermute | solution.py:303
  58.7 2.0 %collective-permute-start.25 = (bf16[64,1024]{1,0:T(8,128)(2,1)S(1)}, bf16[64,1024]{1,0:T(8,128)(2,1)S(1)}, u32[]{:S(2)}, u32[]{:S(2)}) collective-permute-start(bf16[64,1024]{1,0:T(8,128)(2,1)S(1)} %shard_map.131.refs_0_), channel_id=1, source_target_pairs={{0,24},{8,16},{16,8},{24,0},{1,25},{9,17},{17,9},{25,1},{2,26},{10... | collective-permute-start | bytes 393224 | tf_op jit(solution)/shard_map/ppermute | solution.py:303
  62.5 2.2 %collective-permute-done.25.refs_3_ = bf16[64,1024]{1,0:T(8,128)(2,1)S(1)} collective-permute-done((bf16[64,1024]{1,0:T(8,128)(2,1)S(1)}, bf16[64,1024]{1,0:T(8,128)(2,1)S(1)}, u32[]{:S(2)}, u32[]{:S(2)}) %collective-permute-start.25) | collective-permute-done | bytes 131104 | tf_op jit(solution)/shard_map/ppermute | solution.py:303
  67.5 3.3 %collective-permute-start.14 = (bf16[256,256]{1,0:T(8,128)(2,1)S(1)}, bf16[256,256]{1,0:T(8,128)(2,1)S(1)}, u32[]{:S(2)}, u32[]{:S(2)}) collective-permute-start(bf16[256,256]{1,0:T(8,128)(2,1)S(1)} %shard_map.126), channel_id=1, source_target_pairs={{0,4},{1,5},{2,6},{3,7},{4,0},{5,1},{6,2},{7,3},{8,12},{9,13},{10,... | collective-permute-start | bytes 393224 | tf_op jit(solution)/shard_map/ppermute | solution.py:303
  70.8 4.7 %collective-permute-done.12.refs_1_ = bf16[256,256]{1,0:T(8,128)(2,1)S(1)} collective-permute-done((bf16[256,256]{1,0:T(8,128)(2,1)S(1)}, bf16[256,256]{1,0:T(8,128)(2,1)S(1)}, u32[]{:S(2)}, u32[]{:S(2)}) %collective-permute-start.12) | collective-permute-done | bytes 131104 | tf_op jit(solution)/shard_map/ppermute | solution.py:303
  75.5 2.0 %collective-permute-done.14.refs_2_ = bf16[256,256]{1,0:T(8,128)(2,1)S(1)} collective-permute-done((bf16[256,256]{1,0:T(8,128)(2,1)S(1)}, bf16[256,256]{1,0:T(8,128)(2,1)S(1)}, u32[]{:S(2)}, u32[]{:S(2)}) %collective-permute-start.14) | collective-permute-done | bytes 131104 | tf_op jit(solution)/shard_map/ppermute | solution.py:303
  82.5 2.2 %collective-permute-done.29.refs_3_ = bf16[64,256]{1,0:T(8,128)(2,1)S(1)} collective-permute-done((bf16[64,256]{1,0:T(8,128)(2,1)S(1)}, bf16[64,256]{1,0:T(8,128)(2,1)S(1)}, u32[]{:S(2)}, u32[]{:S(2)}) %collective-permute-start.29) | collective-permute-done | bytes 32800 | tf_op jit(solution)/shard_map/ppermute | solution.py:303
  85.0 2.4 %collective-permute-start.32 = (bf16[64,512]{1,0:T(8,128)(2,1)S(1)}, bf16[64,512]{1,0:T(8,128)(2,1)S(1)}, u32[]{:S(2)}, u32[]{:S(2)}) collective-permute-start(bf16[64,512]{1,0:T(8,128)(2,1)S(1)} %shard_map.135.refs_0_), channel_id=1, source_target_pairs={{0,6},{1,7},{2,4},{3,5},{4,2},{5,3},{6,0},{7,1},{8,14},{9,15},{10,... | collective-permute-start | bytes 196616 | tf_op jit(solution)/shard_map/ppermute | solution.py:303
  87.4 2.0 %collective-permute-start.30 = (bf16[64,512]{1,0:T(8,128)(2,1)S(1)}, bf16[64,512]{1,0:T(8,128)(2,1)S(1)}, u32[]{:S(2)}, u32[]{:S(2)}) collective-permute-start(bf16[64,512]{1,0:T(8,128)(2,1)S(1)} %shard_map.135.refs_0_), channel_id=1, source_target_pairs={{0,2},{1,3},{2,0},{3,1},{4,6},{5,7},{6,4},{7,5},{8,10},{9,11},{10,... | collective-permute-start | bytes 196616 | tf_op jit(solution)/shard_map/ppermute | solution.py:303
  89.4 1.7 %collective-permute-done.32.refs_3_ = bf16[64,512]{1,0:T(8,128)(2,1)S(1)} collective-permute-done((bf16[64,512]{1,0:T(8,128)(2,1)S(1)}, bf16[64,512]{1,0:T(8,128)(2,1)S(1)}, u32[]{:S(2)}, u32[]{:S(2)}) %collective-permute-start.32) | collective-permute-done | bytes 65568 | tf_op jit(solution)/shard_map/ppermute | solution.py:303
  96.1 1.7 %collective-permute-done.35.refs_3_ = bf16[64,512]{1,0:T(8,128)(2,1)S(1)} collective-permute-done((bf16[64,512]{1,0:T(8,128)(2,1)S(1)}, bf16[64,512]{1,0:T(8,128)(2,1)S(1)}, u32[]{:S(2)}, u32[]{:S(2)}) %collective-permute-start.35) | collective-permute-done | bytes 65568 | tf_op jit(solution)/shard_map/ppermute | solution.py:303
  (86 shorter events, 35.7 us)
Async XLA Ops:
  3.4 16.1 %collective-permute-start = (bf16[1024,512]{1,0:T(8,128)(2,1)S(1)}, bf16[1024,512]{1,0:T(8,128)(2,1)S(1)}, u32[]{:S(2)}, u32[]{:S(2)}) collective-permute-start(bf16[1024,512]{1,0:T(8,128)(2,1)S(1)} %bitcast_select_fusion.mine), channel_id=1, source_target_pairs={{0,1},{1,0},{2,3},{3,2},{4,5},{5,4},{6,7},{7,6},{8,9},{9,8},{10,11... | collective-permute-start | bytes 3145736 | tf_op jit(solution)/shard_map/ppermute | solution.py:303
  4.2 6.8 %collective-permute-start.8 = (bf16[128,512]{1,0:T(8,128)(2,1)S(1)}, bf16[128,512]{1,0:T(8,128)(2,1)S(1)}, u32[]{:S(2)}, u32[]{:S(2)}) collective-permute-start(bf16[128,512]{1,0:T(8,128)(2,1)S(1)} %shard_map.123.own), channel_id=1, source_target_pairs={{0,1},{1,0},{2,3},{3,2},{4,5},{5,4},{6,7},{7,6},{8,9},{9,8},{10,11... | collective-permute-start | bytes 393224 | tf_op jit(solution)/shard_map/ppermute | solution.py:303
  6.5 7.8 %collective-permute-start.4 = (bf16[256,256]{1,0:T(8,128)(2,1)S(1)}, bf16[256,256]{1,0:T(8,128)(2,1)S(1)}, u32[]{:S(2)}, u32[]{:S(2)}) collective-permute-start(bf16[256,256]{1,0:T(8,128)(2,1)S(1)} %shard_map.119.refs_0_), channel_id=1, source_target_pairs={{0,24},{8,16},{16,8},{24,0},{1,25},{9,17},{17,9},{25,1},{2,26},{10... | collective-permute-start | bytes 393224 | tf_op jit(solution)/shard_map/ppermute | solution.py:303
  10.4 7.9 %collective-permute-start.3 = (bf16[256,256]{1,0:T(8,128)(2,1)S(1)}, bf16[256,256]{1,0:T(8,128)(2,1)S(1)}, u32[]{:S(2)}, u32[]{:S(2)}) collective-permute-start(bf16[256,256]{1,0:T(8,128)(2,1)S(1)} %shard_map.119.refs_0_), channel_id=1, source_target_pairs={{0,16},{8,24},{16,0},{24,8},{1,17},{9,25},{17,1},{25,9},{2,18},{10... | collective-permute-start | bytes 393224 | tf_op jit(solution)/shard_map/ppermute | solution.py:303
  10.9 8.7 %collective-permute-start.2 = (bf16[256,256]{1,0:T(8,128)(2,1)S(1)}, bf16[256,256]{1,0:T(8,128)(2,1)S(1)}, u32[]{:S(2)}, u32[]{:S(2)}) collective-permute-start(bf16[256,256]{1,0:T(8,128)(2,1)S(1)} %shard_map.119.refs_0_), channel_id=1, source_target_pairs={{0,8},{8,0},{16,24},{24,16},{1,9},{9,1},{17,25},{25,17},{2,10},{10... | collective-permute-start | bytes 393224 | tf_op jit(solution)/shard_map/ppermute | solution.py:303
  11.0 9.4 %collective-permute-start.11 = (bf16[256,256]{1,0:T(8,128)(2,1)S(1)}, bf16[256,256]{1,0:T(8,128)(2,1)S(1)}, u32[]{:S(2)}, u32[]{:S(2)}) collective-permute-start(bf16[256,256]{1,0:T(8,128)(2,1)S(1)} %shard_map.124.refs_0_), channel_id=1, source_target_pairs={{0,24},{8,16},{16,8},{24,0},{1,25},{9,17},{17,9},{25,1},{2,26},{10... | collective-permute-start | bytes 393224 | tf_op jit(solution)/shard_map/ppermute | solution.py:303
  14.3 8.3 %collective-permute-start.10 = (bf16[256,256]{1,0:T(8,128)(2,1)S(1)}, bf16[256,256]{1,0:T(8,128)(2,1)S(1)}, u32[]{:S(2)}, u32[]{:S(2)}) collective-permute-start(bf16[256,256]{1,0:T(8,128)(2,1)S(1)} %shard_map.124.refs_0_), channel_id=1, source_target_pairs={{0,16},{8,24},{16,0},{24,8},{1,17},{9,25},{17,1},{25,9},{2,18},{10... | collective-permute-start | bytes 393224 | tf_op jit(solution)/shard_map/ppermute | solution.py:303
  18.3 5.2 %collective-permute-start.9 = (bf16[256,256]{1,0:T(8,128)(2,1)S(1)}, bf16[256,256]{1,0:T(8,128)(2,1)S(1)}, u32[]{:S(2)}, u32[]{:S(2)}) collective-permute-start(bf16[256,256]{1,0:T(8,128)(2,1)S(1)} %shard_map.124.refs_0_), channel_id=1, source_target_pairs={{0,8},{8,0},{16,24},{24,16},{1,9},{9,1},{17,25},{25,17},{2,10},{10... | collective-permute-start | bytes 393224 | tf_op jit(solution)/shard_map/ppermute | solution.py:303
  20.3 25.4 %collective-permute-start.19 = (bf16[1024,256]{1,0:T(8,128)(2,1)S(1)}, bf16[1024,256]{1,0:T(8,128)(2,1)S(1)}, u32[]{:S(2)}, u32[]{:S(2)}) collective-permute-start(bf16[1024,256]{1,0:T(8,128)(2,1)S(1)} %get-tuple-element.51.refs_4_), channel_id=1, source_target_pairs={{0,1},{1,0},{2,3},{3,2},{4,5},{5,4},{6,7},{7,6},{8,9},{9,8},{10,11... | collective-permute-start | bytes 1572872 | tf_op jit(solution)/shard_map/ppermute | solution.py:303
  24.3 21.5 %collective-permute-start.20 = (bf16[1024,256]{1,0:T(8,128)(2,1)S(1)}, bf16[1024,256]{1,0:T(8,128)(2,1)S(1)}, u32[]{:S(2)}, u32[]{:S(2)}) collective-permute-start(bf16[1024,256]{1,0:T(8,128)(2,1)S(1)} %get-tuple-element.52.refs_6_.refs_4_), channel_id=1, source_target_pairs={{0,1},{1,0},{2,3},{3,2},{4,5},{5,4},{6,7},{7,6},{8,9},{9,8},{10,11... | collective-permute-start | bytes 1572872 | tf_op jit(solution)/shard_map/ppermute | solution.py:303
  24.3 6.4 %collective-permute-start.6 = (bf16[256,256]{1,0:T(8,128)(2,1)S(1)}, bf16[256,256]{1,0:T(8,128)(2,1)S(1)}, u32[]{:S(2)}, u32[]{:S(2)}) collective-permute-start(bf16[256,256]{1,0:T(8,128)(2,1)S(1)} %get-tuple-element.37), channel_id=1, source_target_pairs={{0,2},{1,3},{2,0},{3,1},{4,6},{5,7},{6,4},{7,5},{8,10},{9,11},{10,... | collective-permute-start | bytes 393224 | tf_op jit(solution)/shard_map/ppermute | solution.py:303
  26.0 7.5 %collective-permute-start.5 = (bf16[256,256]{1,0:T(8,128)(2,1)S(1)}, bf16[256,256]{1,0:T(8,128)(2,1)S(1)}, u32[]{:S(2)}, u32[]{:S(2)}) collective-permute-start(bf16[256,256]{1,0:T(8,128)(2,1)S(1)} %get-tuple-element.35), channel_id=1, source_target_pairs={{0,2},{1,3},{2,0},{3,1},{4,6},{5,7},{6,4},{7,5},{8,10},{9,11},{10,... | collective-permute-start | bytes 393224 | tf_op jit(solution)/shard_map/ppermute | solution.py:303
  30.8 8.3 %collective-permute-start.7 = (bf16[256,256]{1,0:T(8,128)(2,1)S(1)}, bf16[256,256]{1,0:T(8,128)(2,1)S(1)}, u32[]{:S(2)}, u32[]{:S(2)}) collective-permute-start(bf16[256,256]{1,0:T(8,128)(2,1)S(1)} %shard_map.121), channel_id=1, source_target_pairs={{0,4},{1,5},{2,6},{3,7},{4,0},{5,1},{6,2},{7,3},{8,12},{9,13},{10,... | collective-permute-start | bytes 393224 | tf_op jit(solution)/shard_map/ppermute | solution.py:303
  51.4 7.3 %collective-permute-start.22 = (bf16[64,1024]{1,0:T(8,128)(2,1)S(1)}, bf16[64,1024]{1,0:T(8,128)(2,1)S(1)}, u32[]{:S(2)}, u32[]{:S(2)}) collective-permute-start(bf16[64,1024]{1,0:T(8,128)(2,1)S(1)} %shard_map.130.one), channel_id=1, source_target_pairs={{0,4},{1,5},{2,6},{3,7},{4,0},{5,1},{6,2},{7,3},{8,12},{9,13},{10,... | collective-permute-start | bytes 393224 | tf_op jit(solution)/shard_map/ppermute | solution.py:303
  58.7 6.0 %collective-permute-start.25 = (bf16[64,1024]{1,0:T(8,128)(2,1)S(1)}, bf16[64,1024]{1,0:T(8,128)(2,1)S(1)}, u32[]{:S(2)}, u32[]{:S(2)}) collective-permute-start(bf16[64,1024]{1,0:T(8,128)(2,1)S(1)} %shard_map.131.refs_0_), channel_id=1, source_target_pairs={{0,24},{8,16},{16,8},{24,0},{1,25},{9,17},{17,9},{25,1},{2,26},{10... | collective-permute-start | bytes 393224 | tf_op jit(solution)/shard_map/ppermute | solution.py:303
  60.7 5.3 %collective-permute-start.24 = (bf16[64,1024]{1,0:T(8,128)(2,1)S(1)}, bf16[64,1024]{1,0:T(8,128)(2,1)S(1)}, u32[]{:S(2)}, u32[]{:S(2)}) collective-permute-start(bf16[64,1024]{1,0:T(8,128)(2,1)S(1)} %shard_map.131.refs_0_), channel_id=1, source_target_pairs={{0,16},{8,24},{16,0},{24,8},{1,17},{9,25},{17,1},{25,9},{2,18},{10... | collective-permute-start | bytes 393224 | tf_op jit(solution)/shard_map/ppermute | solution.py:303
  67.0 33.7 %collective-permute-start.26 = (bf16[256,1024]{1,0:T(8,128)(2,1)S(1)}, bf16[256,1024]{1,0:T(8,128)(2,1)S(1)}, u32[]{:S(2)}, u32[]{:S(2)}) collective-permute-start(bf16[256,1024]{1,0:T(8,128)(2,1)S(1)} %shard_map.132.mine), channel_id=1, source_target_pairs={{0,1},{1,0},{2,3},{3,2},{4,5},{5,4},{6,7},{7,6},{8,9},{9,8},{10,11... | collective-permute-start | bytes 1572872 | tf_op jit(solution)/shard_map/ppermute | solution.py:303
  67.1 8.4 %collective-permute-start.12 = (bf16[256,256]{1,0:T(8,128)(2,1)S(1)}, bf16[256,256]{1,0:T(8,128)(2,1)S(1)}, u32[]{:S(2)}, u32[]{:S(2)}) collective-permute-start(bf16[256,256]{1,0:T(8,128)(2,1)S(1)} %get-tuple-element.40), channel_id=1, source_target_pairs={{0,2},{1,3},{2,0},{3,1},{4,6},{5,7},{6,4},{7,5},{8,10},{9,11},{10,... | collective-permute-start | bytes 393224 | tf_op jit(solution)/shard_map/ppermute | solution.py:303
  67.5 10.0 %collective-permute-start.14 = (bf16[256,256]{1,0:T(8,128)(2,1)S(1)}, bf16[256,256]{1,0:T(8,128)(2,1)S(1)}, u32[]{:S(2)}, u32[]{:S(2)}) collective-permute-start(bf16[256,256]{1,0:T(8,128)(2,1)S(1)} %shard_map.126), channel_id=1, source_target_pairs={{0,4},{1,5},{2,6},{3,7},{4,0},{5,1},{6,2},{7,3},{8,12},{9,13},{10,... | collective-permute-start | bytes 393224 | tf_op jit(solution)/shard_map/ppermute | solution.py:303
  85.0 6.1 %collective-permute-start.32 = (bf16[64,512]{1,0:T(8,128)(2,1)S(1)}, bf16[64,512]{1,0:T(8,128)(2,1)S(1)}, u32[]{:S(2)}, u32[]{:S(2)}) collective-permute-start(bf16[64,512]{1,0:T(8,128)(2,1)S(1)} %shard_map.135.refs_0_), channel_id=1, source_target_pairs={{0,6},{1,7},{2,4},{3,5},{4,2},{5,3},{6,0},{7,1},{8,14},{9,15},{10,... | collective-permute-start | bytes 196616 | tf_op jit(solution)/shard_map/ppermute | solution.py:303
  87.4 5.2 %collective-permute-start.31 = (bf16[64,512]{1,0:T(8,128)(2,1)S(1)}, bf16[64,512]{1,0:T(8,128)(2,1)S(1)}, u32[]{:S(2)}, u32[]{:S(2)}) collective-permute-start(bf16[64,512]{1,0:T(8,128)(2,1)S(1)} %shard_map.135.refs_0_), channel_id=1, source_target_pairs={{0,4},{1,5},{2,6},{3,7},{4,0},{5,1},{6,2},{7,3},{8,12},{9,13},{10,... | collective-permute-start | bytes 196616 | tf_op jit(solution)/shard_map/ppermute | solution.py:303
  87.4 5.2 %collective-permute-start.30 = (bf16[64,512]{1,0:T(8,128)(2,1)S(1)}, bf16[64,512]{1,0:T(8,128)(2,1)S(1)}, u32[]{:S(2)}, u32[]{:S(2)}) collective-permute-start(bf16[64,512]{1,0:T(8,128)(2,1)S(1)} %shard_map.135.refs_0_), channel_id=1, source_target_pairs={{0,2},{1,3},{2,0},{3,1},{4,6},{5,7},{6,4},{7,5},{8,10},{9,11},{10,... | collective-permute-start | bytes 196616 | tf_op jit(solution)/shard_map/ppermute | solution.py:303
  89.4 10.4 %collective-permute-start.15 = (f32[128,512]{1,0:T(8,128)S(1)}, f32[128,512]{1,0:T(8,128)S(1)}, u32[]{:S(2)}, u32[]{:S(2)}) collective-permute-start(f32[128,512]{1,0:T(8,128)S(1)} %get-tuple-element.45), channel_id=1, source_target_pairs={{0,1},{1,0},{2,3},{3,2},{4,5},{5,4},{6,7},{7,6},{8,9},{9,8},{10,11... | collective-permute-start | bytes 786440 | tf_op jit(solution)/shard_map/ppermute | solution.py:303
  92.6 5.3 %collective-permute-start.35 = (bf16[64,512]{1,0:T(8,128)(2,1)S(1)}, bf16[64,512]{1,0:T(8,128)(2,1)S(1)}, u32[]{:S(2)}, u32[]{:S(2)}) collective-permute-start(bf16[64,512]{1,0:T(8,128)(2,1)S(1)} %shard_map.136.refs_0_), channel_id=1, source_target_pairs={{0,24},{8,16},{16,8},{24,0},{1,25},{9,17},{17,9},{25,1},{2,26},{10... | collective-permute-start | bytes 196616 | tf_op jit(solution)/shard_map/ppermute | solution.py:303
  (19 other events, 90.1 us)

commit v6 on v5

--- a/solution.py
+++ b/solution.py
@@ -120,8 +120,8 @@
     return stay + [k ^ 1 for k in stay]
 
 
-def product_body(n, nz, mine, theirs, *refs):
-    q, (*outs, rhs) = refs[:n], refs[n:]
+def lead_body(n, nz, mine, theirs, *refs):
+    q, (out, rhs) = refs[:n], refs[n:]
     p, z, c = place()
     depth = rhs.shape[0] // 2
     rows = depth // n
@@ -129,7 +129,15 @@
         rhs[block(p ^ s, rows), :] = q[s][:rows, :]
         rhs[pl.ds(pl.multiple_of(depth + (p ^ s) * rows, rows), rows), :] = q[s][rows:, :]
     order, size = sequence(nz), nz // 4
-    for k in reversed(range(nz)):
+    for k in range(size):
+        emit(out, k, order[3 * size + k], z, c, rows, mine, theirs, rhs)
+
+
+def product_body(n, nz, mine, theirs, rhs, *outs):
+    _, z, c = place()
+    rows = rhs.shape[0] // (2 * n)
+    order, size = sequence(nz), nz // 4
+    for k in range(3 * size):
         emit(outs[k // size], k % size, order[k], z, c, rows, mine, theirs, rhs)
 
 
@@ -141,14 +149,22 @@
         out[block(2 * k + (c ^ t), rows), :] = value[t * rows : (t + 1) * rows].astype(out.dtype)
 
 
-def product(mine, theirs, q, nz):
+def lead(mine, theirs, q, nz):
     n, (rows, half) = len(q), q[0].shape
     depth = mine.shape[1]
     shape = (nz // 4 * rows, half)
-    out = [sds(shape, F32)] * 2 + [sds(shape, BF)] * 2 + [sds((2 * depth, half), BF)]
-    return call(
-        functools.partial(product_body, n, nz), out, [],
-        [mine, theirs, *q], 4 * mine.shape[0] * depth * half,
+    return call(
+        functools.partial(lead_body, n, nz), [sds(shape, BF), sds((2 * depth, half), BF)], [],
+        [mine, theirs, *q], mine.shape[0] * depth * half,
+    )
+
+
+def product(mine, theirs, rhs, n, nz):
+    depth, half = mine.shape[1], rhs.shape[1]
+    shape = (mine.shape[0] // 4, half)
+    return call(
+        functools.partial(product_body, n, nz), [sds(shape, F32)] * 2 + [sds(shape, BF)], [],
+        [mine, theirs, rhs], 3 * mine.shape[0] * depth * half,
     )
 
 
@@ -347,10 +363,12 @@
         held = stack([here] + [over_p(here, s) for s in range(1, n)])
         return held, swap(held)
 
-    *parts_one, rows_one = product(masked, others, gathered_one, nz)
-    parts_one = exchange(*parts_one)
-    *parts_two, rows_two = product(masked, others, gathered_two, nz)
-    parts_two = exchange(*parts_two)
+    go_one, rows_one = lead(masked, others, gathered_one, nz)
+    rest_one = product(masked, others, rows_one, n, nz)
+    parts_one = exchange(*rest_one, go_one)
+    go_two, rows_two = lead(masked, others, gathered_two, nz)
+    rest_two = product(masked, others, rows_two, n, nz)
+    parts_two = exchange(*rest_two, go_two)
     panels = [rows_one, swap(rows_one), rows_two, swap(rows_two)]
     keep_one, give_one, *pieces_one = first_turn(parts_one, n)
     pieces_one = spread(pieces_one)

time: 104 us -> 106 us (1.019)
  waiting for transfers between devices: 50.4 us -> 53.7 us
  starting transfers between devices: 42.3 us -> 41.2 us
    ppermute x37, waiting for transfers between devices: 50.4 us -> 53.7 us  [on_device(): lax.ppermute(x, axis, [(k, k ^ s) for k in range(size)])]
    ppermute x37, starting transfers between devices: 42.3 us -> 41.2 us  [on_device(): lax.ppermute(x, axis, [(k, k ^ s) for k in range(size)])]
    pallas_call x20 -> x22, Pallas kernels: 6.83 us -> 7.18 us  [call(): pl.pallas_call(body, out_shape=out, in_specs=[VMEM] * len(args), out_spec...]
where the time goes in v6:
time: 106 us
  waiting for transfers between devices  53.7 us (51%)
  starting transfers between devices  41.2 us (39%)
  Pallas kernels  7.18 us (7%)
  other arithmetic  2.33 us (2%)
    ppermute x37, waiting for transfers between devices, on_device(): lax.ppermute(x, axis, [(k, k ^ s) for k in range(size)])  53.7 us
    ppermute x37, starting transfers between devices, on_device(): lax.ppermute(x, axis, [(k, k ^ s) for k in range(size)])  41.2 us
    pallas_call x22, Pallas kernels, call(): pl.pallas_call(body, out_shape=out, in_specs=[VMEM] * len(args), out_spec...  7.18 us
  transfers between devices with their start and end apart: 37, of which 26 were waited for; matrix products, arithmetic and copies ran while one was open for 0% of the time, Pallas kernels for 5%

profile of v6, /device:TPU:0, one launch (start us, length us, event | category | flops | bytes accessed | tf_op | source)
XLA Modules:
  0.0 106.2 jit_solution(395469546785508932)
XLA Ops:
  6.5 2.9 %collective-permute-start.10 = (bf16[256,256]{1,0:T(8,128)(2,1)S(1)}, bf16[256,256]{1,0:T(8,128)(2,1)S(1)}, u32[]{:S(2)}, u32[]{:S(2)}) collective-permute-start(bf16[256,256]{1,0:T(8,128)(2,1)S(1)} %shard_map.125.refs_0_), channel_id=1, source_target_pairs={{0,16},{8,24},{16,0},{24,8},{1,17},{9,25},{17,1},{25,9},{2,18},{10... | collective-permute-start | bytes 393224 | tf_op jit(solution)/shard_map/ppermute | solution.py:319
  11.0 2.0 %collective-permute-start.2 = (bf16[256,256]{1,0:T(8,128)(2,1)S(1)}, bf16[256,256]{1,0:T(8,128)(2,1)S(1)}, u32[]{:S(2)}, u32[]{:S(2)}) collective-permute-start(bf16[256,256]{1,0:T(8,128)(2,1)S(1)} %shard_map.119.refs_0_), channel_id=1, source_target_pairs={{0,8},{8,0},{16,24},{24,16},{1,9},{9,1},{17,25},{25,17},{2,10},{10... | collective-permute-start | bytes 393224 | tf_op jit(solution)/shard_map/ppermute | solution.py:319
  13.0 2.4 %collective-permute-done.10.refs_2_ = bf16[256,256]{1,0:T(8,128)(2,1)S(1)} collective-permute-done((bf16[256,256]{1,0:T(8,128)(2,1)S(1)}, bf16[256,256]{1,0:T(8,128)(2,1)S(1)}, u32[]{:S(2)}, u32[]{:S(2)}) %collective-permute-start.10) | collective-permute-done | bytes 131104 | tf_op jit(solution)/shard_map/ppermute | solution.py:319
  15.4 2.4 %collective-permute-start.3 = (bf16[256,256]{1,0:T(8,128)(2,1)S(1)}, bf16[256,256]{1,0:T(8,128)(2,1)S(1)}, u32[]{:S(2)}, u32[]{:S(2)}) collective-permute-start(bf16[256,256]{1,0:T(8,128)(2,1)S(1)} %shard_map.119.refs_0_), channel_id=1, source_target_pairs={{0,16},{8,24},{16,0},{24,8},{1,17},{9,25},{17,1},{25,9},{2,18},{10... | collective-permute-start | bytes 393224 | tf_op jit(solution)/shard_map/ppermute | solution.py:319
  19.2 1.8 %collective-permute-done.2.refs_1_ = bf16[256,256]{1,0:T(8,128)(2,1)S(1)} collective-permute-done((bf16[256,256]{1,0:T(8,128)(2,1)S(1)}, bf16[256,256]{1,0:T(8,128)(2,1)S(1)}, u32[]{:S(2)}, u32[]{:S(2)}) %collective-permute-start.2) | collective-permute-done | bytes 131104 | tf_op jit(solution)/shard_map/ppermute | solution.py:319
  21.0 1.8 %collective-permute-done.3.refs_2_ = bf16[256,256]{1,0:T(8,128)(2,1)S(1)} collective-permute-done((bf16[256,256]{1,0:T(8,128)(2,1)S(1)}, bf16[256,256]{1,0:T(8,128)(2,1)S(1)}, u32[]{:S(2)}, u32[]{:S(2)}) %collective-permute-start.3) | collective-permute-done | bytes 131104 | tf_op jit(solution)/shard_map/ppermute | solution.py:319
  27.2 3.7 %collective-permute-done.6.two = bf16[256,256]{1,0:T(8,128)(2,1)S(1)} collective-permute-done((bf16[256,256]{1,0:T(8,128)(2,1)S(1)}, bf16[256,256]{1,0:T(8,128)(2,1)S(1)}, u32[]{:S(2)}, u32[]{:S(2)}) %collective-permute-start.6) | collective-permute-done | bytes 131104 | tf_op jit(solution)/shard_map/ppermute | solution.py:319
  30.9 2.7 %collective-permute-start.7 = (bf16[256,256]{1,0:T(8,128)(2,1)S(1)}, bf16[256,256]{1,0:T(8,128)(2,1)S(1)}, u32[]{:S(2)}, u32[]{:S(2)}) collective-permute-start(bf16[256,256]{1,0:T(8,128)(2,1)S(1)} %shard_map.122), channel_id=1, source_target_pairs={{0,4},{1,5},{2,6},{3,7},{4,0},{5,1},{6,2},{7,3},{8,12},{9,13},{10,... | collective-permute-start | bytes 393224 | tf_op jit(solution)/shard_map/ppermute | solution.py:319
  33.6 5.7 %collective-permute-done.7.refs_2_ = bf16[256,256]{1,0:T(8,128)(2,1)S(1)} collective-permute-done((bf16[256,256]{1,0:T(8,128)(2,1)S(1)}, bf16[256,256]{1,0:T(8,128)(2,1)S(1)}, u32[]{:S(2)}, u32[]{:S(2)}) %collective-permute-start.7) | collective-permute-done | bytes 131104 | tf_op jit(solution)/shard_map/ppermute | solution.py:319
  44.9 2.1 %collective-permute-done.18.refs_3_ = bf16[64,256]{1,0:T(8,128)(2,1)S(1)} collective-permute-done((bf16[64,256]{1,0:T(8,128)(2,1)S(1)}, bf16[64,256]{1,0:T(8,128)(2,1)S(1)}, u32[]{:S(2)}, u32[]{:S(2)}) %collective-permute-start.18) | collective-permute-done | bytes 32800 | tf_op jit(solution)/shard_map/ppermute | solution.py:319
  48.1 4.4 %collective-permute-done.21.two = bf16[64,1024]{1,0:T(8,128)(2,1)S(1)} collective-permute-done((bf16[64,1024]{1,0:T(8,128)(2,1)S(1)}, bf16[64,1024]{1,0:T(8,128)(2,1)S(1)}, u32[]{:S(2)}, u32[]{:S(2)}) %collective-permute-start.21) | collective-permute-done | bytes 131104 | tf_op jit(solution)/shard_map/ppermute | solution.py:319
  52.6 2.2 %collective-permute-start.22 = (bf16[64,1024]{1,0:T(8,128)(2,1)S(1)}, bf16[64,1024]{1,0:T(8,128)(2,1)S(1)}, u32[]{:S(2)}, u32[]{:S(2)}) collective-permute-start(bf16[64,1024]{1,0:T(8,128)(2,1)S(1)} %shard_map.132.one), channel_id=1, source_target_pairs={{0,4},{1,5},{2,6},{3,7},{4,0},{5,1},{6,2},{7,3},{8,12},{9,13},{10,... | collective-permute-start | bytes 393224 | tf_op jit(solution)/shard_map/ppermute | solution.py:319
  54.7 5.2 %collective-permute-done.22.two = bf16[64,1024]{1,0:T(8,128)(2,1)S(1)} collective-permute-done((bf16[64,1024]{1,0:T(8,128)(2,1)S(1)}, bf16[64,1024]{1,0:T(8,128)(2,1)S(1)}, u32[]{:S(2)}, u32[]{:S(2)}) %collective-permute-start.22) | collective-permute-done | bytes 131104 | tf_op jit(solution)/shard_map/ppermute | solution.py:319
  61.4 2.1 %collective-permute-start.25 = (bf16[64,1024]{1,0:T(8,128)(2,1)S(1)}, bf16[64,1024]{1,0:T(8,128)(2,1)S(1)}, u32[]{:S(2)}, u32[]{:S(2)}) collective-permute-start(bf16[64,1024]{1,0:T(8,128)(2,1)S(1)} %shard_map.133.refs_0_), channel_id=1, source_target_pairs={{0,24},{8,16},{16,8},{24,0},{1,25},{9,17},{17,9},{25,1},{2,26},{10... | collective-permute-start | bytes 393224 | tf_op jit(solution)/shard_map/ppermute | solution.py:319
  65.5 1.8 %collective-permute-done.25.refs_3_ = bf16[64,1024]{1,0:T(8,128)(2,1)S(1)} collective-permute-done((bf16[64,1024]{1,0:T(8,128)(2,1)S(1)}, bf16[64,1024]{1,0:T(8,128)(2,1)S(1)}, u32[]{:S(2)}, u32[]{:S(2)}) %collective-permute-start.25) | collective-permute-done | bytes 131104 | tf_op jit(solution)/shard_map/ppermute | solution.py:319
  68.5 3.0 %collective-permute-start.14 = (bf16[256,256]{1,0:T(8,128)(2,1)S(1)}, bf16[256,256]{1,0:T(8,128)(2,1)S(1)}, u32[]{:S(2)}, u32[]{:S(2)}) collective-permute-start(bf16[256,256]{1,0:T(8,128)(2,1)S(1)} %shard_map.128), channel_id=1, source_target_pairs={{0,4},{1,5},{2,6},{3,7},{4,0},{5,1},{6,2},{7,3},{8,12},{9,13},{10,... | collective-permute-start | bytes 393224 | tf_op jit(solution)/shard_map/ppermute | solution.py:319
  71.5 5.0 %collective-permute-done.12.refs_1_ = bf16[256,256]{1,0:T(8,128)(2,1)S(1)} collective-permute-done((bf16[256,256]{1,0:T(8,128)(2,1)S(1)}, bf16[256,256]{1,0:T(8,128)(2,1)S(1)}, u32[]{:S(2)}, u32[]{:S(2)}) %collective-permute-start.12) | collective-permute-done | bytes 131104 | tf_op jit(solution)/shard_map/ppermute | solution.py:319
  76.5 1.8 %collective-permute-done.14.refs_2_ = bf16[256,256]{1,0:T(8,128)(2,1)S(1)} collective-permute-done((bf16[256,256]{1,0:T(8,128)(2,1)S(1)}, bf16[256,256]{1,0:T(8,128)(2,1)S(1)}, u32[]{:S(2)}, u32[]{:S(2)}) %collective-permute-start.14) | collective-permute-done | bytes 131104 | tf_op jit(solution)/shard_map/ppermute | solution.py:319
  78.4 1.8 %collective-permute-start.27 = (bf16[64,256]{1,0:T(8,128)(2,1)S(1)}, bf16[64,256]{1,0:T(8,128)(2,1)S(1)}, u32[]{:S(2)}, u32[]{:S(2)}) collective-permute-start(bf16[64,256]{1,0:T(8,128)(2,1)S(1)} %get-tuple-element.59), channel_id=1, source_target_pairs={{0,8},{8,0},{16,24},{24,16},{1,9},{9,1},{17,25},{25,17},{2,10},{10... | collective-permute-start | bytes 98312 | tf_op jit(solution)/shard_map/ppermute | solution.py:319
  84.2 2.0 %collective-permute-done.29.refs_3_ = bf16[64,256]{1,0:T(8,128)(2,1)S(1)} collective-permute-done((bf16[64,256]{1,0:T(8,128)(2,1)S(1)}, bf16[64,256]{1,0:T(8,128)(2,1)S(1)}, u32[]{:S(2)}, u32[]{:S(2)}) %collective-permute-start.29) | collective-permute-done | bytes 32800 | tf_op jit(solution)/shard_map/ppermute | solution.py:319
  86.8 2.7 %collective-permute-start.31 = (bf16[64,512]{1,0:T(8,128)(2,1)S(1)}, bf16[64,512]{1,0:T(8,128)(2,1)S(1)}, u32[]{:S(2)}, u32[]{:S(2)}) collective-permute-start(bf16[64,512]{1,0:T(8,128)(2,1)S(1)} %shard_map.137.refs_0_), channel_id=1, source_target_pairs={{0,4},{1,5},{2,6},{3,7},{4,0},{5,1},{6,2},{7,3},{8,12},{9,13},{10,... | collective-permute-start | bytes 196616 | tf_op jit(solution)/shard_map/ppermute | solution.py:319
  90.9 2.4 %collective-permute-done.31.refs_2_ = bf16[64,512]{1,0:T(8,128)(2,1)S(1)} collective-permute-done((bf16[64,512]{1,0:T(8,128)(2,1)S(1)}, bf16[64,512]{1,0:T(8,128)(2,1)S(1)}, u32[]{:S(2)}, u32[]{:S(2)}) %collective-permute-start.31) | collective-permute-done | bytes 65568 | tf_op jit(solution)/shard_map/ppermute | solution.py:319
  93.3 2.2 %collective-permute-done.32.refs_3_ = bf16[64,512]{1,0:T(8,128)(2,1)S(1)} collective-permute-done((bf16[64,512]{1,0:T(8,128)(2,1)S(1)}, bf16[64,512]{1,0:T(8,128)(2,1)S(1)}, u32[]{:S(2)}, u32[]{:S(2)}) %collective-permute-start.32) | collective-permute-done | bytes 65568 | tf_op jit(solution)/shard_map/ppermute | solution.py:319
  96.8 2.3 %collective-permute-start.35 = (bf16[64,512]{1,0:T(8,128)(2,1)S(1)}, bf16[64,512]{1,0:T(8,128)(2,1)S(1)}, u32[]{:S(2)}, u32[]{:S(2)}) collective-permute-start(bf16[64,512]{1,0:T(8,128)(2,1)S(1)} %shard_map.138.refs_0_), channel_id=1, source_target_pairs={{0,24},{8,16},{16,8},{24,0},{1,25},{9,17},{17,9},{25,1},{2,26},{10... | collective-permute-start | bytes 196616 | tf_op jit(solution)/shard_map/ppermute | solution.py:319
  (88 shorter events, 39.0 us)
Async XLA Ops:
  3.4 15.3 %collective-permute-start = (bf16[1024,512]{1,0:T(8,128)(2,1)S(1)}, bf16[1024,512]{1,0:T(8,128)(2,1)S(1)}, u32[]{:S(2)}, u32[]{:S(2)}) collective-permute-start(bf16[1024,512]{1,0:T(8,128)(2,1)S(1)} %bitcast_select_fusion.mine), channel_id=1, source_target_pairs={{0,1},{1,0},{2,3},{3,2},{4,5},{5,4},{6,7},{7,6},{8,9},{9,8},{10,11... | collective-permute-start | bytes 3145736 | tf_op jit(solution)/shard_map/ppermute | solution.py:319
  5.0 6.0 %collective-permute-start.1 = (bf16[128,512]{1,0:T(8,128)(2,1)S(1)}, bf16[128,512]{1,0:T(8,128)(2,1)S(1)}, u32[]{:S(2)}, u32[]{:S(2)}) collective-permute-start(bf16[128,512]{1,0:T(8,128)(2,1)S(1)} %copy-done.3), channel_id=1, source_target_pairs={{0,1},{1,0},{2,3},{3,2},{4,5},{5,4},{6,7},{7,6},{8,9},{9,8},{10,11... | collective-permute-start | bytes 393224 | tf_op jit(solution)/shard_map/ppermute | solution.py:319
  6.5 8.9 %collective-permute-start.10 = (bf16[256,256]{1,0:T(8,128)(2,1)S(1)}, bf16[256,256]{1,0:T(8,128)(2,1)S(1)}, u32[]{:S(2)}, u32[]{:S(2)}) collective-permute-start(bf16[256,256]{1,0:T(8,128)(2,1)S(1)} %shard_map.125.refs_0_), channel_id=1, source_target_pairs={{0,16},{8,24},{16,0},{24,8},{1,17},{9,25},{17,1},{25,9},{2,18},{10... | collective-permute-start | bytes 393224 | tf_op jit(solution)/shard_map/ppermute | solution.py:319
  9.4 8.4 %collective-permute-start.11 = (bf16[256,256]{1,0:T(8,128)(2,1)S(1)}, bf16[256,256]{1,0:T(8,128)(2,1)S(1)}, u32[]{:S(2)}, u32[]{:S(2)}) collective-permute-start(bf16[256,256]{1,0:T(8,128)(2,1)S(1)} %shard_map.125.refs_0_), channel_id=1, source_target_pairs={{0,24},{8,16},{16,8},{24,0},{1,25},{9,17},{17,9},{25,1},{2,26},{10... | collective-permute-start | bytes 393224 | tf_op jit(solution)/shard_map/ppermute | solution.py:319
  10.9 7.9 %collective-permute-start.9 = (bf16[256,256]{1,0:T(8,128)(2,1)S(1)}, bf16[256,256]{1,0:T(8,128)(2,1)S(1)}, u32[]{:S(2)}, u32[]{:S(2)}) collective-permute-start(bf16[256,256]{1,0:T(8,128)(2,1)S(1)} %shard_map.125.refs_0_), channel_id=1, source_target_pairs={{0,8},{8,0},{16,24},{24,16},{1,9},{9,1},{17,25},{25,17},{2,10},{10... | collective-permute-start | bytes 393224 | tf_op jit(solution)/shard_map/ppermute | solution.py:319
  11.0 10.0 %collective-permute-start.2 = (bf16[256,256]{1,0:T(8,128)(2,1)S(1)}, bf16[256,256]{1,0:T(8,128)(2,1)S(1)}, u32[]{:S(2)}, u32[]{:S(2)}) collective-permute-start(bf16[256,256]{1,0:T(8,128)(2,1)S(1)} %shard_map.119.refs_0_), channel_id=1, source_target_pairs={{0,8},{8,0},{16,24},{24,16},{1,9},{9,1},{17,25},{25,17},{2,10},{10... | collective-permute-start | bytes 393224 | tf_op jit(solution)/shard_map/ppermute | solution.py:319
  15.4 7.4 %collective-permute-start.3 = (bf16[256,256]{1,0:T(8,128)(2,1)S(1)}, bf16[256,256]{1,0:T(8,128)(2,1)S(1)}, u32[]{:S(2)}, u32[]{:S(2)}) collective-permute-start(bf16[256,256]{1,0:T(8,128)(2,1)S(1)} %shard_map.119.refs_0_), channel_id=1, source_target_pairs={{0,16},{8,24},{16,0},{24,8},{1,17},{9,25},{17,1},{25,9},{2,18},{10... | collective-permute-start | bytes 393224 | tf_op jit(solution)/shard_map/ppermute | solution.py:319
  17.8 6.3 %collective-permute-start.4 = (bf16[256,256]{1,0:T(8,128)(2,1)S(1)}, bf16[256,256]{1,0:T(8,128)(2,1)S(1)}, u32[]{:S(2)}, u32[]{:S(2)}) collective-permute-start(bf16[256,256]{1,0:T(8,128)(2,1)S(1)} %shard_map.119.refs_0_), channel_id=1, source_target_pairs={{0,24},{8,16},{16,8},{24,0},{1,25},{9,17},{17,9},{25,1},{2,26},{10... | collective-permute-start | bytes 393224 | tf_op jit(solution)/shard_map/ppermute | solution.py:319
  19.1 27.9 %collective-permute-start.20 = (bf16[1024,256]{1,0:T(8,128)(2,1)S(1)}, bf16[1024,256]{1,0:T(8,128)(2,1)S(1)}, u32[]{:S(2)}, u32[]{:S(2)}) collective-permute-start(bf16[1024,256]{1,0:T(8,128)(2,1)S(1)} %get-tuple-element.40.rhs.refs_6_.refs_4_), channel_id=1, source_target_pairs={{0,1},{1,0},{2,3},{3,2},{4,5},{5,4},{6,7},{7,6},{8,9},{9,8},{10,11... | collective-permute-start | bytes 1572872 | tf_op jit(solution)/shard_map/ppermute | solution.py:319
  24.4 22.6 %collective-permute-start.19 = (bf16[1024,256]{1,0:T(8,128)(2,1)S(1)}, bf16[1024,256]{1,0:T(8,128)(2,1)S(1)}, u32[]{:S(2)}, u32[]{:S(2)}) collective-permute-start(bf16[1024,256]{1,0:T(8,128)(2,1)S(1)} %get-tuple-element.34.rhs.refs_4_), channel_id=1, source_target_pairs={{0,1},{1,0},{2,3},{3,2},{4,5},{5,4},{6,7},{7,6},{8,9},{9,8},{10,11... | collective-permute-start | bytes 1572872 | tf_op jit(solution)/shard_map/ppermute | solution.py:319
  24.5 6.4 %collective-permute-start.6 = (bf16[256,256]{1,0:T(8,128)(2,1)S(1)}, bf16[256,256]{1,0:T(8,128)(2,1)S(1)}, u32[]{:S(2)}, u32[]{:S(2)}) collective-permute-start(bf16[256,256]{1,0:T(8,128)(2,1)S(1)} %get-tuple-element.38), channel_id=1, source_target_pairs={{0,2},{1,3},{2,0},{3,1},{4,6},{5,7},{6,4},{7,5},{8,10},{9,11},{10,... | collective-permute-start | bytes 393224 | tf_op jit(solution)/shard_map/ppermute | solution.py:319
  26.7 6.9 %collective-permute-start.5 = (bf16[256,256]{1,0:T(8,128)(2,1)S(1)}, bf16[256,256]{1,0:T(8,128)(2,1)S(1)}, u32[]{:S(2)}, u32[]{:S(2)}) collective-permute-start(bf16[256,256]{1,0:T(8,128)(2,1)S(1)} %get-tuple-element.36), channel_id=1, source_target_pairs={{0,2},{1,3},{2,0},{3,1},{4,6},{5,7},{6,4},{7,5},{8,10},{9,11},{10,... | collective-permute-start | bytes 393224 | tf_op jit(solution)/shard_map/ppermute | solution.py:319
  30.9 8.3 %collective-permute-start.7 = (bf16[256,256]{1,0:T(8,128)(2,1)S(1)}, bf16[256,256]{1,0:T(8,128)(2,1)S(1)}, u32[]{:S(2)}, u32[]{:S(2)}) collective-permute-start(bf16[256,256]{1,0:T(8,128)(2,1)S(1)} %shard_map.122), channel_id=1, source_target_pairs={{0,4},{1,5},{2,6},{3,7},{4,0},{5,1},{6,2},{7,3},{8,12},{9,13},{10,... | collective-permute-start | bytes 393224 | tf_op jit(solution)/shard_map/ppermute | solution.py:319
  47.5 5.0 %collective-permute-start.21 = (bf16[64,1024]{1,0:T(8,128)(2,1)S(1)}, bf16[64,1024]{1,0:T(8,128)(2,1)S(1)}, u32[]{:S(2)}, u32[]{:S(2)}) collective-permute-start(bf16[64,1024]{1,0:T(8,128)(2,1)S(1)} %shard_map.131.one), channel_id=1, source_target_pairs={{0,2},{1,3},{2,0},{3,1},{4,6},{5,7},{6,4},{7,5},{8,10},{9,11},{10,... | collective-permute-start | bytes 393224 | tf_op jit(solution)/shard_map/ppermute | solution.py:319
  52.6 7.4 %collective-permute-start.22 = (bf16[64,1024]{1,0:T(8,128)(2,1)S(1)}, bf16[64,1024]{1,0:T(8,128)(2,1)S(1)}, u32[]{:S(2)}, u32[]{:S(2)}) collective-permute-start(bf16[64,1024]{1,0:T(8,128)(2,1)S(1)} %shard_map.132.one), channel_id=1, source_target_pairs={{0,4},{1,5},{2,6},{3,7},{4,0},{5,1},{6,2},{7,3},{8,12},{9,13},{10,... | collective-permute-start | bytes 393224 | tf_op jit(solution)/shard_map/ppermute | solution.py:319
  60.0 5.0 %collective-permute-start.23 = (bf16[64,1024]{1,0:T(8,128)(2,1)S(1)}, bf16[64,1024]{1,0:T(8,128)(2,1)S(1)}, u32[]{:S(2)}, u32[]{:S(2)}) collective-permute-start(bf16[64,1024]{1,0:T(8,128)(2,1)S(1)} %shard_map.133.refs_0_), channel_id=1, source_target_pairs={{0,8},{8,0},{16,24},{24,16},{1,9},{9,1},{17,25},{25,17},{2,10},{10... | collective-permute-start | bytes 393224 | tf_op jit(solution)/shard_map/ppermute | solution.py:319
  61.4 5.9 %collective-permute-start.25 = (bf16[64,1024]{1,0:T(8,128)(2,1)S(1)}, bf16[64,1024]{1,0:T(8,128)(2,1)S(1)}, u32[]{:S(2)}, u32[]{:S(2)}) collective-permute-start(bf16[64,1024]{1,0:T(8,128)(2,1)S(1)} %shard_map.133.refs_0_), channel_id=1, source_target_pairs={{0,24},{8,16},{16,8},{24,0},{1,25},{9,17},{17,9},{25,1},{2,26},{10... | collective-permute-start | bytes 393224 | tf_op jit(solution)/shard_map/ppermute | solution.py:319
  67.4 36.1 %collective-permute-start.26 = (bf16[256,1024]{1,0:T(8,128)(2,1)S(1)}, bf16[256,1024]{1,0:T(8,128)(2,1)S(1)}, u32[]{:S(2)}, u32[]{:S(2)}) collective-permute-start(bf16[256,1024]{1,0:T(8,128)(2,1)S(1)} %shard_map.134.mine), channel_id=1, source_target_pairs={{0,1},{1,0},{2,3},{3,2},{4,5},{5,4},{6,7},{7,6},{8,9},{9,8},{10,11... | collective-permute-start | bytes 1572872 | tf_op jit(solution)/shard_map/ppermute | solution.py:319
  68.0 8.4 %collective-permute-start.12 = (bf16[256,256]{1,0:T(8,128)(2,1)S(1)}, bf16[256,256]{1,0:T(8,128)(2,1)S(1)}, u32[]{:S(2)}, u32[]{:S(2)}) collective-permute-start(bf16[256,256]{1,0:T(8,128)(2,1)S(1)} %get-tuple-element.42), channel_id=1, source_target_pairs={{0,2},{1,3},{2,0},{3,1},{4,6},{5,7},{6,4},{7,5},{8,10},{9,11},{10,... | collective-permute-start | bytes 393224 | tf_op jit(solution)/shard_map/ppermute | solution.py:319
  68.5 9.7 %collective-permute-start.14 = (bf16[256,256]{1,0:T(8,128)(2,1)S(1)}, bf16[256,256]{1,0:T(8,128)(2,1)S(1)}, u32[]{:S(2)}, u32[]{:S(2)}) collective-permute-start(bf16[256,256]{1,0:T(8,128)(2,1)S(1)} %shard_map.128), channel_id=1, source_target_pairs={{0,4},{1,5},{2,6},{3,7},{4,0},{5,1},{6,2},{7,3},{8,12},{9,13},{10,... | collective-permute-start | bytes 393224 | tf_op jit(solution)/shard_map/ppermute | solution.py:319
  86.8 6.6 %collective-permute-start.31 = (bf16[64,512]{1,0:T(8,128)(2,1)S(1)}, bf16[64,512]{1,0:T(8,128)(2,1)S(1)}, u32[]{:S(2)}, u32[]{:S(2)}) collective-permute-start(bf16[64,512]{1,0:T(8,128)(2,1)S(1)} %shard_map.137.refs_0_), channel_id=1, source_target_pairs={{0,4},{1,5},{2,6},{3,7},{4,0},{5,1},{6,2},{7,3},{8,12},{9,13},{10,... | collective-permute-start | bytes 196616 | tf_op jit(solution)/shard_map/ppermute | solution.py:319
  89.5 6.1 %collective-permute-start.32 = (bf16[64,512]{1,0:T(8,128)(2,1)S(1)}, bf16[64,512]{1,0:T(8,128)(2,1)S(1)}, u32[]{:S(2)}, u32[]{:S(2)}) collective-permute-start(bf16[64,512]{1,0:T(8,128)(2,1)S(1)} %shard_map.137.refs_0_), channel_id=1, source_target_pairs={{0,6},{1,7},{2,4},{3,5},{4,2},{5,3},{6,0},{7,1},{8,14},{9,15},{10,... | collective-permute-start | bytes 196616 | tf_op jit(solution)/shard_map/ppermute | solution.py:319
  90.9 11.7 %collective-permute-start.15 = (f32[128,512]{1,0:T(8,128)S(1)}, f32[128,512]{1,0:T(8,128)S(1)}, u32[]{:S(2)}, u32[]{:S(2)}) collective-permute-start(f32[128,512]{1,0:T(8,128)S(1)} %get-tuple-element.47), channel_id=1, source_target_pairs={{0,1},{1,0},{2,3},{3,2},{4,5},{5,4},{6,7},{7,6},{8,9},{9,8},{10,11... | collective-permute-start | bytes 786440 | tf_op jit(solution)/shard_map/ppermute | solution.py:319
  96.8 5.2 %collective-permute-start.35 = (bf16[64,512]{1,0:T(8,128)(2,1)S(1)}, bf16[64,512]{1,0:T(8,128)(2,1)S(1)}, u32[]{:S(2)}, u32[]{:S(2)}) collective-permute-start(bf16[64,512]{1,0:T(8,128)(2,1)S(1)} %shard_map.138.refs_0_), channel_id=1, source_target_pairs={{0,24},{8,16},{16,8},{24,0},{1,25},{9,17},{17,9},{25,1},{2,26},{10... | collective-permute-start | bytes 196616 | tf_op jit(solution)/shard_map/ppermute | solution.py:319
  (19 other events, 90.4 us)
